TPU v7x, 256 devices: a whole 4x4x8 slice. The times are simulated.
256 devices in a mesh: dp: 4 (over x), vocab: 64 (over y, z, core).
Axes of the slice: x: 4, y: 4, z: 8, core: 2. Of those that a mesh axis runs over, the one named last changes fastest.
Arguments:
- teacher_hidden: bfloat16 [1024, 8192], P('dp', 'vocab'), may hold values from -200 to 200
- student_hidden: bfloat16 [1024, 3584], P('dp', 'vocab'), may hold values from -200 to 200
- teacher_head: bfloat16 [8192, 81920], P('dp', 'vocab'), may hold values from -0.0625 to 0.0625
- student_head: bfloat16 [3584, 81920], P('dp', 'vocab'), may hold values from -0.09375 to 0.09375
- allowed: int32 [1024, 640], P('dp', 'vocab'), may hold values from 0 to 1, as said below
- sampled: int32 [1024], P('dp'), may hold values from 0 to 81919, as said below
Outputs:
- row_kl: float32 [1024], P('dp')
- sampled_logprob: float32 [1024], P('dp')
- head_grad: float32 [3584, 81920], P('dp', 'vocab')
Inputs may be any that keep to these rules, and one draw needn't show every extreme that they name: allowed is 0 or 1; the block of every row's sampled token is allowed, so every row has an allowed block; the share of allowed blocks differs from block to block. sampled[r] lies in a block that allowed marks for row r.
All inputs are finite; a program needn't handle non-finite values.
Results may differ from a plain program's by a relative error of at most 0.004.
Values may be sent and summed in bfloat16 or wider, within the bound.
No kernel may reach another device: no remote copies, remote signals or barrier semaphores. Data moves between devices by JAX's collectives and lax.ppermute only.
A program may use at most 128 MiB of HBM per device.

v0:
```python
import functools

import jax
import jax.numpy as jnp
from jax import lax
from jax.experimental import pallas as pl
from jax.experimental.pallas import tpu as pltpu
from jax.sharding import Mesh
from jax.sharding import PartitionSpec as P

CAP = 80
NEG = -1e30
BLOCK = 128
LOCAL = ("y", "z", "c")


def dot(a, b, dims):
    return lax.dot_general(a, b, (dims, ((), ())), preferred_element_type=jnp.float32)


def params(**kw):
    return pltpu.CompilerParams(vmem_limit_bytes=48 << 20, **kw)


def selector(pos_row):
    lines = lax.broadcasted_iota(jnp.int32, (CAP, pos_row.shape[-1]), 0)
    return lines == pos_row


def diagonal():
    rows = lax.broadcasted_iota(jnp.int32, (CAP, BLOCK), 0)
    return rows == lax.broadcasted_iota(jnp.int32, (CAP, BLOCK), 1)


def coded(logits):
    peak = jnp.max(jnp.abs(logits), axis=1, keepdims=True)
    power = jnp.floor(jnp.log2(jnp.maximum(peak, 1e-30)))
    scaled = jnp.round(logits * jnp.exp2(14.0 - power))
    values = jnp.clip(scaled, -32767.0, 32767.0).astype(jnp.int32).astype(jnp.int16)
    return values, jnp.sum(jnp.where(diagonal(), power, 0.0), axis=0, keepdims=True)


def decoded(values, powers):
    power = jnp.sum(jnp.where(diagonal(), powers, 0.0), axis=1, keepdims=True)
    return values.astype(jnp.int32).astype(jnp.float32) * jnp.exp2(power - 14.0)


def partial_kernel(steps, meta, pos, *refs):
    count = len(steps)
    mine, others = refs[:count], refs[count : 2 * count]
    head_t, head_s = refs[2 * count : 2 * count + 2]
    outs = refs[2 * count + 2 : 3 * count + 2]
    kept, sel, rows_t, rows_s, powers = refs[3 * count + 2 :]
    blocks = sel.shape[0] // CAP
    depth, tokens = mine[0].shape[0], sel.shape[1]
    both = kept.shape[1] // depth
    b = pl.program_id(0)

    @pl.when(b == 0)
    def _():
        first = meta[0] == 0
        powers[...] = jnp.zeros_like(powers)
        for i in range(count):
            held = meta[1 + steps[i]]
            for k in range(blocks):
                mark = selector(pos[held, k : k + 1, :]).astype(jnp.float32)
                sel[k * CAP : (k + 1) * CAP, :] = mark.astype(jnp.bfloat16)

            def chunk(z, _, i=i):
                a, o = mine[i][z, :tokens, :], others[i][z, :tokens, :]
                pair = jnp.concatenate([jnp.where(first, a, o), jnp.where(first, o, a)], axis=1)
                rows_t[i, :, pl.ds(pl.multiple_of(z * 256, 256), 256)] = dot(
                    sel[...], pair, ((1,), (0,))
                ).astype(jnp.bfloat16)
                a = mine[i][z, tokens:, :].astype(jnp.float32)
                o = others[i][z, tokens:, :].astype(jnp.float32)
                parts = []
                for part in (jnp.where(first, a, o), jnp.where(first, o, a)):
                    parts.append(jnp.concatenate([part[: both // 2], part[both // 2 :]], axis=1))
                kept[i, pl.ds(pl.multiple_of(z * both, 16), both), :] = jnp.concatenate(
                    parts, axis=0
                ).astype(jnp.bfloat16)
                return 0

            lax.fori_loop(0, depth, chunk, 0)
            deep_s = kept.shape[1]
            for at in range(0, deep_s, 256):
                end = min(at + 256, deep_s)
                rows_s[i, :, at:end] = dot(sel[...], kept[i, at:end, :], ((1,), (1,))).astype(
                    jnp.bfloat16
                )

    here = pl.ds(pl.multiple_of(b * 2 * CAP, 16), 2 * CAP)
    for h, (rows, head) in enumerate(((rows_t, head_t), (rows_s, head_s))):
        lines = rows[:, here, :].reshape(count * 2 * CAP, rows.shape[-1])
        product = dot(lines, head[...], ((1,), (0,)))
        for i in range(count):
            for k in range(2):
                at = (2 * i + k) * CAP
                values, power = coded(product[at : at + CAP, k * BLOCK : (k + 1) * BLOCK])
                outs[i][0, h, pl.ds(pl.multiple_of((2 * b + k) * CAP, 16), CAP), :] = values
                powers[2 * i + h, pl.ds(2 * b + k, 1), :] = power

    @pl.when(b == pl.num_programs(0) - 1)
    def _():
        for i in range(count):
            for h in range(2):
                outs[i][0, h, blocks * CAP :, :] = (
                    powers[2 * i + h].astype(jnp.int32).astype(jnp.int16)
                )


def partial_logits(meta, pos, steps, mine, others, head_t, head_s):
    count = len(steps)
    tokens = pos.shape[-1]
    deep_t, width = head_t.shape
    deep_s = head_s.shape[0]
    blocks = width // BLOCK
    coded_rows = blocks * CAP + 16
    whole = lambda a: pl.BlockSpec(a.shape, lambda b, meta: (0,) * a.ndim)
    return pl.pallas_call(
        functools.partial(partial_kernel, steps),
        name="partial_logits",
        grid_spec=pltpu.PrefetchScalarGridSpec(
            num_scalar_prefetch=1,
            grid=(blocks // 2,),
            in_specs=[whole(pos)]
            + [whole(a) for a in (*mine, *others)]
            + [
                pl.BlockSpec((deep_t, 2 * BLOCK), lambda b, meta: (0, b)),
                pl.BlockSpec((deep_s, 2 * BLOCK), lambda b, meta: (0, b)),
            ],
            out_specs=[pl.BlockSpec((1, 2, coded_rows, BLOCK), lambda b, meta: (0, 0, 0, 0))] * count
            + [pl.BlockSpec((count, deep_s, tokens), lambda b, meta: (0, 0, 0))],
            scratch_shapes=[
                pltpu.VMEM((blocks * CAP, tokens), jnp.bfloat16),
                pltpu.VMEM((count, blocks * CAP, deep_t), jnp.bfloat16),
                pltpu.VMEM((count, blocks * CAP, deep_s), jnp.bfloat16),
                pltpu.VMEM((2 * count, 16, BLOCK), jnp.float32),
            ],
        ),
        out_shape=[jax.ShapeDtypeStruct((1, 2, coded_rows, BLOCK), jnp.int16)] * count
        + [jax.ShapeDtypeStruct((count, deep_s, tokens), jnp.bfloat16)],
        compiler_params=params(),
        cost_estimate=pl.CostEstimate(
            flops=8 * count * blocks * CAP * (deep_t + deep_s) * tokens,
            bytes_accessed=2 * (deep_t + deep_s) * (width + count * tokens),
            transcendentals=0,
        ),
    )(meta, pos, *mine, *others, head_t, head_s)


def spread(mark, line):
    return jnp.sum(jnp.where(mark, line, jnp.zeros_like(line)), axis=1, keepdims=True)


def fold(mark, column):
    return jnp.sum(jnp.where(mark, column, jnp.zeros_like(column)), axis=0, keepdims=True)


def stats_kernel(pos, target, places, a0, a1, a2, a3, logits, stats):
    blocks = logits.shape[1]
    tokens = pos.shape[-1]
    tops = [jnp.full((1, tokens), NEG, jnp.float32) for _ in range(2)]
    first = blocks * CAP
    powers = [
        [a[0, h, first:, :].astype(jnp.int32).astype(jnp.float32) for a in (a0, a1, a2, a3)]
        for h in range(2)
    ]
    for b in range(blocks):
        mark = selector(pos[b : b + 1, :])
        for h in range(2):
            total = 0.0
            for a, power in zip((a0, a1, a2, a3), powers[h]):
                total = total + decoded(a[0, h, b * CAP : (b + 1) * CAP, :], power[b : b + 1, :])
            logits[h, b] = total
            peak = jnp.max(total, axis=1, keepdims=True)
            tops[h] = jnp.maximum(
                tops[h], jnp.max(jnp.where(mark, peak, NEG), axis=0, keepdims=True)
            )
    zero = jnp.zeros((1, tokens), jnp.float32)
    sum_t, cross, sum_s, picked = zero, zero, zero, zero
    lanes = lax.broadcasted_iota(jnp.int32, (CAP, BLOCK), 1)
    for b in range(blocks):
        mark = selector(pos[b : b + 1, :])
        lt, ls = logits[0, b], logits[1, b]
        et = jnp.exp(lt - spread(mark, tops[0]))
        es = jnp.exp(ls - spread(mark, tops[1]))
        wanted = spread(mark, target[...] - b * BLOCK)
        sum_t = sum_t + fold(mark, jnp.sum(et, axis=1, keepdims=True))
        cross = cross + fold(mark, jnp.sum(et * (lt - ls), axis=1, keepdims=True))
        sum_s = sum_s + fold(mark, jnp.sum(es, axis=1, keepdims=True))
        picked = picked + fold(
            mark, jnp.sum(jnp.where(lanes == wanted, ls, 0.0), axis=1, keepdims=True)
        )
    most = jnp.max(places[...].astype(jnp.float32), axis=(0, 1))[None]
    most = jnp.broadcast_to(jnp.max(most, axis=1, keepdims=True), zero.shape)
    lines = [tops[0], sum_t, cross, tops[1], sum_s, picked, most, zero]
    stats[...] = jnp.concatenate(lines, axis=0)


def row_stats(pos, target, places, parts):
    blocks = parts[0].shape[2] // CAP
    return pl.pallas_call(
        stats_kernel,
        name="row_stats",
        out_shape=[
            jax.ShapeDtypeStruct((2, blocks, CAP, BLOCK), jnp.float32),
            jax.ShapeDtypeStruct((8, pos.shape[-1]), jnp.float32),
        ],
        compiler_params=params(),
    )(pos, target, places, *parts)


def combined(seen):
    top_t = jnp.max(seen[:, 0, :], axis=0, keepdims=True)
    top_s = jnp.max(seen[:, 3, :], axis=0, keepdims=True)
    scale_t = jnp.exp(seen[:, 0, :] - top_t)
    scale_s = jnp.exp(seen[:, 3, :] - top_s)
    total = lambda a: jnp.sum(a, axis=0, keepdims=True)
    sum_t = total(seen[:, 1, :] * scale_t)
    cross = total(seen[:, 2, :] * scale_t)
    sum_s = total(seen[:, 4, :] * scale_s)
    picked = total(seen[:, 5, :])
    log_t = top_t + jnp.log(sum_t)
    log_s = top_s + jnp.log(sum_s)
    return top_t, sum_t, top_s, sum_s, cross / sum_t - log_t + log_s, picked - log_s


def grad_kernel(pos, seen, logits, grad, rows):
    top_t, sum_t, top_s, sum_s, row_kl, logprob = combined(seen[...])
    most = jnp.max(seen[:, 6, :], axis=0, keepdims=True)
    rows[...] = jnp.concatenate([row_kl, logprob, most] + [most] * 5, axis=0)
    inv_t, inv_s = 1.0 / sum_t, 1.0 / sum_s
    for b in range(logits.shape[1]):
        mark = selector(pos[b : b + 1, :])
        et = jnp.exp(logits[0, b] - spread(mark, top_t)) * spread(mark, inv_t)
        es = jnp.exp(logits[1, b] - spread(mark, top_s)) * spread(mark, inv_s)
        grad[b] = (es - et).astype(jnp.bfloat16)


def row_grads(pos, seen, logits):
    return pl.pallas_call(
        grad_kernel,
        name="row_grads",
        out_shape=[
            jax.ShapeDtypeStruct(logits.shape[1:], jnp.bfloat16),
            jax.ShapeDtypeStruct((8, pos.shape[-1]), jnp.float32),
        ],
        compiler_params=params(),
    )(pos, seen, logits)


def head_kernel(meta, places, *refs):
    *studs, out, left = refs
    grads, studs = studs[:4], studs[4:]
    tokens = places.shape[-1]
    b = pl.program_id(0)

    @pl.when(b == 0)
    def _():
        step = 1
        for ref in studs:
            for i in range(ref.shape[0]):
                at = pl.multiple_of(meta[step] * tokens, tokens)
                left[:, pl.ds(at, tokens)] = ref[i]
                step += 1

    right = []
    for t, grad in enumerate(grads):
        pair = []
        for k in range(2):
            mark = selector(places[t, 2 * b + k][None]).astype(jnp.float32).astype(jnp.bfloat16)
            pair.append(dot(mark, grad[k], ((0,), (0,))).astype(jnp.bfloat16))
        right.append(jnp.concatenate(pair, axis=1))
    out[...] = dot(left[...], jnp.concatenate(right, axis=0), ((1,), (0,)))


def head_gradient(meta, places, grads, studs):
    deep, tokens = studs[0].shape[1:]
    blocks = grads[0].shape[0]
    whole = lambda a: pl.BlockSpec(a.shape, lambda b, meta: (0,) * a.ndim)
    return pl.pallas_call(
        head_kernel,
        name="head_gradient",
        grid_spec=pltpu.PrefetchScalarGridSpec(
            num_scalar_prefetch=1,
            grid=(blocks // 2,),
            in_specs=[whole(places)]
            + [pl.BlockSpec((2, CAP, BLOCK), lambda b, meta: (b, 0, 0)) for _ in grads]
            + [whole(a) for a in studs],
            out_specs=pl.BlockSpec((deep, 2 * BLOCK), lambda b, meta: (0, b)),
            scratch_shapes=[pltpu.VMEM((deep, 4 * tokens), jnp.bfloat16)],
        ),
        out_shape=jax.ShapeDtypeStruct((deep, blocks * BLOCK), jnp.float32),
        compiler_params=params(),
    )(meta, places, *grads, *studs)


def build(sx, sz, sc):
    turn = lambda step: [
        (x * sx + y, ((y + step - x) % sx) * sx + y) for x in range(sx) for y in range(sx)
    ]
    spread_out = [(x * sx + y, y * sx + (x + y) % sx) for x in range(sx) for y in range(sx)]
    shift = lambda step: [(y, (y + step) % sx) for y in range(sx)]

    def to_owner(a, step):
        return lax.ppermute(a, ("x", "y"), turn(step))

    def both_cores(mine):
        if sc == 1:
            return mine[:, None]
        other = lax.ppermute(mine, "c", [(0, 1), (1, 0)])
        first = lax.axis_index("c") == 0
        return jnp.stack([jnp.where(first, mine, other), jnp.where(first, other, mine)], axis=1)

    def features(pay, tokens):
        full = both_cores(pay)
        chunks = full.shape[0] * full.shape[1]
        full = full.reshape(chunks, -1, BLOCK)
        teach = full[:, :tokens]
        stud = full[:, tokens:].reshape(chunks, tokens // BLOCK, -1, BLOCK)
        stud = stud.transpose(0, 2, 1, 3).reshape(-1, tokens)
        return teach, stud

    def neighbours(pay):
        after = lax.ppermute(pay, "y", shift(-1))
        before = lax.ppermute(pay, "y", shift(1))
        return after, before

    def opposite(after, before):
        half = after.shape[0] // 2
        if half == 0:
            return lax.ppermute(after, "y", shift(-1))
        low = lax.ppermute(after[:half], "y", shift(-1))
        high = lax.ppermute(before[half:], "y", shift(1))
        return jnp.concatenate([low, high], axis=0)

    def everyone(stats):
        copies = jnp.broadcast_to(stats[None], (sx * sz * sc, *stats.shape))
        return lax.all_to_all(copies, LOCAL, split_axis=0, concat_axis=0, tiled=True)

    def dense(pays, head_t, head_s, allowed, target):
        tokens, blocks = allowed.shape
        width = head_t.shape[1]
        studs, total = {}, 0.0
        for step in range(sx):
            teach, stud = features(pays[step], tokens)
            studs[step] = stud
            teach = teach.transpose(1, 0, 2).reshape(tokens, -1)
            part = jnp.concatenate(
                [dot(teach, head_t, ((1,), (0,))), dot(stud, head_s, ((0,), (0,)))], axis=1
            )
            total = total + to_owner(part, step)
        lt, ls = total[:, :width], total[:, width:]
        open_ = jnp.broadcast_to((allowed > 0)[:, :, None], (tokens, blocks, BLOCK))
        open_ = open_.reshape(tokens, width)
        ids = jnp.arange(width, dtype=jnp.int32)
        picked = jnp.sum(jnp.where(ids[None, :] == target[:, None], ls, 0.0), axis=1)
        top_t = jnp.max(jnp.where(open_, lt, NEG), axis=1)
        top_s = jnp.max(jnp.where(open_, ls, NEG), axis=1)
        et = jnp.where(open_, jnp.exp(jnp.where(open_, lt, NEG) - top_t[:, None]), 0.0)
        es = jnp.where(open_, jnp.exp(jnp.where(open_, ls, NEG) - top_s[:, None]), 0.0)
        lines = [top_t, et.sum(1), (et * (lt - ls)).sum(1), top_s, es.sum(1), picked]
        stats = jnp.stack(lines + [jnp.zeros_like(top_t)] * 2)
        all_t, sum_t, all_s, sum_s, row_kl, logprob = combined(everyone(stats))
        scale_t = (jnp.exp(top_t[None] - all_t) / sum_t)[0]
        scale_s = (jnp.exp(top_s[None] - all_s) / sum_s)[0]
        grad = (es * scale_s[:, None] - et * scale_t[:, None]).astype(jnp.bfloat16)
        head = sum(
            dot(studs[step], to_owner(grad, step), ((1,), (0,))) for step in range(sx)
        )
        return row_kl[0], logprob[0], head

    def other_core(pay):
        return lax.ppermute(pay, "c", [(0, 1), (1, 0)]) if sc > 1 else pay

    def per_device(teacher_hidden, student_hidden, head_t, head_s, allowed, sampled):
        tokens, blocks = allowed.shape
        width = head_t.shape[1]
        stud = student_hidden.T.reshape(-1, tokens // BLOCK, BLOCK).transpose(1, 0, 2)
        pay = jnp.concatenate([teacher_hidden, stud.reshape(-1, BLOCK)], axis=0)
        pay = lax.ppermute(pay, ("x", "y"), spread_out)
        open_ = (allowed > 0).T.astype(jnp.float32)
        before = jnp.triu(jnp.ones((tokens, tokens), jnp.float32), 1)
        place = dot(open_.astype(jnp.bfloat16), before.astype(jnp.bfloat16), ((1,), (0,)))
        own_pos = jnp.where(open_ > 0, place.astype(jnp.int32), -1)
        own_pos = jnp.pad(own_pos, ((0, -blocks % 8), (0, 0)), constant_values=-1)
        order = (0, 1, 3, 2)
        from_line = lambda a, far: lax.ppermute(a, "x", [(x, (x - far) % sx) for x in range(sx)])
        places = [own_pos] + [from_line(own_pos, far) for far in range(1, sx)]
        pay, places = lax.optimization_barrier((pay, places))
        places = jnp.stack(places)
        pay = lax.all_to_all(
            jnp.broadcast_to(pay[None], (sz, *pay.shape)), "z", 0, 0, tiled=True
        )
        here, row, core = (lax.axis_index(name).astype(jnp.int32) for name in ("x", "y", "c"))
        meta = jnp.stack([core] + [(row + step - 2 * here) % sx for step in order])
        place_of = (row * sz + lax.axis_index("z")) * sc + core
        target = sampled - place_of * width

        def run(steps, mine, others):
            return partial_logits(meta, places, steps, mine, others, head_t, head_s)

        pay, other = lax.optimization_barrier((pay, other_core(pay)))
        after, ahead = neighbours(pay)
        part, stud0 = run((0,), [pay], [other])
        got = [to_owner(part, order[0])]
        far = opposite(after, ahead)
        part, other_part, stud1 = run((1, 2), [after, ahead], [other_core(after), other_core(ahead)])
        got += [to_owner(part, order[1]), to_owner(other_part, order[2])]
        part, stud2 = run((3,), [far], [other_core(far)])
        got.append(to_owner(part, order[3]))

        logits, stats = row_stats(own_pos, target[None], places, got)
        grad, rows = row_grads(own_pos, everyone(stats), logits)
        grads = [grad] + [from_line(grad, far) for far in range(1, sx)]
        head = head_gradient(meta, places, grads, [stud0, stud1, stud2])
        start = (rows[2, 0] >= CAP, rows[0], rows[1], head)
        pays = {0: pay, 1: after, 3: ahead, 2: far}

        def redo(_):
            return (False, *dense(pays, head_t, head_s, allowed, target))

        return lax.while_loop(lambda held: held[0], redo, start)[1:]

    return per_device


def solution(mesh, sizes=(4, 8, 2)):
    sx, sz, sc = sizes
    grid = Mesh(mesh.devices.reshape(sx, sx, sz, sc), ("x", "y", "z", "c"))
    both = P("x", LOCAL)
    return jax.shard_map(
        build(sx, sz, sc),
        mesh=grid,
        in_specs=(both, both, both, both, both, P("x")),
        out_specs=(P("x"), P("x"), both),
        check_vma=False,
    )
```

profile of v0, /device:TPU:1, one launch (start us, length us, event | category | flops | bytes accessed | tf_op | source)
XLA Modules:
  0.0 180.0 jit_solution(9880640254504944122)
XLA Ops:
  0.6 0.8 reshape.122
  1.4 0.8 pad_maximum_fusion.8
  2.3 0.7 collective-permute-start.12
  2.9 0.9 fusion.40
  3.9 7.3 %collective-permute-start.13 = (s32[16,256]{1,0:T(8,128)S(1)}, s32[16,256]{1,0:T(8,128)S(1)}, u32[]{:S(2)}, u32[]{:S(2)}) collective-permute-start(s32[16,256]{1,0:T(8,128)S(1)} %pad.4.pos), channel_id=1, source_target_pairs={{0,192},{64,0},{128,64},{192,128},{1,193},{65,1},{129,65},{193,129... | collective-permute-start | bytes 49160 | tf_op jit(solution)/shard_map/ppermute | solution.py:390
  11.1 0.6 collective-permute-start.14
  11.7 0.8 collective-permute-start.15
  12.5 0.0 collective-permute-done.13
  12.5 2.8 %collective-permute-done.14 = s32[16,256]{1,0:T(8,128)S(1)} collective-permute-done((s32[16,256]{1,0:T(8,128)S(1)}, s32[16,256]{1,0:T(8,128)S(1)}, u32[]{:S(2)}, u32[]{:S(2)}) %collective-permute-start.14) | collective-permute-done | bytes 16416 | tf_op jit(solution)/shard_map/ppermute | solution.py:390
  15.2 0.3 collective-permute-done.15
  15.5 0.0 collective-permute-done.12
  15.5 0.1 broadcast_in_dim.66
  15.6 27.6 %all_to_all.15.refs_0_ = bf16[8,368,128]{2,1,0:T(8,128)(2,1)S(1)} all-to-all(bf16[8,368,128]{2,1,0:T(8,128)(2,1)S(1)} %broadcast_in_dim.66), channel_id=1, replica_groups=mesh['x'=4,'y'=4,'z'=8,'c'=2] {'z'}, dimensions={0} | all-to-all | bytes 1507328 | tf_op jit(solution)/shard_map/all_to_all | solution.py:394
  43.2 3.8 %collective-permute-start.16 = (bf16[8,368,128]{2,1,0:T(8,128)(2,1)S(1)}, bf16[8,368,128]{2,1,0:T(8,128)(2,1)S(1)}, u32[]{:S(2)}, u32[]{:S(2)}) collective-permute-start(bf16[8,368,128]{2,1,0:T(8,128)(2,1)S(1)} %all_to_all.15.refs_0_), channel_id=1, source_target_pairs={{0,1},{1,0},{2,3},{3,2},{4,5},{5,4},{6,7},{7,6},{8,9},{9,8},{10,11... | collective-permute-start | bytes 2261000 | tf_op jit(solution)/shard_map/ppermute | solution.py:376
  47.0 1.9 %collective-permute-done.16.refs_1_ = bf16[8,368,128]{2,1,0:T(8,128)(2,1)S(1)} collective-permute-done((bf16[8,368,128]{2,1,0:T(8,128)(2,1)S(1)}, bf16[8,368,128]{2,1,0:T(8,128)(2,1)S(1)}, u32[]{:S(2)}, u32[]{:S(2)}) %collective-permute-start.16) | collective-permute-done | bytes 753696 | tf_op jit(solution)/shard_map/ppermute | solution.py:376
  48.8 1.8 %collective-permute-start.18 = (bf16[8,368,128]{2,1,0:T(8,128)(2,1)S(1)}, bf16[8,368,128]{2,1,0:T(8,128)(2,1)}, u32[]{:S(2)}, u32[]{:S(2)}) collective-permute-start(bf16[8,368,128]{2,1,0:T(8,128)(2,1)S(1)} %all_to_all.15.refs_0_), channel_id=1, source_target_pairs={{0,48},{16,0},{32,16},{48,32},{1,49},{17,1},{33,17},{49,33},{2,50}... | collective-permute-start | bytes 2261000 | tf_op jit(solution)/shard_map/ppermute | solution.py:327
  50.7 0.0 collective-permute-start.19
  50.7 0.1 stack.100.meta
  50.8 16.2 %collective-permute-done.18.refs_0_ = bf16[8,368,128]{2,1,0:T(8,128)(2,1)} collective-permute-done((bf16[8,368,128]{2,1,0:T(8,128)(2,1)S(1)}, bf16[8,368,128]{2,1,0:T(8,128)(2,1)}, u32[]{:S(2)}, u32[]{:S(2)}) %collective-permute-start.18) | collective-permute-done | bytes 753696 | tf_op jit(solution)/shard_map/ppermute | solution.py:327
  67.0 1.2 collective-permute-start.20
  68.2 1.5 collective-permute-done.19.refs_1_
  69.7 1.5 collective-permute-start.21
  71.2 1.0 slice.86
  72.3 0.1 collective-permute-start.24
  72.4 0.0 slice-start
  72.4 1.2 slice.87
  73.5 0.0 slice-start.1
  73.5 1.5 collective-permute-start.25
  75.1 10.0 %partial_logits.3 = (s16[1,2,816,128]{3,2,1,0:T(8,128)(2,1)}, bf16[1,896,256]{2,1,0:T(8,128)(2,1)S(1)}) custom-call(s32[5]{0:T(128)S(1)} %stack.100.meta, s32[4,16,256]{2,1,0:T(8,128)S(1)} %pad_add_fusion.pos.places, bf16[8,368,128]{2,1,0:T(8,128)(2,1)S(1)} %all_to_all.15.refs_0_, bf16[8,368,128]{2,1,0:T(8,128)(2,1)S(1)} %collective-permute-done.16.refs_1_, ...), custom_call_target="tpu_custom_call" | custom-call | flops 4823449600 | bytes 9043968 | tf_op jit(solution)/shard_map/partial_logits/pallas_call | solution.py:121
  85.1 1.7 collective-permute-start.17
  86.8 0.0 collective-permute-done.24
  86.8 0.8 constant_dynamic-update-slice_fusion.1
  87.5 0.0 collective-permute-done.25
  87.5 0.8 constant_dynamic-update-slice_fusion.refs_0_
  88.3 0.6 collective-permute-start.26
  88.8 0.0 collective-permute-done.20.refs_2_
  88.9 0.0 collective-permute-done.21.refs_3_
  88.9 0.0 slice-done.1
  88.9 0.0 copy-done
  88.9 13.0 %partial_logits.4 = (s16[1,2,816,128]{3,2,1,0:T(8,128)(2,1)}, s16[1,2,816,128]{3,2,1,0:T(8,128)(2,1)}, bf16[2,896,256]{2,1,0:T(8,128)(2,1)S(1)}) custom-call(s32[5]{0:T(128)S(1)} %stack.100.meta, s32[4,16,256]{2,1,0:T(8,128)S(1)} %pad_add_fusion.pos.places, bf16[8,368,128]{2,1,0:T(8,128)(2,1)} %collective-permute-done.18.refs_0_, ...), custom_call_target="tpu_custom_call" | custom-call | flops 9646899200 | bytes 10551296 | tf_op jit(solution)/shard_map/partial_logits/pallas_call | solution.py:121
  101.9 4.2 %collective-permute-start.22 = (s16[1,2,816,128]{3,2,1,0:T(8,128)(2,1)}, s16[1,2,816,128]{3,2,1,0:T(8,128)(2,1)S(1)}, u32[]{:S(2)}, u32[]{:S(2)}) collective-permute-start(s16[1,2,816,128]{3,2,1,0:T(8,128)(2,1)} %get-tuple-element.89), channel_id=1, source_target_pairs={{0,64},{16,144},{32,224},{48,48},{64,0},{80,80},{96,160},{112,240}... | collective-permute-start | bytes 1253384 | tf_op jit(solution)/shard_map/ppermute | solution.py:308
  106.1 0.0 copy-start.22
  106.1 3.3 %collective-permute-start.23 = (s16[1,2,816,128]{3,2,1,0:T(8,128)(2,1)}, s16[1,2,816,128]{3,2,1,0:T(8,128)(2,1)S(1)}, u32[]{:S(2)}, u32[]{:S(2)}) collective-permute-start(s16[1,2,816,128]{3,2,1,0:T(8,128)(2,1)} %get-tuple-element.90), channel_id=1, source_target_pairs={{0,192},{16,16},{32,96},{48,176},{64,128},{80,208},{96,32},{112,11... | collective-permute-start | bytes 1253384 | tf_op jit(solution)/shard_map/ppermute | solution.py:308
  109.4 0.0 collective-permute-done.26.refs_1_
  109.4 8.5 %partial_logits.5 = (s16[1,2,816,128]{3,2,1,0:T(8,128)(2,1)}, bf16[1,896,256]{2,1,0:T(8,128)(2,1)S(1)}) custom-call(s32[5]{0:T(128)S(1)} %stack.100.meta, s32[4,16,256]{2,1,0:T(8,128)S(1)} %pad_add_fusion.pos.places, bf16[8,368,128]{2,1,0:T(8,128)(2,1)} %constant_dynamic-update-slice_fusion.refs_0_, ...), custom_call_target="tpu_custom_call" | custom-call | flops 4823449600 | bytes 9043968 | tf_op jit(solution)/shard_map/partial_logits/pallas_call | solution.py:121
  117.9 3.1 %collective-permute-start.27 = (s16[1,2,816,128]{3,2,1,0:T(8,128)(2,1)}, s16[1,2,816,128]{3,2,1,0:T(8,128)(2,1)}, u32[]{:S(2)}, u32[]{:S(2)}) collective-permute-start(s16[1,2,816,128]{3,2,1,0:T(8,128)(2,1)} %get-tuple-element.91), channel_id=1, source_target_pairs={{0,128},{16,208},{32,32},{48,112},{64,64},{80,144},{96,224},{112,4... | collective-permute-start | bytes 1253384 | tf_op jit(solution)/shard_map/ppermute | solution.py:308
  121.0 0.0 copy-done.22
  121.1 0.0 collective-permute-done.17.a0
  121.1 0.0 collective-permute-done.22.a1
  121.1 0.0 collective-permute-done.23.a2
  121.1 11.4 %collective-permute-done.27.a3 = s16[1,2,816,128]{3,2,1,0:T(8,128)(2,1)} collective-permute-done((s16[1,2,816,128]{3,2,1,0:T(8,128)(2,1)}, s16[1,2,816,128]{3,2,1,0:T(8,128)(2,1)}, u32[]{:S(2)}, u32[]{:S(2)}) %collective-permute-start.27) | collective-permute-done | bytes 417824 | tf_op jit(solution)/shard_map/ppermute | solution.py:308
  132.6 5.0 %row_stats.1 = (f32[2,10,80,128]{3,2,1,0:T(8,128)S(1)}, f32[8,256]{1,0:T(8,128)S(1)}) custom-call(s32[16,256]{1,0:T(8,128)S(1)} %pad.4.pos, s32[1,256]{1,0:T(1,128)S(1)} %bitcast.183, s32[4,16,256]{2,1,0:T(8,128)S(1)} %pad_add_fusion.pos.places, s16[1,2,816,128]{3,2,1,0:T(8,128)(2,1)S(1)} %collective-permute-done.17.a0, ...), custom_call_target="tpu_custom_call" | custom-call | tf_op jit(solution)/shard_map/row_stats/pallas_call | solution.py:204
  137.6 21.7 %all_to_all.16.seen = f32[64,8,256]{2,1,0:T(8,128)S(1)} all-to-all(f32[64,8,256]{2,1,0:T(8,128)S(1)} %broadcast_in_dim.67), channel_id=1, replica_groups=mesh['x'=4,'y'=4,'z'=8,'c'=2] {'y','z','c'}, dimensions={0} | all-to-all | bytes 1048576 | tf_op jit(solution)/shard_map/all_to_all | solution.py:341
  159.3 0.8 row_grads.1
  160.2 0.1 collective-permute-start.28
  160.2 1.3 collective-permute-start.29
  161.5 0.8 collective-permute-start.30
  162.3 0.5 slice.67
  163.4 0.6 fusion.50
  164.0 2.6 %collective-permute-done.28.refs_1_ = bf16[10,80,128]{2,1,0:T(8,128)(2,1)S(1)} collective-permute-done((bf16[10,80,128]{2,1,0:T(8,128)(2,1)S(1)}, bf16[10,80,128]{2,1,0:T(8,128)(2,1)S(1)}, u32[]{:S(2)}, u32[]{:S(2)}) %collective-permute-start.28) | collective-permute-done | bytes 204832 | tf_op jit(solution)/shard_map/ppermute | solution.py:390
  166.6 1.6 collective-permute-done.29.refs_2_
  168.2 5.0 %collective-permute-done.30.refs_3_ = bf16[10,80,128]{2,1,0:T(8,128)(2,1)S(1)} collective-permute-done((bf16[10,80,128]{2,1,0:T(8,128)(2,1)S(1)}, bf16[10,80,128]{2,1,0:T(8,128)(2,1)S(1)}, u32[]{:S(2)}, u32[]{:S(2)}) %collective-permute-start.30) | collective-permute-done | bytes 204832 | tf_op jit(solution)/shard_map/ppermute | solution.py:390
  173.2 6.3 %head_gradient.1 = f32[896,1280]{1,0:T(8,128)} custom-call(s32[5]{0:T(128)S(1)} %stack.100.meta, s32[4,16,256]{2,1,0:T(8,128)S(1)} %pad_add_fusion.pos.places, bf16[10,80,128]{2,1,0:T(8,128)(2,1)S(1)} %get-tuple-element.95.refs_0_, bf16[10,80,128]{2,1,0:T(8,128)(2,1)S(1)} %collective-permute-done.28.refs_1_, ...), custom_call_target="tpu_custom_call" | custom-call | tf_op jit(solution)/shard_map/head_gradient/pallas_call | solution.py:283
  179.6 0.2 while.13
  (18 shorter events, 0.1 us)
Async XLA Ops:
  2.3 13.3 %collective-permute-start.12 = (bf16[368,128]{1,0:T(8,128)(2,1)S(1)}, bf16[368,128]{1,0:T(8,128)(2,1)S(1)}, u32[]{:S(2)}, u32[]{:S(2)}) collective-permute-start(bf16[368,128]{1,0:T(8,128)(2,1)S(1)} %pad_maximum_fusion.8), channel_id=1, source_target_pairs={{0,0},{16,80},{32,160},{48,240},{64,16},{80,96},{96,176},{112,192}... | collective-permute-start | bytes 282632 | tf_op jit(solution)/shard_map/ppermute | solution.py:383
  3.9 8.6 %collective-permute-start.13 = (s32[16,256]{1,0:T(8,128)S(1)}, s32[16,256]{1,0:T(8,128)S(1)}, u32[]{:S(2)}, u32[]{:S(2)}) collective-permute-start(s32[16,256]{1,0:T(8,128)S(1)} %pad.4.pos), channel_id=1, source_target_pairs={{0,192},{64,0},{128,64},{192,128},{1,193},{65,1},{129,65},{193,129... | collective-permute-start | bytes 49160 | tf_op jit(solution)/shard_map/ppermute | solution.py:390
  11.1 4.1 %collective-permute-start.14 = (s32[16,256]{1,0:T(8,128)S(1)}, s32[16,256]{1,0:T(8,128)S(1)}, u32[]{:S(2)}, u32[]{:S(2)}) collective-permute-start(s32[16,256]{1,0:T(8,128)S(1)} %pad.4.pos), channel_id=1, source_target_pairs={{0,128},{64,192},{128,0},{192,64},{1,129},{65,193},{129,1},{193,65... | collective-permute-start | bytes 49160 | tf_op jit(solution)/shard_map/ppermute | solution.py:390
  11.7 3.8 %collective-permute-start.15 = (s32[16,256]{1,0:T(8,128)S(1)}, s32[16,256]{1,0:T(8,128)S(1)}, u32[]{:S(2)}, u32[]{:S(2)}) collective-permute-start(s32[16,256]{1,0:T(8,128)S(1)} %pad.4.pos), channel_id=1, source_target_pairs={{0,64},{64,128},{128,192},{192,0},{1,65},{65,129},{129,193},{193,1... | collective-permute-start | bytes 49160 | tf_op jit(solution)/shard_map/ppermute | solution.py:390
  43.2 41.9 %copy-start.16 = (bf16[8,368,128]{2,1,0:T(8,128)(2,1)}, bf16[8,368,128]{2,1,0:T(8,128)(2,1)S(1)}, u32[]{:S(2)}) copy-start(bf16[8,368,128]{2,1,0:T(8,128)(2,1)S(1)} %all_to_all.15.refs_0_) | copy-start | bytes 2260996
  43.2 5.6 %collective-permute-start.16 = (bf16[8,368,128]{2,1,0:T(8,128)(2,1)S(1)}, bf16[8,368,128]{2,1,0:T(8,128)(2,1)S(1)}, u32[]{:S(2)}, u32[]{:S(2)}) collective-permute-start(bf16[8,368,128]{2,1,0:T(8,128)(2,1)S(1)} %all_to_all.15.refs_0_), channel_id=1, source_target_pairs={{0,1},{1,0},{2,3},{3,2},{4,5},{5,4},{6,7},{7,6},{8,9},{9,8},{10,11... | collective-permute-start | bytes 2261000 | tf_op jit(solution)/shard_map/ppermute | solution.py:376
  48.8 18.1 %collective-permute-start.18 = (bf16[8,368,128]{2,1,0:T(8,128)(2,1)S(1)}, bf16[8,368,128]{2,1,0:T(8,128)(2,1)}, u32[]{:S(2)}, u32[]{:S(2)}) collective-permute-start(bf16[8,368,128]{2,1,0:T(8,128)(2,1)S(1)} %all_to_all.15.refs_0_), channel_id=1, source_target_pairs={{0,48},{16,0},{32,16},{48,32},{1,49},{17,1},{33,17},{49,33},{2,50}... | collective-permute-start | bytes 2261000 | tf_op jit(solution)/shard_map/ppermute | solution.py:327
  50.7 19.1 %collective-permute-start.19 = (bf16[8,368,128]{2,1,0:T(8,128)(2,1)S(1)}, bf16[8,368,128]{2,1,0:T(8,128)(2,1)}, u32[]{:S(2)}, u32[]{:S(2)}) collective-permute-start(bf16[8,368,128]{2,1,0:T(8,128)(2,1)S(1)} %all_to_all.15.refs_0_), channel_id=1, source_target_pairs={{0,16},{16,32},{32,48},{48,0},{1,17},{17,33},{33,49},{49,1},{2,18}... | collective-permute-start | bytes 2261000 | tf_op jit(solution)/shard_map/ppermute | solution.py:328
  67.0 21.9 %collective-permute-start.20 = (bf16[8,368,128]{2,1,0:T(8,128)(2,1)}, bf16[8,368,128]{2,1,0:T(8,128)(2,1)S(1)}, u32[]{:S(2)}, u32[]{:S(2)}) collective-permute-start(bf16[8,368,128]{2,1,0:T(8,128)(2,1)} %collective-permute-done.18.refs_0_), channel_id=1, source_target_pairs={{0,1},{1,0},{2,3},{3,2},{4,5},{5,4},{6,7},{7,6},{8,9},{9,8},{10,11... | collective-permute-start | bytes 2261000 | tf_op jit(solution)/shard_map/ppermute | solution.py:376
  69.7 19.1 %collective-permute-start.21 = (bf16[8,368,128]{2,1,0:T(8,128)(2,1)}, bf16[8,368,128]{2,1,0:T(8,128)(2,1)S(1)}, u32[]{:S(2)}, u32[]{:S(2)}) collective-permute-start(bf16[8,368,128]{2,1,0:T(8,128)(2,1)} %collective-permute-done.19.refs_1_), channel_id=1, source_target_pairs={{0,1},{1,0},{2,3},{3,2},{4,5},{5,4},{6,7},{7,6},{8,9},{9,8},{10,11... | collective-permute-start | bytes 2261000 | tf_op jit(solution)/shard_map/ppermute | solution.py:376
  72.3 14.5 %collective-permute-start.24 = (bf16[4,368,128]{2,1,0:T(8,128)(2,1)S(1)}, bf16[4,368,128]{2,1,0:T(8,128)(2,1)S(1)}, u32[]{:S(2)}, u32[]{:S(2)}) collective-permute-start(bf16[4,368,128]{2,1,0:T(8,128)(2,1)S(1)} %slice.86), channel_id=1, source_target_pairs={{0,48},{16,0},{32,16},{48,32},{1,49},{17,1},{33,17},{49,33},{2,50}... | collective-permute-start | bytes 1130504 | tf_op jit(solution)/shard_map/ppermute | solution.py:335
  72.4 16.5 %slice-start = ((s8[5242880]{0:T(1024)(128)(4,1)}), s8[4194304]{0:T(1024)(128)(4,1)S(1)}, s32[]{:S(2)}) async-start(s8[5242880]{0:T(1024)(128)(4,1)} %bitcast.148), calls=%async_computation.3 | async-start | bytes 8388608
  73.5 15.3 %slice-start.1 = ((s8[5242880]{0:T(1024)(128)(4,1)}), s8[1048576]{0:T(1024)(128)(4,1)S(1)}, s32[]{:S(2)}) async-start(s8[5242880]{0:T(1024)(128)(4,1)} %bitcast.148), calls=%async_computation.4 | async-start | bytes 2097152
  73.5 14.0 %collective-permute-start.25 = (bf16[4,368,128]{2,1,0:T(8,128)(2,1)S(1)}, bf16[4,368,128]{2,1,0:T(8,128)(2,1)S(1)}, u32[]{:S(2)}, u32[]{:S(2)}) collective-permute-start(bf16[4,368,128]{2,1,0:T(8,128)(2,1)S(1)} %slice.87), channel_id=1, source_target_pairs={{0,16},{16,32},{32,48},{48,0},{1,17},{17,33},{33,49},{49,1},{2,18}... | collective-permute-start | bytes 1130504 | tf_op jit(solution)/shard_map/ppermute | solution.py:336
  75.1 13.8 %copy-start = (bf16[896,1280]{1,0:T(8,128)(2,1)S(1)}, bf16[896,1280]{1,0:T(8,128)(2,1)}, u32[]{:S(2)}) copy-start(bf16[896,1280]{1,0:T(8,128)(2,1)} %refs_3_.3) | copy-start | bytes 6881284
  85.1 36.0 %collective-permute-start.17 = (s16[1,2,816,128]{3,2,1,0:T(8,128)(2,1)}, s16[1,2,816,128]{3,2,1,0:T(8,128)(2,1)S(1)}, u32[]{:S(2)}, u32[]{:S(2)}) collective-permute-start(s16[1,2,816,128]{3,2,1,0:T(8,128)(2,1)} %get-tuple-element.88), channel_id=1, source_target_pairs={{0,0},{16,80},{32,160},{48,240},{64,192},{80,16},{96,96},{112,176}... | collective-permute-start | bytes 1253384 | tf_op jit(solution)/shard_map/ppermute | solution.py:308
  88.3 21.1 %collective-permute-start.26 = (bf16[8,368,128]{2,1,0:T(8,128)(2,1)}, bf16[8,368,128]{2,1,0:T(8,128)(2,1)S(1)}, u32[]{:S(2)}, u32[]{:S(2)}) collective-permute-start(bf16[8,368,128]{2,1,0:T(8,128)(2,1)} %constant_dynamic-update-slice_fusion.refs_0_), channel_id=1, source_target_pairs={{0,1},{1,0},{2,3},{3,2},{4,5},{5,4},{6,7},{7,6},{8,9},{9,8},{10,11... | collective-permute-start | bytes 2261000 | tf_op jit(solution)/shard_map/ppermute | solution.py:376
  101.9 19.2 %collective-permute-start.22 = (s16[1,2,816,128]{3,2,1,0:T(8,128)(2,1)}, s16[1,2,816,128]{3,2,1,0:T(8,128)(2,1)S(1)}, u32[]{:S(2)}, u32[]{:S(2)}) collective-permute-start(s16[1,2,816,128]{3,2,1,0:T(8,128)(2,1)} %get-tuple-element.89), channel_id=1, source_target_pairs={{0,64},{16,144},{32,224},{48,48},{64,0},{80,80},{96,160},{112,240}... | collective-permute-start | bytes 1253384 | tf_op jit(solution)/shard_map/ppermute | solution.py:308
  106.1 14.9 %copy-start.22 = (s32[256]{0:T(256)S(1)}, s32[256]{0:T(256)}, u32[]{:S(2)}) copy-start(s32[256]{0:T(256)} %param.13) | copy-start | bytes 3076
  106.1 15.0 %collective-permute-start.23 = (s16[1,2,816,128]{3,2,1,0:T(8,128)(2,1)}, s16[1,2,816,128]{3,2,1,0:T(8,128)(2,1)S(1)}, u32[]{:S(2)}, u32[]{:S(2)}) collective-permute-start(s16[1,2,816,128]{3,2,1,0:T(8,128)(2,1)} %get-tuple-element.90), channel_id=1, source_target_pairs={{0,192},{16,16},{32,96},{48,176},{64,128},{80,208},{96,32},{112,11... | collective-permute-start | bytes 1253384 | tf_op jit(solution)/shard_map/ppermute | solution.py:308
  117.9 14.6 %collective-permute-start.27 = (s16[1,2,816,128]{3,2,1,0:T(8,128)(2,1)}, s16[1,2,816,128]{3,2,1,0:T(8,128)(2,1)}, u32[]{:S(2)}, u32[]{:S(2)}) collective-permute-start(s16[1,2,816,128]{3,2,1,0:T(8,128)(2,1)} %get-tuple-element.91), channel_id=1, source_target_pairs={{0,128},{16,208},{32,32},{48,112},{64,64},{80,144},{96,224},{112,4... | collective-permute-start | bytes 1253384 | tf_op jit(solution)/shard_map/ppermute | solution.py:308
  121.1 38.3 %copy-start.20 = (s32[256]{0:T(256)}, s32[256]{0:T(256)S(1)}, u32[]{:S(2)}) copy-start(s32[256]{0:T(256)S(1)} %broadcast_subtract_fusion) | copy-start | bytes 3076
  160.2 6.4 %collective-permute-start.28 = (bf16[10,80,128]{2,1,0:T(8,128)(2,1)S(1)}, bf16[10,80,128]{2,1,0:T(8,128)(2,1)S(1)}, u32[]{:S(2)}, u32[]{:S(2)}) collective-permute-start(bf16[10,80,128]{2,1,0:T(8,128)(2,1)S(1)} %get-tuple-element.95.refs_0_), channel_id=1, source_target_pairs={{0,192},{64,0},{128,64},{192,128},{1,193},{65,1},{129,65},{193,129... | collective-permute-start | bytes 614408 | tf_op jit(solution)/shard_map/ppermute | solution.py:390
  160.2 8.0 %collective-permute-start.29 = (bf16[10,80,128]{2,1,0:T(8,128)(2,1)S(1)}, bf16[10,80,128]{2,1,0:T(8,128)(2,1)S(1)}, u32[]{:S(2)}, u32[]{:S(2)}) collective-permute-start(bf16[10,80,128]{2,1,0:T(8,128)(2,1)S(1)} %get-tuple-element.95.refs_0_), channel_id=1, source_target_pairs={{0,128},{64,192},{128,0},{192,64},{1,129},{65,193},{129,1},{193,65... | collective-permute-start | bytes 614408 | tf_op jit(solution)/shard_map/ppermute | solution.py:390
  161.5 11.7 %collective-permute-start.30 = (bf16[10,80,128]{2,1,0:T(8,128)(2,1)S(1)}, bf16[10,80,128]{2,1,0:T(8,128)(2,1)S(1)}, u32[]{:S(2)}, u32[]{:S(2)}) collective-permute-start(bf16[10,80,128]{2,1,0:T(8,128)(2,1)S(1)} %get-tuple-element.95.refs_0_), channel_id=1, source_target_pairs={{0,64},{64,128},{128,192},{192,0},{1,65},{65,129},{129,193},{193,1... | collective-permute-start | bytes 614408 | tf_op jit(solution)/shard_map/ppermute | solution.py:390
  173.2 6.3 %copy-start.17 = (bf16[8,368,128]{2,1,0:T(8,128)(2,1)S(1)}, bf16[8,368,128]{2,1,0:T(8,128)(2,1)}, u32[]{:S(2)}) copy-start(bf16[8,368,128]{2,1,0:T(8,128)(2,1)} %copy-done.16) | copy-start | bytes 2260996
  173.2 6.3 %copy-start.19 = (s32[256,10]{0,1:T(8,128)S(1)}, s32[256,10]{0,1:T(8,128)}, u32[]{:S(2)}) copy-start(s32[256,10]{0,1:T(8,128)} %param.12) | copy-start | bytes 30724
  173.2 6.3 %copy-start.21 = (s32[256]{0:T(256)S(1)}, s32[256]{0:T(256)}, u32[]{:S(2)}) copy-start(s32[256]{0:T(256)} %copy-done.20) | copy-start | bytes 3076
where the time goes:
time: 181 us; the launch traced here: 180 us
  blocking collectives  49.3 us (27%)
  Pallas kernels  43.7 us (24%)
  waiting for transfers between devices  43.3 us (24%)
  starting transfers between devices  34.1 us (19%)
  local copies, waits for them, and re-layouts  5.83 us (3%)
    pallas_call x3, Pallas kernels, partial_logits(): pl.pallas_call(functools.partial(partial_kernel, steps), name='partial_lo...  31.6 us
    all_to_all x1, blocking collectives, per_device(): lax.all_to_all(jnp.broadcast_to(pay[None], (sz, *pay.shape)), 'z', 0, 0,...  27.6 us
    all_to_all x1, blocking collectives, everyone(): lax.all_to_all(copies, LOCAL, split_axis=0, concat_axis=0, tiled=True)  21.7 us
    ppermute x1, waiting for transfers between devices, neighbours(): after = lax.ppermute(pay, 'y', shift(-1))  16.2 us
    ppermute x6, waiting for transfers between devices, per_device(): lax.ppermute(a, 'x', [(x, (x - far) % sx) for x in range(sx)])  12.2 us
    ppermute x4, starting transfers between devices, to_owner(): return lax.ppermute(a, ('x', 'y'), turn(step))  12.2 us
    ppermute x4, waiting for transfers between devices, to_owner(): return lax.ppermute(a, ('x', 'y'), turn(step))  11.5 us
    ppermute x6, starting transfers between devices, per_device(): lax.ppermute(a, 'x', [(x, (x - far) % sx) for x in range(sx)])  10.7 us
  transfers between devices with their start and end apart: 19, of which 9 were waited for; matrix products, arithmetic and copies ran while one was open for 3% of the time, Pallas kernels for 18%

commit v1 on v0

--- a/solution.py
+++ b/solution.py
@@ -158,23 +158,40 @@
     return jnp.sum(jnp.where(mark, column, jnp.zeros_like(column)), axis=0, keepdims=True)
 
 
-def stats_kernel(pos, target, places, a0, a1, a2, a3, logits, stats):
+def unpacked(ref, h, blocks):
+    powers = ref[0, h, blocks * CAP :, :].astype(jnp.int32).astype(jnp.float32)
+    return [
+        decoded(ref[0, h, b * CAP : (b + 1) * CAP, :], powers[b : b + 1, :]) for b in range(blocks)
+    ]
+
+
+def early_kernel(a0, a1, a2, total):
+    blocks = total.shape[1]
+    for h in range(2):
+        for b, (x, y, z) in enumerate(zip(*(unpacked(a, h, blocks) for a in (a0, a1, a2)))):
+            total[h, b] = x + y + z
+
+
+def early_sum(parts):
+    blocks = parts[0].shape[2] // CAP
+    return pl.pallas_call(
+        early_kernel,
+        name="early_sum",
+        out_shape=jax.ShapeDtypeStruct((2, blocks, CAP, BLOCK), jnp.float32),
+        compiler_params=params(),
+    )(*parts)
+
+
+def stats_kernel(pos, target, places, early, last, logits, stats):
     blocks = logits.shape[1]
     tokens = pos.shape[-1]
     tops = [jnp.full((1, tokens), NEG, jnp.float32) for _ in range(2)]
-    first = blocks * CAP
-    powers = [
-        [a[0, h, first:, :].astype(jnp.int32).astype(jnp.float32) for a in (a0, a1, a2, a3)]
-        for h in range(2)
-    ]
-    for b in range(blocks):
-        mark = selector(pos[b : b + 1, :])
-        for h in range(2):
-            total = 0.0
-            for a, power in zip((a0, a1, a2, a3), powers[h]):
-                total = total + decoded(a[0, h, b * CAP : (b + 1) * CAP, :], power[b : b + 1, :])
+    for h in range(2):
+        for b, part in enumerate(unpacked(last, h, blocks)):
+            total = early[h, b] + part
             logits[h, b] = total
             peak = jnp.max(total, axis=1, keepdims=True)
+            mark = selector(pos[b : b + 1, :])
             tops[h] = jnp.maximum(
                 tops[h], jnp.max(jnp.where(mark, peak, NEG), axis=0, keepdims=True)
             )
@@ -199,17 +216,16 @@
     stats[...] = jnp.concatenate(lines, axis=0)
 
 
-def row_stats(pos, target, places, parts):
-    blocks = parts[0].shape[2] // CAP
+def row_stats(pos, target, places, early, last):
     return pl.pallas_call(
         stats_kernel,
         name="row_stats",
         out_shape=[
-            jax.ShapeDtypeStruct((2, blocks, CAP, BLOCK), jnp.float32),
+            jax.ShapeDtypeStruct(early.shape, jnp.float32),
             jax.ShapeDtypeStruct((8, pos.shape[-1]), jnp.float32),
         ],
         compiler_params=params(),
-    )(pos, target, places, *parts)
+    )(pos, target, places, early, last)
 
 
 def combined(seen):
@@ -328,13 +344,8 @@
         before = lax.ppermute(pay, "y", shift(1))
         return after, before
 
-    def opposite(after, before):
-        half = after.shape[0] // 2
-        if half == 0:
-            return lax.ppermute(after, "y", shift(-1))
-        low = lax.ppermute(after[:half], "y", shift(-1))
-        high = lax.ppermute(before[half:], "y", shift(1))
-        return jnp.concatenate([low, high], axis=0)
+    def opposite(pay):
+        return lax.ppermute(pay, "y", shift(2))
 
     def everyone(stats):
         copies = jnp.broadcast_to(stats[None], (sx * sz * sc, *stats.shape))
@@ -343,15 +354,15 @@
     def dense(pays, head_t, head_s, allowed, target):
         tokens, blocks = allowed.shape
         width = head_t.shape[1]
-        studs, total = {}, 0.0
-        for step in range(sx):
-            teach, stud = features(pays[step], tokens)
-            studs[step] = stud
-            teach = teach.transpose(1, 0, 2).reshape(tokens, -1)
-            part = jnp.concatenate(
-                [dot(teach, head_t, ((1,), (0,))), dot(stud, head_s, ((0,), (0,)))], axis=1
-            )
-            total = total + to_owner(part, step)
+        pairs = [features(pays[step], tokens) for step in range(sx)]
+        teach = jnp.concatenate([t.transpose(1, 0, 2).reshape(tokens, -1) for t, _ in pairs])
+        studs = jnp.concatenate([stud for _, stud in pairs], axis=1)
+        part = jnp.concatenate(
+            [dot(teach, head_t, ((1,), (0,))), dot(studs, head_s, ((0,), (0,)))], axis=1
+        )
+        total = sum(
+            to_owner(part[step * tokens : (step + 1) * tokens], step) for step in range(sx)
+        )
         lt, ls = total[:, :width], total[:, width:]
         open_ = jnp.broadcast_to((allowed > 0)[:, :, None], (tokens, blocks, BLOCK))
         open_ = open_.reshape(tokens, width)
@@ -367,9 +378,8 @@
         scale_t = (jnp.exp(top_t[None] - all_t) / sum_t)[0]
         scale_s = (jnp.exp(top_s[None] - all_s) / sum_s)[0]
         grad = (es * scale_s[:, None] - et * scale_t[:, None]).astype(jnp.bfloat16)
-        head = sum(
-            dot(studs[step], to_owner(grad, step), ((1,), (0,))) for step in range(sx)
-        )
+        grads = jnp.concatenate([to_owner(grad, step) for step in range(sx)])
+        head = dot(studs, grads, ((1,), (0,)))
         return row_kl[0], logprob[0], head
 
     def other_core(pay):
@@ -387,13 +397,13 @@
         own_pos = jnp.where(open_ > 0, place.astype(jnp.int32), -1)
         own_pos = jnp.pad(own_pos, ((0, -blocks % 8), (0, 0)), constant_values=-1)
         order = (0, 1, 3, 2)
-        from_line = lambda a, far: lax.ppermute(a, "x", [(x, (x - far) % sx) for x in range(sx)])
+
+        def from_line(a, far):
+            return lax.ppermute(a, "x", [(x, (x - far) % sx) for x in range(sx)])
+
         places = [own_pos] + [from_line(own_pos, far) for far in range(1, sx)]
-        pay, places = lax.optimization_barrier((pay, places))
         places = jnp.stack(places)
-        pay = lax.all_to_all(
-            jnp.broadcast_to(pay[None], (sz, *pay.shape)), "z", 0, 0, tiled=True
-        )
+        pay = lax.all_to_all(jnp.broadcast_to(pay[None], (sz, *pay.shape)), "z", 0, 0, tiled=True)
         here, row, core = (lax.axis_index(name).astype(jnp.int32) for name in ("x", "y", "c"))
         meta = jnp.stack([core] + [(row + step - 2 * here) % sx for step in order])
         place_of = (row * sz + lax.axis_index("z")) * sc + core
@@ -406,13 +416,14 @@
         after, ahead = neighbours(pay)
         part, stud0 = run((0,), [pay], [other])
         got = [to_owner(part, order[0])]
-        far = opposite(after, ahead)
+        far = opposite(pay)
         part, other_part, stud1 = run((1, 2), [after, ahead], [other_core(after), other_core(ahead)])
         got += [to_owner(part, order[1]), to_owner(other_part, order[2])]
         part, stud2 = run((3,), [far], [other_core(far)])
         got.append(to_owner(part, order[3]))
 
-        logits, stats = row_stats(own_pos, target[None], places, got)
+        early = early_sum(got[:3])
+        logits, stats = row_stats(own_pos, target[None], places, early, got[3])
         grad, rows = row_grads(own_pos, everyone(stats), logits)
         grads = [grad] + [from_line(grad, far) for far in range(1, sx)]
         head = head_gradient(meta, places, grads, [stud0, stud1, stud2])

time: 181 us -> 198 us (1.094)
  waiting for transfers between devices: 43.3 us -> 56.6 us
  starting transfers between devices: 34.1 us -> 40.2 us
  local copies, waits for them, and re-layouts: 5.83 us -> 2.11 us
  blocking collectives: 49.3 us -> 52.6 us
    ppermute x1, waiting for transfers between devices: 16.2 us -> 31.1 us  [neighbours(): after = lax.ppermute(pay, 'y', shift(-1))]
    ppermute x1, starting transfers between devices: 1.83 us -> 13.4 us  [neighbours(): after = lax.ppermute(pay, 'y', shift(-1))]
    ppermute x8 -> x7, starting transfers between devices: 12.3 us -> 7.17 us  [the longest x6 5.99 us: from_line(): return lax.ppermute(a, 'x', [(x, (x - far) % sx) for x in range(sx)])]
    pallas_call x1, Pallas kernels: 4.99 us -> 1.96 us  [row_stats(): pl.pallas_call(stats_kernel, name='row_stats', out_shape=[jax.ShapeDtypeS...]
    ppermute x4, waiting for transfers between devices: 11.5 us -> 8.95 us  [to_owner(): return lax.ppermute(a, ('x', 'y'), turn(step))]
    all_to_all x1, blocking collectives: 27.6 us -> 30 us  [per_device(): lax.all_to_all(jnp.broadcast_to(pay[None], (sz, *pay.shape)), 'z', 0, 0,...]
    slice x2 -> x0, local copies, waits for them, and re-layouts: 2.18 us -> none  [the longest x1 1.17 us: opposite(): high = lax.ppermute(before[half:], 'y', shift(1))]
    ppermute x8 -> x7, waiting for transfers between devices: 12.3 us -> 12.5 us  [the longest x6 12.5 us: from_line(): return lax.ppermute(a, 'x', [(x, (x - far) % sx) for x in range(sx)])]
  transfers between devices with their start and end apart: 19 -> 18, of which waited for: 9 -> 10; matrix products, arithmetic and copies ran while one was open for 3% -> 1% of each run, Pallas kernels for 18% -> 17%
where the time goes in v1:
time: 198 us
  waiting for transfers between devices  56.6 us (29%)
  blocking collectives  52.6 us (27%)
  Pallas kernels  43.6 us (22%)
  starting transfers between devices  40.2 us (20%)
  local copies, waits for them, and re-layouts  2.11 us (1%)
    pallas_call x3, Pallas kernels, partial_logits(): pl.pallas_call(functools.partial(partial_kernel, steps), name='partial_lo...  32.8 us
    ppermute x1, waiting for transfers between devices, neighbours(): after = lax.ppermute(pay, 'y', shift(-1))  31.1 us
    all_to_all x1, blocking collectives, per_device(): lax.all_to_all(jnp.broadcast_to(pay[None], (sz, *pay.shape)), 'z', 0, 0,...  30 us
    all_to_all x1, blocking collectives, everyone(): lax.all_to_all(copies, LOCAL, split_axis=0, concat_axis=0, tiled=True)  22.6 us
    ppermute x1, starting transfers between devices, neighbours(): after = lax.ppermute(pay, 'y', shift(-1))  13.4 us
    ppermute x6, waiting for transfers between devices, from_line(): return lax.ppermute(a, 'x', [(x, (x - far) % sx) for x in range(sx)])  12.5 us
    ppermute x4, starting transfers between devices, to_owner(): return lax.ppermute(a, ('x', 'y'), turn(step))  11.7 us
    ppermute x4, waiting for transfers between devices, to_owner(): return lax.ppermute(a, ('x', 'y'), turn(step))  8.95 us
  transfers between devices with their start and end apart: 18, of which 10 were waited for; matrix products, arithmetic and copies ran while one was open for 1% of the time, Pallas kernels for 17%

profile of v1, /device:TPU:1, one launch (start us, length us, event | category | flops | bytes accessed | tf_op | source)
XLA Modules:
  0.0 197.6 jit_solution(4809812819095698710)
XLA Ops:
  0.6 0.0 copy-start.7
  0.6 0.8 reshape.122
  1.4 0.8 pad_maximum_fusion.5
  2.3 0.7 collective-permute-start.15
  2.9 0.0 collective-permute-done.15
  2.9 0.1 broadcast_in_dim.66
  3.1 30.0 %all_to_all.15.refs_0_ = bf16[8,368,128]{2,1,0:T(8,128)(2,1)} all-to-all(bf16[8,368,128]{2,1,0:T(8,128)(2,1)S(1)} %broadcast_in_dim.66), channel_id=1, replica_groups=mesh['x'=4,'y'=4,'z'=8,'c'=2] {'z'}, dimensions={0} | all-to-all | bytes 1507328 | tf_op jit(solution)/shard_map/all_to_all | solution.py:406
  33.1 2.3 %collective-permute-start.16 = (bf16[8,368,128]{2,1,0:T(8,128)(2,1)}, bf16[8,368,128]{2,1,0:T(8,128)(2,1)S(1)}, u32[]{:S(2)}, u32[]{:S(2)}) collective-permute-start(bf16[8,368,128]{2,1,0:T(8,128)(2,1)} %all_to_all.15.refs_0_), channel_id=1, source_target_pairs={{0,1},{1,0},{2,3},{3,2},{4,5},{5,4},{6,7},{7,6},{8,9},{9,8},{10,11... | collective-permute-start | bytes 2261000 | tf_op jit(solution)/shard_map/ppermute | solution.py:386
  35.3 2.1 %collective-permute-done.16.refs_1_ = bf16[8,368,128]{2,1,0:T(8,128)(2,1)S(1)} collective-permute-done((bf16[8,368,128]{2,1,0:T(8,128)(2,1)}, bf16[8,368,128]{2,1,0:T(8,128)(2,1)S(1)}, u32[]{:S(2)}, u32[]{:S(2)}) %collective-permute-start.16) | collective-permute-done | bytes 753696 | tf_op jit(solution)/shard_map/ppermute | solution.py:386
  37.4 13.4 %collective-permute-start.18 = (bf16[8,368,128]{2,1,0:T(8,128)(2,1)}, bf16[8,368,128]{2,1,0:T(8,128)(2,1)}, u32[]{:S(2)}, u32[]{:S(2)}) collective-permute-start(bf16[8,368,128]{2,1,0:T(8,128)(2,1)} %all_to_all.15.refs_0_), channel_id=1, source_target_pairs={{0,48},{16,0},{32,16},{48,32},{1,49},{17,1},{33,17},{49,33},{2,50}... | collective-permute-start | bytes 2261000 | tf_op jit(solution)/shard_map/ppermute | solution.py:343
  50.8 0.0 collective-permute-start.19
  50.8 1.2 collective-permute-start.24
  52.0 31.1 %collective-permute-done.18.refs_0_ = bf16[8,368,128]{2,1,0:T(8,128)(2,1)} collective-permute-done((bf16[8,368,128]{2,1,0:T(8,128)(2,1)}, bf16[8,368,128]{2,1,0:T(8,128)(2,1)}, u32[]{:S(2)}, u32[]{:S(2)}) %collective-permute-start.18) | collective-permute-done | bytes 753696 | tf_op jit(solution)/shard_map/ppermute | solution.py:343
  83.1 1.2 collective-permute-start.20
  84.4 1.9 collective-permute-done.19.refs_1_
  86.3 1.5 collective-permute-start.21
  87.8 0.0 copy-done.7
  87.8 0.1 fusion.35
  87.9 0.8 collective-permute-start.12
  88.8 1.4 collective-permute-start.13
  90.2 0.4 collective-permute-done.12
  90.6 0.4 collective-permute-start.14
  91.0 0.1 stack.100.meta
  91.1 1.8 collective-permute-done.13
  92.9 1.5 collective-permute-done.14
  94.4 0.0 copy-start.13
  94.4 10.3 %partial_logits.3 = (s16[1,2,816,128]{3,2,1,0:T(8,128)(2,1)}, bf16[1,896,256]{2,1,0:T(8,128)(2,1)S(1)}) custom-call(s32[5]{0:T(128)S(1)} %stack.100.meta, s32[4,16,256]{2,1,0:T(8,128)S(1)} %pad_add_fusion.pos.places, bf16[8,368,128]{2,1,0:T(8,128)(2,1)} %all_to_all.15.refs_0_, bf16[8,368,128]{2,1,0:T(8,128)(2,1)S(1)} %collective-permute-done.16.refs_1_, ...), custom_call_target="tpu_custom_call" | custom-call | flops 4823449600 | bytes 9043968 | tf_op jit(solution)/shard_map/partial_logits/pallas_call | solution.py:121
  104.7 0.0 slice-start
  104.7 0.0 slice-start.1
  104.7 2.2 %collective-permute-start.17 = (s16[1,2,816,128]{3,2,1,0:T(8,128)(2,1)}, s16[1,2,816,128]{3,2,1,0:T(8,128)(2,1)S(1)}, u32[]{:S(2)}, u32[]{:S(2)}) collective-permute-start(s16[1,2,816,128]{3,2,1,0:T(8,128)(2,1)} %get-tuple-element.78), channel_id=1, source_target_pairs={{0,0},{16,80},{32,160},{48,240},{64,192},{80,16},{96,96},{112,176}... | collective-permute-start | bytes 1253384 | tf_op jit(solution)/shard_map/ppermute | solution.py:324
  106.9 0.0 collective-permute-done.24.refs_0_
  106.9 2.3 %collective-permute-start.25 = (bf16[8,368,128]{2,1,0:T(8,128)(2,1)}, bf16[8,368,128]{2,1,0:T(8,128)(2,1)S(1)}, u32[]{:S(2)}, u32[]{:S(2)}) collective-permute-start(bf16[8,368,128]{2,1,0:T(8,128)(2,1)} %collective-permute-done.24.refs_0_), channel_id=1, source_target_pairs={{0,1},{1,0},{2,3},{3,2},{4,5},{5,4},{6,7},{7,6},{8,9},{9,8},{10,11... | collective-permute-start | bytes 2261000 | tf_op jit(solution)/shard_map/ppermute | solution.py:386
  109.2 0.0 collective-permute-done.20.refs_2_
  109.2 0.0 collective-permute-done.21.refs_3_
  109.2 0.0 copy-done.13
  109.2 14.0 %partial_logits.4 = (s16[1,2,816,128]{3,2,1,0:T(8,128)(2,1)}, s16[1,2,816,128]{3,2,1,0:T(8,128)(2,1)}, bf16[2,896,256]{2,1,0:T(8,128)(2,1)S(1)}) custom-call(s32[5]{0:T(128)S(1)} %stack.100.meta, s32[4,16,256]{2,1,0:T(8,128)S(1)} %pad_add_fusion.pos.places, bf16[8,368,128]{2,1,0:T(8,128)(2,1)} %collective-permute-done.18.refs_0_, ...), custom_call_target="tpu_custom_call" | custom-call | flops 9646899200 | bytes 10551296 | tf_op jit(solution)/shard_map/partial_logits/pallas_call | solution.py:121
  123.2 3.6 %collective-permute-start.22 = (s16[1,2,816,128]{3,2,1,0:T(8,128)(2,1)}, s16[1,2,816,128]{3,2,1,0:T(8,128)(2,1)S(1)}, u32[]{:S(2)}, u32[]{:S(2)}) collective-permute-start(s16[1,2,816,128]{3,2,1,0:T(8,128)(2,1)} %get-tuple-element.79), channel_id=1, source_target_pairs={{0,64},{16,144},{32,224},{48,48},{64,0},{80,80},{96,160},{112,240}... | collective-permute-start | bytes 1253384 | tf_op jit(solution)/shard_map/ppermute | solution.py:324
  126.8 0.0 copy-start.12
  126.8 2.1 %collective-permute-start.23 = (s16[1,2,816,128]{3,2,1,0:T(8,128)(2,1)}, s16[1,2,816,128]{3,2,1,0:T(8,128)(2,1)}, u32[]{:S(2)}, u32[]{:S(2)}) collective-permute-start(s16[1,2,816,128]{3,2,1,0:T(8,128)(2,1)} %get-tuple-element.80), channel_id=1, source_target_pairs={{0,192},{16,16},{32,96},{48,176},{64,128},{80,208},{96,32},{112,11... | collective-permute-start | bytes 1253384 | tf_op jit(solution)/shard_map/ppermute | solution.py:324
  129.0 0.0 collective-permute-done.25.refs_1_
  129.0 0.0 slice-done
  129.0 0.0 slice-done.1
  129.0 8.5 %partial_logits.5 = (s16[1,2,816,128]{3,2,1,0:T(8,128)(2,1)}, bf16[1,896,256]{2,1,0:T(8,128)(2,1)S(1)}) custom-call(s32[5]{0:T(128)S(1)} %stack.100.meta, s32[4,16,256]{2,1,0:T(8,128)S(1)} %pad_add_fusion.pos.places, bf16[8,368,128]{2,1,0:T(8,128)(2,1)} %collective-permute-done.24.refs_0_, bf16[8,368,128]{2,1,0:T(8,128)(2,1)S(1)} %collective-permute-done.25.refs_1_, ...), custom_call_target="tpu_custom_call" | custom-call | flops 4823449600 | bytes 9043968 | tf_op jit(solution)/shard_map/partial_logits/pallas_call | solution.py:121
  137.5 3.8 %collective-permute-start.26 = (s16[1,2,816,128]{3,2,1,0:T(8,128)(2,1)}, s16[1,2,816,128]{3,2,1,0:T(8,128)(2,1)S(1)}, u32[]{:S(2)}, u32[]{:S(2)}) collective-permute-start(s16[1,2,816,128]{3,2,1,0:T(8,128)(2,1)} %get-tuple-element.81), channel_id=1, source_target_pairs={{0,128},{16,208},{32,32},{48,112},{64,64},{80,144},{96,224},{112,4... | collective-permute-start | bytes 1253384 | tf_op jit(solution)/shard_map/ppermute | solution.py:324
  141.3 0.0 copy-done.12
  141.3 0.0 collective-permute-done.17.a0
  141.3 0.0 collective-permute-done.22.a1
  141.3 0.0 collective-permute-done.23.a2
  141.3 1.7 early_sum.1.early
  143.1 8.9 %collective-permute-done.26.last = s16[1,2,816,128]{3,2,1,0:T(8,128)(2,1)S(1)} collective-permute-done((s16[1,2,816,128]{3,2,1,0:T(8,128)(2,1)}, s16[1,2,816,128]{3,2,1,0:T(8,128)(2,1)S(1)}, u32[]{:S(2)}, u32[]{:S(2)}) %collective-permute-start.26) | collective-permute-done | bytes 417824 | tf_op jit(solution)/shard_map/ppermute | solution.py:324
  152.0 2.0 row_stats.1
  154.0 22.6 %all_to_all.16.seen = f32[64,8,256]{2,1,0:T(8,128)S(1)} all-to-all(f32[64,8,256]{2,1,0:T(8,128)S(1)} %broadcast_in_dim.67), channel_id=1, replica_groups=mesh['x'=4,'y'=4,'z'=8,'c'=2] {'y','z','c'}, dimensions={0} | all-to-all | bytes 1048576 | tf_op jit(solution)/shard_map/all_to_all | solution.py:352
  176.6 0.8 row_grads.1
  177.4 1.0 collective-permute-start.27
  178.4 2.4 %collective-permute-start.28 = (bf16[10,80,128]{2,1,0:T(8,128)(2,1)S(1)}, bf16[10,80,128]{2,1,0:T(8,128)(2,1)S(1)}, u32[]{:S(2)}, u32[]{:S(2)}) collective-permute-start(bf16[10,80,128]{2,1,0:T(8,128)(2,1)S(1)} %get-tuple-element.85.refs_0_), channel_id=1, source_target_pairs={{0,128},{64,192},{128,0},{192,64},{1,129},{65,193},{129,1},{193,65... | collective-permute-start | bytes 614408 | tf_op jit(solution)/shard_map/ppermute | solution.py:402
  180.8 0.0 collective-permute-start.29
  180.8 0.5 slice.71
  181.9 0.6 fusion.45
  182.5 1.4 collective-permute-done.27.refs_1_
  183.9 2.1 %collective-permute-done.28.refs_2_ = bf16[10,80,128]{2,1,0:T(8,128)(2,1)S(1)} collective-permute-done((bf16[10,80,128]{2,1,0:T(8,128)(2,1)S(1)}, bf16[10,80,128]{2,1,0:T(8,128)(2,1)S(1)}, u32[]{:S(2)}, u32[]{:S(2)}) %collective-permute-start.28) | collective-permute-done | bytes 204832 | tf_op jit(solution)/shard_map/ppermute | solution.py:402
  186.0 5.2 %collective-permute-done.29.refs_3_ = bf16[10,80,128]{2,1,0:T(8,128)(2,1)S(1)} collective-permute-done((bf16[10,80,128]{2,1,0:T(8,128)(2,1)S(1)}, bf16[10,80,128]{2,1,0:T(8,128)(2,1)S(1)}, u32[]{:S(2)}, u32[]{:S(2)}) %collective-permute-start.29) | collective-permute-done | bytes 204832 | tf_op jit(solution)/shard_map/ppermute | solution.py:402
  191.3 0.0 copy-start.8
  191.3 6.3 %head_gradient.1 = f32[896,1280]{1,0:T(8,128)} custom-call(s32[5]{0:T(128)S(1)} %stack.100.meta, s32[4,16,256]{2,1,0:T(8,128)S(1)} %pad_add_fusion.pos.places, bf16[10,80,128]{2,1,0:T(8,128)(2,1)S(1)} %get-tuple-element.85.refs_0_, bf16[10,80,128]{2,1,0:T(8,128)(2,1)S(1)} %collective-permute-done.27.refs_1_, ...), custom_call_target="tpu_custom_call" | custom-call | tf_op jit(solution)/shard_map/head_gradient/pallas_call | solution.py:299
  197.6 0.0 copy-done.8
  (7 shorter events, 0.1 us)
Async XLA Ops:
  0.6 87.1 %copy-start.7 = (s32[256,10]{0,1:T(8,128)S(1)}, s32[256,10]{0,1:T(8,128)}, u32[]{:S(2)}) copy-start(s32[256,10]{0,1:T(8,128)} %param.12) | copy-start | bytes 30724
  2.3 0.7 collective-permute-start.15
  33.1 4.3 %collective-permute-start.16 = (bf16[8,368,128]{2,1,0:T(8,128)(2,1)}, bf16[8,368,128]{2,1,0:T(8,128)(2,1)S(1)}, u32[]{:S(2)}, u32[]{:S(2)}) collective-permute-start(bf16[8,368,128]{2,1,0:T(8,128)(2,1)} %all_to_all.15.refs_0_), channel_id=1, source_target_pairs={{0,1},{1,0},{2,3},{3,2},{4,5},{5,4},{6,7},{7,6},{8,9},{9,8},{10,11... | collective-permute-start | bytes 2261000 | tf_op jit(solution)/shard_map/ppermute | solution.py:386
  37.4 45.7 %collective-permute-start.18 = (bf16[8,368,128]{2,1,0:T(8,128)(2,1)}, bf16[8,368,128]{2,1,0:T(8,128)(2,1)}, u32[]{:S(2)}, u32[]{:S(2)}) collective-permute-start(bf16[8,368,128]{2,1,0:T(8,128)(2,1)} %all_to_all.15.refs_0_), channel_id=1, source_target_pairs={{0,48},{16,0},{32,16},{48,32},{1,49},{17,1},{33,17},{49,33},{2,50}... | collective-permute-start | bytes 2261000 | tf_op jit(solution)/shard_map/ppermute | solution.py:343
  50.8 35.4 %collective-permute-start.19 = (bf16[8,368,128]{2,1,0:T(8,128)(2,1)}, bf16[8,368,128]{2,1,0:T(8,128)(2,1)}, u32[]{:S(2)}, u32[]{:S(2)}) collective-permute-start(bf16[8,368,128]{2,1,0:T(8,128)(2,1)} %all_to_all.15.refs_0_), channel_id=1, source_target_pairs={{0,16},{16,32},{32,48},{48,0},{1,17},{17,33},{33,49},{49,1},{2,18}... | collective-permute-start | bytes 2261000 | tf_op jit(solution)/shard_map/ppermute | solution.py:344
  50.8 56.1 %collective-permute-start.24 = (bf16[8,368,128]{2,1,0:T(8,128)(2,1)}, bf16[8,368,128]{2,1,0:T(8,128)(2,1)}, u32[]{:S(2)}, u32[]{:S(2)}) collective-permute-start(bf16[8,368,128]{2,1,0:T(8,128)(2,1)} %all_to_all.15.refs_0_), channel_id=1, source_target_pairs={{0,32},{16,48},{32,0},{48,16},{1,33},{17,49},{33,1},{49,17},{2,34}... | collective-permute-start | bytes 2261000 | tf_op jit(solution)/shard_map/ppermute | solution.py:348
  83.1 26.1 %collective-permute-start.20 = (bf16[8,368,128]{2,1,0:T(8,128)(2,1)}, bf16[8,368,128]{2,1,0:T(8,128)(2,1)S(1)}, u32[]{:S(2)}, u32[]{:S(2)}) collective-permute-start(bf16[8,368,128]{2,1,0:T(8,128)(2,1)} %collective-permute-done.18.refs_0_), channel_id=1, source_target_pairs={{0,1},{1,0},{2,3},{3,2},{4,5},{5,4},{6,7},{7,6},{8,9},{9,8},{10,11... | collective-permute-start | bytes 2261000 | tf_op jit(solution)/shard_map/ppermute | solution.py:386
  86.3 22.9 %collective-permute-start.21 = (bf16[8,368,128]{2,1,0:T(8,128)(2,1)}, bf16[8,368,128]{2,1,0:T(8,128)(2,1)}, u32[]{:S(2)}, u32[]{:S(2)}) collective-permute-start(bf16[8,368,128]{2,1,0:T(8,128)(2,1)} %collective-permute-done.19.refs_1_), channel_id=1, source_target_pairs={{0,1},{1,0},{2,3},{3,2},{4,5},{5,4},{6,7},{7,6},{8,9},{9,8},{10,11... | collective-permute-start | bytes 2261000 | tf_op jit(solution)/shard_map/ppermute | solution.py:386
  87.9 2.7 %collective-permute-start.12 = (s32[16,256]{1,0:T(8,128)S(1)}, s32[16,256]{1,0:T(8,128)S(1)}, u32[]{:S(2)}, u32[]{:S(2)}) collective-permute-start(s32[16,256]{1,0:T(8,128)S(1)} %get-tuple-element.165.pos), channel_id=1, source_target_pairs={{0,192},{64,0},{128,64},{192,128},{1,193},{65,1},{129,65},{193,129... | collective-permute-start | bytes 49160 | tf_op jit(solution)/shard_map/ppermute | solution.py:402
  88.8 4.1 %collective-permute-start.13 = (s32[16,256]{1,0:T(8,128)S(1)}, s32[16,256]{1,0:T(8,128)S(1)}, u32[]{:S(2)}, u32[]{:S(2)}) collective-permute-start(s32[16,256]{1,0:T(8,128)S(1)} %get-tuple-element.165.pos), channel_id=1, source_target_pairs={{0,128},{64,192},{128,0},{192,64},{1,129},{65,193},{129,1},{193,65... | collective-permute-start | bytes 49160 | tf_op jit(solution)/shard_map/ppermute | solution.py:402
  90.6 3.8 %collective-permute-start.14 = (s32[16,256]{1,0:T(8,128)S(1)}, s32[16,256]{1,0:T(8,128)S(1)}, u32[]{:S(2)}, u32[]{:S(2)}) collective-permute-start(s32[16,256]{1,0:T(8,128)S(1)} %get-tuple-element.165.pos), channel_id=1, source_target_pairs={{0,64},{64,128},{128,192},{192,0},{1,65},{65,129},{129,193},{193,1... | collective-permute-start | bytes 49160 | tf_op jit(solution)/shard_map/ppermute | solution.py:402
  94.4 14.8 %copy-start.13 = (bf16[896,1280]{1,0:T(8,128)(2,1)S(1)}, bf16[896,1280]{1,0:T(8,128)(2,1)}, u32[]{:S(2)}) copy-start(bf16[896,1280]{1,0:T(8,128)(2,1)} %refs_3_.3) | copy-start | bytes 6881284
  104.7 24.3 %slice-start = ((s8[5242880]{0:T(1024)(128)(4,1)}), s8[4194304]{0:T(1024)(128)(4,1)S(1)}, s32[]{:S(2)}) async-start(s8[5242880]{0:T(1024)(128)(4,1)} %bitcast.158), calls=%async_computation.3 | async-start | bytes 8388608
  104.7 24.3 %slice-start.1 = ((s8[5242880]{0:T(1024)(128)(4,1)}), s8[1048576]{0:T(1024)(128)(4,1)S(1)}, s32[]{:S(2)}) async-start(s8[5242880]{0:T(1024)(128)(4,1)} %bitcast.158), calls=%async_computation.4 | async-start | bytes 2097152
  104.7 36.6 %collective-permute-start.17 = (s16[1,2,816,128]{3,2,1,0:T(8,128)(2,1)}, s16[1,2,816,128]{3,2,1,0:T(8,128)(2,1)S(1)}, u32[]{:S(2)}, u32[]{:S(2)}) collective-permute-start(s16[1,2,816,128]{3,2,1,0:T(8,128)(2,1)} %get-tuple-element.78), channel_id=1, source_target_pairs={{0,0},{16,80},{32,160},{48,240},{64,192},{80,16},{96,96},{112,176}... | collective-permute-start | bytes 1253384 | tf_op jit(solution)/shard_map/ppermute | solution.py:324
  106.9 22.1 %collective-permute-start.25 = (bf16[8,368,128]{2,1,0:T(8,128)(2,1)}, bf16[8,368,128]{2,1,0:T(8,128)(2,1)S(1)}, u32[]{:S(2)}, u32[]{:S(2)}) collective-permute-start(bf16[8,368,128]{2,1,0:T(8,128)(2,1)} %collective-permute-done.24.refs_0_), channel_id=1, source_target_pairs={{0,1},{1,0},{2,3},{3,2},{4,5},{5,4},{6,7},{7,6},{8,9},{9,8},{10,11... | collective-permute-start | bytes 2261000 | tf_op jit(solution)/shard_map/ppermute | solution.py:386
  123.2 18.2 %collective-permute-start.22 = (s16[1,2,816,128]{3,2,1,0:T(8,128)(2,1)}, s16[1,2,816,128]{3,2,1,0:T(8,128)(2,1)S(1)}, u32[]{:S(2)}, u32[]{:S(2)}) collective-permute-start(s16[1,2,816,128]{3,2,1,0:T(8,128)(2,1)} %get-tuple-element.79), channel_id=1, source_target_pairs={{0,64},{16,144},{32,224},{48,48},{64,0},{80,80},{96,160},{112,240}... | collective-permute-start | bytes 1253384 | tf_op jit(solution)/shard_map/ppermute | solution.py:324
  126.8 14.5 %copy-start.12 = (s32[256]{0:T(256)S(1)}, s32[256]{0:T(256)}, u32[]{:S(2)}) copy-start(s32[256]{0:T(256)} %param.13) | copy-start | bytes 3076
  126.8 14.5 %collective-permute-start.23 = (s16[1,2,816,128]{3,2,1,0:T(8,128)(2,1)}, s16[1,2,816,128]{3,2,1,0:T(8,128)(2,1)}, u32[]{:S(2)}, u32[]{:S(2)}) collective-permute-start(s16[1,2,816,128]{3,2,1,0:T(8,128)(2,1)} %get-tuple-element.80), channel_id=1, source_target_pairs={{0,192},{16,16},{32,96},{48,176},{64,128},{80,208},{96,32},{112,11... | collective-permute-start | bytes 1253384 | tf_op jit(solution)/shard_map/ppermute | solution.py:324
  137.5 14.5 %collective-permute-start.26 = (s16[1,2,816,128]{3,2,1,0:T(8,128)(2,1)}, s16[1,2,816,128]{3,2,1,0:T(8,128)(2,1)S(1)}, u32[]{:S(2)}, u32[]{:S(2)}) collective-permute-start(s16[1,2,816,128]{3,2,1,0:T(8,128)(2,1)} %get-tuple-element.81), channel_id=1, source_target_pairs={{0,128},{16,208},{32,32},{48,112},{64,64},{80,144},{96,224},{112,4... | collective-permute-start | bytes 1253384 | tf_op jit(solution)/shard_map/ppermute | solution.py:324
  177.4 6.5 %collective-permute-start.27 = (bf16[10,80,128]{2,1,0:T(8,128)(2,1)S(1)}, bf16[10,80,128]{2,1,0:T(8,128)(2,1)S(1)}, u32[]{:S(2)}, u32[]{:S(2)}) collective-permute-start(bf16[10,80,128]{2,1,0:T(8,128)(2,1)S(1)} %get-tuple-element.85.refs_0_), channel_id=1, source_target_pairs={{0,192},{64,0},{128,64},{192,128},{1,193},{65,1},{129,65},{193,129... | collective-permute-start | bytes 614408 | tf_op jit(solution)/shard_map/ppermute | solution.py:402
  178.4 7.6 %collective-permute-start.28 = (bf16[10,80,128]{2,1,0:T(8,128)(2,1)S(1)}, bf16[10,80,128]{2,1,0:T(8,128)(2,1)S(1)}, u32[]{:S(2)}, u32[]{:S(2)}) collective-permute-start(bf16[10,80,128]{2,1,0:T(8,128)(2,1)S(1)} %get-tuple-element.85.refs_0_), channel_id=1, source_target_pairs={{0,128},{64,192},{128,0},{192,64},{1,129},{65,193},{129,1},{193,65... | collective-permute-start | bytes 614408 | tf_op jit(solution)/shard_map/ppermute | solution.py:402
  180.8 10.5 %collective-permute-start.29 = (bf16[10,80,128]{2,1,0:T(8,128)(2,1)S(1)}, bf16[10,80,128]{2,1,0:T(8,128)(2,1)S(1)}, u32[]{:S(2)}, u32[]{:S(2)}) collective-permute-start(bf16[10,80,128]{2,1,0:T(8,128)(2,1)S(1)} %get-tuple-element.85.refs_0_), channel_id=1, source_target_pairs={{0,64},{64,128},{128,192},{192,0},{1,65},{65,129},{129,193},{193,1... | collective-permute-start | bytes 614408 | tf_op jit(solution)/shard_map/ppermute | solution.py:402
  191.3 6.3 %copy-start.8 = (s32[256,10]{0,1:T(8,128)S(1)}, s32[256,10]{0,1:T(8,128)}, u32[]{:S(2)}) copy-start(s32[256,10]{0,1:T(8,128)} %param.12) | copy-start | bytes 30724

commit v2 on v1

--- a/solution.py
+++ b/solution.py
@@ -19,7 +19,7 @@
 
 
 def params(**kw):
-    return pltpu.CompilerParams(vmem_limit_bytes=48 << 20, **kw)
+    return pltpu.CompilerParams(vmem_limit_bytes=36 << 20, **kw)
 
 
 def selector(pos_row):
@@ -48,66 +48,68 @@
 def partial_kernel(steps, meta, pos, *refs):
     count = len(steps)
     mine, others = refs[:count], refs[count : 2 * count]
-    head_t, head_s = refs[2 * count : 2 * count + 2]
+    far_t, far_s = refs[2 * count : 2 * count + 2]
     outs = refs[2 * count + 2 : 3 * count + 2]
-    kept, sel, rows_t, rows_s, powers = refs[3 * count + 2 :]
+    kept, sel, rows_t, rows_s, powers, head_t, head_s, sems = refs[3 * count + 2 :]
+    fetch_t = pltpu.make_async_copy(far_t, head_t, sems.at[0])
+    fetch_s = pltpu.make_async_copy(far_s, head_s, sems.at[1])
+    fetch_t.start()
+    fetch_s.start()
     blocks = sel.shape[0] // CAP
     depth, tokens = mine[0].shape[0], sel.shape[1]
     both = kept.shape[1] // depth
-    b = pl.program_id(0)
-
-    @pl.when(b == 0)
-    def _():
-        first = meta[0] == 0
-        powers[...] = jnp.zeros_like(powers)
-        for i in range(count):
-            held = meta[1 + steps[i]]
-            for k in range(blocks):
-                mark = selector(pos[held, k : k + 1, :]).astype(jnp.float32)
-                sel[k * CAP : (k + 1) * CAP, :] = mark.astype(jnp.bfloat16)
-
-            def chunk(z, _, i=i):
-                a, o = mine[i][z, :tokens, :], others[i][z, :tokens, :]
-                pair = jnp.concatenate([jnp.where(first, a, o), jnp.where(first, o, a)], axis=1)
-                rows_t[i, :, pl.ds(pl.multiple_of(z * 256, 256), 256)] = dot(
-                    sel[...], pair, ((1,), (0,))
-                ).astype(jnp.bfloat16)
-                a = mine[i][z, tokens:, :].astype(jnp.float32)
-                o = others[i][z, tokens:, :].astype(jnp.float32)
-                parts = []
-                for part in (jnp.where(first, a, o), jnp.where(first, o, a)):
-                    parts.append(jnp.concatenate([part[: both // 2], part[both // 2 :]], axis=1))
-                kept[i, pl.ds(pl.multiple_of(z * both, 16), both), :] = jnp.concatenate(
-                    parts, axis=0
-                ).astype(jnp.bfloat16)
-                return 0
-
-            lax.fori_loop(0, depth, chunk, 0)
-            deep_s = kept.shape[1]
-            for at in range(0, deep_s, 256):
-                end = min(at + 256, deep_s)
-                rows_s[i, :, at:end] = dot(sel[...], kept[i, at:end, :], ((1,), (1,))).astype(
-                    jnp.bfloat16
-                )
-
-    here = pl.ds(pl.multiple_of(b * 2 * CAP, 16), 2 * CAP)
-    for h, (rows, head) in enumerate(((rows_t, head_t), (rows_s, head_s))):
-        lines = rows[:, here, :].reshape(count * 2 * CAP, rows.shape[-1])
-        product = dot(lines, head[...], ((1,), (0,)))
-        for i in range(count):
-            for k in range(2):
-                at = (2 * i + k) * CAP
-                values, power = coded(product[at : at + CAP, k * BLOCK : (k + 1) * BLOCK])
-                outs[i][0, h, pl.ds(pl.multiple_of((2 * b + k) * CAP, 16), CAP), :] = values
-                powers[2 * i + h, pl.ds(2 * b + k, 1), :] = power
-
-    @pl.when(b == pl.num_programs(0) - 1)
-    def _():
-        for i in range(count):
-            for h in range(2):
-                outs[i][0, h, blocks * CAP :, :] = (
-                    powers[2 * i + h].astype(jnp.int32).astype(jnp.int16)
-                )
+    first = meta[0] == 0
+    powers[...] = jnp.zeros_like(powers)
+    for i in range(count):
+        held = meta[1 + steps[i]]
+        for k in range(blocks):
+            mark = selector(pos[held, k : k + 1, :]).astype(jnp.float32)
+            sel[k * CAP : (k + 1) * CAP, :] = mark.astype(jnp.bfloat16)
+
+        def chunk(z, _, i=i):
+            a, o = mine[i][z, :tokens, :], others[i][z, :tokens, :]
+            pair = jnp.concatenate([jnp.where(first, a, o), jnp.where(first, o, a)], axis=1)
+            rows_t[i, :, pl.ds(pl.multiple_of(z * 256, 256), 256)] = dot(
+                sel[...], pair, ((1,), (0,))
+            ).astype(jnp.bfloat16)
+            a = mine[i][z, tokens:, :].astype(jnp.float32)
+            o = others[i][z, tokens:, :].astype(jnp.float32)
+            parts = []
+            for part in (jnp.where(first, a, o), jnp.where(first, o, a)):
+                parts.append(jnp.concatenate([part[: both // 2], part[both // 2 :]], axis=1))
+            kept[i, pl.ds(pl.multiple_of(z * both, 16), both), :] = jnp.concatenate(
+                parts, axis=0
+            ).astype(jnp.bfloat16)
+            return 0
+
+        lax.fori_loop(0, depth, chunk, 0)
+        deep_s = kept.shape[1]
+        for at in range(0, deep_s, 256):
+            end = min(at + 256, deep_s)
+            rows_s[i, :, at:end] = dot(sel[...], kept[i, at:end, :], ((1,), (1,))).astype(
+                jnp.bfloat16
+            )
+
+    def two_blocks(b, _):
+        here = pl.ds(pl.multiple_of(b * 2 * CAP, 16), 2 * CAP)
+        columns = pl.ds(pl.multiple_of(b * 2 * BLOCK, 2 * BLOCK), 2 * BLOCK)
+        for h, (rows, head) in enumerate(((rows_t, head_t), (rows_s, head_s))):
+            lines = rows[:, here, :].reshape(count * 2 * CAP, rows.shape[-1])
+            product = dot(lines, head[:, columns], ((1,), (0,)))
+            for i in range(count):
+                for k in range(2):
+                    at = (2 * i + k) * CAP
+                    values, power = coded(product[at : at + CAP, k * BLOCK : (k + 1) * BLOCK])
+                    outs[i][0, h, pl.ds(pl.multiple_of((2 * b + k) * CAP, 16), CAP), :] = values
+                    powers[2 * i + h, pl.ds(2 * b + k, 1), :] = power
+        return 0
+
+    fetch_t.wait()
+    fetch_s.wait()
+    lax.fori_loop(0, blocks // 2, two_blocks, 0)
+    for i in range(count):
+        for h in range(2):
+            outs[i][0, h, blocks * CAP :, :] = powers[2 * i + h].astype(jnp.int32).astype(jnp.int16)
 
 
 def partial_logits(meta, pos, steps, mine, others, head_t, head_s):
@@ -117,28 +119,21 @@
     deep_s = head_s.shape[0]
     blocks = width // BLOCK
     coded_rows = blocks * CAP + 16
-    whole = lambda a: pl.BlockSpec(a.shape, lambda b, meta: (0,) * a.ndim)
     return pl.pallas_call(
         functools.partial(partial_kernel, steps),
         name="partial_logits",
-        grid_spec=pltpu.PrefetchScalarGridSpec(
-            num_scalar_prefetch=1,
-            grid=(blocks // 2,),
-            in_specs=[whole(pos)]
-            + [whole(a) for a in (*mine, *others)]
-            + [
-                pl.BlockSpec((deep_t, 2 * BLOCK), lambda b, meta: (0, b)),
-                pl.BlockSpec((deep_s, 2 * BLOCK), lambda b, meta: (0, b)),
-            ],
-            out_specs=[pl.BlockSpec((1, 2, coded_rows, BLOCK), lambda b, meta: (0, 0, 0, 0))] * count
-            + [pl.BlockSpec((count, deep_s, tokens), lambda b, meta: (0, 0, 0))],
-            scratch_shapes=[
-                pltpu.VMEM((blocks * CAP, tokens), jnp.bfloat16),
-                pltpu.VMEM((count, blocks * CAP, deep_t), jnp.bfloat16),
-                pltpu.VMEM((count, blocks * CAP, deep_s), jnp.bfloat16),
-                pltpu.VMEM((2 * count, 16, BLOCK), jnp.float32),
-            ],
-        ),
+        in_specs=[pl.BlockSpec(memory_space=pltpu.SMEM)]
+        + [pl.BlockSpec(memory_space=pltpu.VMEM)] * (2 * count + 1)
+        + [pl.BlockSpec(memory_space=pl.ANY)] * 2,
+        scratch_shapes=[
+            pltpu.VMEM((blocks * CAP, tokens), jnp.bfloat16),
+            pltpu.VMEM((count, blocks * CAP, deep_t), jnp.bfloat16),
+            pltpu.VMEM((count, blocks * CAP, deep_s), jnp.bfloat16),
+            pltpu.VMEM((2 * count, 16, BLOCK), jnp.float32),
+            pltpu.VMEM(head_t.shape, head_t.dtype),
+            pltpu.VMEM(head_s.shape, head_s.dtype),
+            pltpu.SemaphoreType.DMA((2,)),
+        ],
         out_shape=[jax.ShapeDtypeStruct((1, 2, coded_rows, BLOCK), jnp.int16)] * count
         + [jax.ShapeDtypeStruct((count, deep_s, tokens), jnp.bfloat16)],
         compiler_params=params(),

time: 198 us -> 195 us (0.985)
  Pallas kernels: 43.6 us -> 39.9 us
    pallas_call x3, Pallas kernels: 32.8 us -> 29 us  [partial_logits(): pl.pallas_call(functools.partial(partial_kernel, steps), name='partial_lo...]
  transfers between devices with their start and end apart: 18 -> 18, of which waited for: 10 -> 10; matrix products, arithmetic and copies ran while one was open for 1% -> 1% of each run, Pallas kernels for 17% -> 16%
where the time goes in v2:
time: 195 us; the launch traced here: 194 us
  waiting for transfers between devices  56.5 us (29%)
  blocking collectives  52.6 us (27%)
  starting transfers between devices  40.3 us (21%)
  Pallas kernels  39.9 us (20%)
  local copies, waits for them, and re-layouts  2.12 us (1%)
    ppermute x1, waiting for transfers between devices, neighbours(): after = lax.ppermute(pay, 'y', shift(-1))  31.1 us
    all_to_all x1, blocking collectives, per_device(): lax.all_to_all(jnp.broadcast_to(pay[None], (sz, *pay.shape)), 'z', 0, 0,...  30 us
    pallas_call x3, Pallas kernels, partial_logits(): pl.pallas_call(functools.partial(partial_kernel, steps), name='partial_lo...  29 us
    all_to_all x1, blocking collectives, everyone(): lax.all_to_all(copies, LOCAL, split_axis=0, concat_axis=0, tiled=True)  22.6 us
    ppermute x1, starting transfers between devices, neighbours(): after = lax.ppermute(pay, 'y', shift(-1))  13.4 us
    ppermute x6, waiting for transfers between devices, from_line(): return lax.ppermute(a, 'x', [(x, (x - far) % sx) for x in range(sx)])  12.5 us
    ppermute x4, starting transfers between devices, to_owner(): return lax.ppermute(a, ('x', 'y'), turn(step))  11.7 us
    ppermute x4, waiting for transfers between devices, to_owner(): return lax.ppermute(a, ('x', 'y'), turn(step))  8.94 us
  transfers between devices with their start and end apart: 18, of which 10 were waited for; matrix products, arithmetic and copies ran while one was open for 1% of the time, Pallas kernels for 16%

profile of v2, /device:TPU:1, one launch (start us, length us, event | category | flops | bytes accessed | tf_op | source)
XLA Modules:
  0.0 193.9 jit_solution(12587742473559337709)
XLA Ops:
  0.6 0.0 copy-start.7
  0.6 0.8 reshape.122
  1.4 0.8 pad_maximum_fusion.5
  2.3 0.7 collective-permute-start.15
  2.9 0.0 collective-permute-done.15
  2.9 0.1 broadcast_in_dim.66
  3.1 30.0 %all_to_all.15.refs_0_ = bf16[8,368,128]{2,1,0:T(8,128)(2,1)} all-to-all(bf16[8,368,128]{2,1,0:T(8,128)(2,1)S(1)} %broadcast_in_dim.66), channel_id=1, replica_groups=mesh['x'=4,'y'=4,'z'=8,'c'=2] {'z'}, dimensions={0} | all-to-all | bytes 1507328 | tf_op jit(solution)/shard_map/all_to_all | solution.py:401
  33.1 2.3 %collective-permute-start.16 = (bf16[8,368,128]{2,1,0:T(8,128)(2,1)}, bf16[8,368,128]{2,1,0:T(8,128)(2,1)S(1)}, u32[]{:S(2)}, u32[]{:S(2)}) collective-permute-start(bf16[8,368,128]{2,1,0:T(8,128)(2,1)} %all_to_all.15.refs_0_), channel_id=1, source_target_pairs={{0,1},{1,0},{2,3},{3,2},{4,5},{5,4},{6,7},{7,6},{8,9},{9,8},{10,11... | collective-permute-start | bytes 2261000 | tf_op jit(solution)/shard_map/ppermute | solution.py:381
  35.3 2.1 %collective-permute-done.16.refs_1_ = bf16[8,368,128]{2,1,0:T(8,128)(2,1)S(1)} collective-permute-done((bf16[8,368,128]{2,1,0:T(8,128)(2,1)}, bf16[8,368,128]{2,1,0:T(8,128)(2,1)S(1)}, u32[]{:S(2)}, u32[]{:S(2)}) %collective-permute-start.16) | collective-permute-done | bytes 753696 | tf_op jit(solution)/shard_map/ppermute | solution.py:381
  37.4 13.4 %collective-permute-start.18 = (bf16[8,368,128]{2,1,0:T(8,128)(2,1)}, bf16[8,368,128]{2,1,0:T(8,128)(2,1)}, u32[]{:S(2)}, u32[]{:S(2)}) collective-permute-start(bf16[8,368,128]{2,1,0:T(8,128)(2,1)} %all_to_all.15.refs_0_), channel_id=1, source_target_pairs={{0,48},{16,0},{32,16},{48,32},{1,49},{17,1},{33,17},{49,33},{2,50}... | collective-permute-start | bytes 2261000 | tf_op jit(solution)/shard_map/ppermute | solution.py:338
  50.8 0.0 collective-permute-start.19
  50.8 1.2 collective-permute-start.24
  52.0 31.1 %collective-permute-done.18.refs_0_ = bf16[8,368,128]{2,1,0:T(8,128)(2,1)} collective-permute-done((bf16[8,368,128]{2,1,0:T(8,128)(2,1)}, bf16[8,368,128]{2,1,0:T(8,128)(2,1)}, u32[]{:S(2)}, u32[]{:S(2)}) %collective-permute-start.18) | collective-permute-done | bytes 753696 | tf_op jit(solution)/shard_map/ppermute | solution.py:338
  83.1 1.2 collective-permute-start.20
  84.4 1.9 collective-permute-done.19.refs_1_
  86.3 1.5 collective-permute-start.21
  87.8 0.0 copy-done.7
  87.8 0.1 fusion.35
  87.9 0.8 collective-permute-start.12
  88.8 1.4 collective-permute-start.13
  90.2 0.4 collective-permute-done.12
  90.6 0.4 collective-permute-start.14
  91.0 0.1 stack.100.meta
  91.1 1.8 collective-permute-done.13
  92.9 1.5 collective-permute-done.14
  94.4 0.0 copy-start.13
  94.4 8.1 %partial_logits.3 = (s16[1,2,816,128]{3,2,1,0:T(8,128)(2,1)}, bf16[1,896,256]{2,1,0:T(8,128)(2,1)S(1)}) custom-call(s32[5]{0:T(128)S(1)} %stack.100.meta, s32[4,16,256]{2,1,0:T(8,128)S(1)} %pad_add_fusion.pos.places, bf16[8,368,128]{2,1,0:T(8,128)(2,1)} %all_to_all.15.refs_0_, bf16[8,368,128]{2,1,0:T(8,128)(2,1)S(1)} %collective-permute-done.16.refs_1_, ...), custom_call_target="tpu_custom_call" | custom-call | flops 4823449600 | bytes 9043968 | tf_op jit(solution)/shard_map/partial_logits/pallas_call | solution.py:122
  102.5 0.0 slice-start
  102.5 0.0 slice-start.1
  102.5 2.2 %collective-permute-start.17 = (s16[1,2,816,128]{3,2,1,0:T(8,128)(2,1)}, s16[1,2,816,128]{3,2,1,0:T(8,128)(2,1)S(1)}, u32[]{:S(2)}, u32[]{:S(2)}) collective-permute-start(s16[1,2,816,128]{3,2,1,0:T(8,128)(2,1)} %get-tuple-element.78), channel_id=1, source_target_pairs={{0,0},{16,80},{32,160},{48,240},{64,192},{80,16},{96,96},{112,176}... | collective-permute-start | bytes 1253384 | tf_op jit(solution)/shard_map/ppermute | solution.py:319
  104.7 0.0 collective-permute-done.24.refs_0_
  104.7 2.3 %collective-permute-start.25 = (bf16[8,368,128]{2,1,0:T(8,128)(2,1)}, bf16[8,368,128]{2,1,0:T(8,128)(2,1)S(1)}, u32[]{:S(2)}, u32[]{:S(2)}) collective-permute-start(bf16[8,368,128]{2,1,0:T(8,128)(2,1)} %collective-permute-done.24.refs_0_), channel_id=1, source_target_pairs={{0,1},{1,0},{2,3},{3,2},{4,5},{5,4},{6,7},{7,6},{8,9},{9,8},{10,11... | collective-permute-start | bytes 2261000 | tf_op jit(solution)/shard_map/ppermute | solution.py:381
  107.0 0.0 collective-permute-done.20.refs_2_
  107.0 0.0 collective-permute-done.21.refs_3_
  107.0 0.0 copy-done.13
  107.0 12.7 %partial_logits.4 = (s16[1,2,816,128]{3,2,1,0:T(8,128)(2,1)}, s16[1,2,816,128]{3,2,1,0:T(8,128)(2,1)}, bf16[2,896,256]{2,1,0:T(8,128)(2,1)S(1)}) custom-call(s32[5]{0:T(128)S(1)} %stack.100.meta, s32[4,16,256]{2,1,0:T(8,128)S(1)} %pad_add_fusion.pos.places, bf16[8,368,128]{2,1,0:T(8,128)(2,1)} %collective-permute-done.18.refs_0_, ...), custom_call_target="tpu_custom_call" | custom-call | flops 9646899200 | bytes 10551296 | tf_op jit(solution)/shard_map/partial_logits/pallas_call | solution.py:122
  119.7 3.7 %collective-permute-start.22 = (s16[1,2,816,128]{3,2,1,0:T(8,128)(2,1)}, s16[1,2,816,128]{3,2,1,0:T(8,128)(2,1)S(1)}, u32[]{:S(2)}, u32[]{:S(2)}) collective-permute-start(s16[1,2,816,128]{3,2,1,0:T(8,128)(2,1)} %get-tuple-element.79), channel_id=1, source_target_pairs={{0,64},{16,144},{32,224},{48,48},{64,0},{80,80},{96,160},{112,240}... | collective-permute-start | bytes 1253384 | tf_op jit(solution)/shard_map/ppermute | solution.py:319
  123.4 0.0 copy-start.12
  123.4 2.1 %collective-permute-start.23 = (s16[1,2,816,128]{3,2,1,0:T(8,128)(2,1)}, s16[1,2,816,128]{3,2,1,0:T(8,128)(2,1)}, u32[]{:S(2)}, u32[]{:S(2)}) collective-permute-start(s16[1,2,816,128]{3,2,1,0:T(8,128)(2,1)} %get-tuple-element.80), channel_id=1, source_target_pairs={{0,192},{16,16},{32,96},{48,176},{64,128},{80,208},{96,32},{112,11... | collective-permute-start | bytes 1253384 | tf_op jit(solution)/shard_map/ppermute | solution.py:319
  125.5 0.0 collective-permute-done.25.refs_1_
  125.5 0.0 slice-done
  125.5 0.0 slice-done.1
  125.6 8.3 %partial_logits.5 = (s16[1,2,816,128]{3,2,1,0:T(8,128)(2,1)}, bf16[1,896,256]{2,1,0:T(8,128)(2,1)S(1)}) custom-call(s32[5]{0:T(128)S(1)} %stack.100.meta, s32[4,16,256]{2,1,0:T(8,128)S(1)} %pad_add_fusion.pos.places, bf16[8,368,128]{2,1,0:T(8,128)(2,1)} %collective-permute-done.24.refs_0_, bf16[8,368,128]{2,1,0:T(8,128)(2,1)S(1)} %collective-permute-done.25.refs_1_, ...), custom_call_target="tpu_custom_call" | custom-call | flops 4823449600 | bytes 9043968 | tf_op jit(solution)/shard_map/partial_logits/pallas_call | solution.py:122
  133.9 3.8 %collective-permute-start.26 = (s16[1,2,816,128]{3,2,1,0:T(8,128)(2,1)}, s16[1,2,816,128]{3,2,1,0:T(8,128)(2,1)S(1)}, u32[]{:S(2)}, u32[]{:S(2)}) collective-permute-start(s16[1,2,816,128]{3,2,1,0:T(8,128)(2,1)} %get-tuple-element.81), channel_id=1, source_target_pairs={{0,128},{16,208},{32,32},{48,112},{64,64},{80,144},{96,224},{112,4... | collective-permute-start | bytes 1253384 | tf_op jit(solution)/shard_map/ppermute | solution.py:319
  137.6 0.0 copy-done.12
  137.7 0.0 collective-permute-done.17.a0
  137.7 0.0 collective-permute-done.22.a1
  137.7 0.0 collective-permute-done.23.a2
  137.7 1.7 early_sum.1.early
  139.4 8.9 %collective-permute-done.26.last = s16[1,2,816,128]{3,2,1,0:T(8,128)(2,1)S(1)} collective-permute-done((s16[1,2,816,128]{3,2,1,0:T(8,128)(2,1)}, s16[1,2,816,128]{3,2,1,0:T(8,128)(2,1)S(1)}, u32[]{:S(2)}, u32[]{:S(2)}) %collective-permute-start.26) | collective-permute-done | bytes 417824 | tf_op jit(solution)/shard_map/ppermute | solution.py:319
  148.4 2.0 %row_stats.1 = (f32[2,10,80,128]{3,2,1,0:T(8,128)S(1)}, f32[8,256]{1,0:T(8,128)S(1)}) custom-call(s32[16,256]{1,0:T(8,128)S(1)} %get-tuple-element.165.pos, s32[1,256]{1,0:T(1,128)S(1)} %bitcast.151, s32[4,16,256]{2,1,0:T(8,128)S(1)} %pad_add_fusion.pos.places, f32[2,10,80,128]{3,2,1,0:T(8,128)S(1)} %early_sum.1.early, ...), custom_call_target="tpu_custom_call" | custom-call | tf_op jit(solution)/shard_map/row_stats/pallas_call | solution.py:215
  150.4 22.6 %all_to_all.16.seen = f32[64,8,256]{2,1,0:T(8,128)S(1)} all-to-all(f32[64,8,256]{2,1,0:T(8,128)S(1)} %broadcast_in_dim.67), channel_id=1, replica_groups=mesh['x'=4,'y'=4,'z'=8,'c'=2] {'y','z','c'}, dimensions={0} | all-to-all | bytes 1048576 | tf_op jit(solution)/shard_map/all_to_all | solution.py:347
  172.9 0.8 row_grads.1
  173.8 1.0 collective-permute-start.27
  174.7 2.4 %collective-permute-start.28 = (bf16[10,80,128]{2,1,0:T(8,128)(2,1)S(1)}, bf16[10,80,128]{2,1,0:T(8,128)(2,1)S(1)}, u32[]{:S(2)}, u32[]{:S(2)}) collective-permute-start(bf16[10,80,128]{2,1,0:T(8,128)(2,1)S(1)} %get-tuple-element.85.refs_0_), channel_id=1, source_target_pairs={{0,128},{64,192},{128,0},{192,64},{1,129},{65,193},{129,1},{193,65... | collective-permute-start | bytes 614408 | tf_op jit(solution)/shard_map/ppermute | solution.py:397
  177.1 0.0 collective-permute-start.29
  177.1 0.5 slice.71
  178.3 0.6 fusion.45
  178.8 1.4 collective-permute-done.27.refs_1_
  180.3 2.1 %collective-permute-done.28.refs_2_ = bf16[10,80,128]{2,1,0:T(8,128)(2,1)S(1)} collective-permute-done((bf16[10,80,128]{2,1,0:T(8,128)(2,1)S(1)}, bf16[10,80,128]{2,1,0:T(8,128)(2,1)S(1)}, u32[]{:S(2)}, u32[]{:S(2)}) %collective-permute-start.28) | collective-permute-done | bytes 204832 | tf_op jit(solution)/shard_map/ppermute | solution.py:397
  182.4 5.2 %collective-permute-done.29.refs_3_ = bf16[10,80,128]{2,1,0:T(8,128)(2,1)S(1)} collective-permute-done((bf16[10,80,128]{2,1,0:T(8,128)(2,1)S(1)}, bf16[10,80,128]{2,1,0:T(8,128)(2,1)S(1)}, u32[]{:S(2)}, u32[]{:S(2)}) %collective-permute-start.29) | collective-permute-done | bytes 204832 | tf_op jit(solution)/shard_map/ppermute | solution.py:397
  187.6 0.0 copy-start.8
  187.6 6.3 %head_gradient.1 = f32[896,1280]{1,0:T(8,128)} custom-call(s32[5]{0:T(128)S(1)} %stack.100.meta, s32[4,16,256]{2,1,0:T(8,128)S(1)} %pad_add_fusion.pos.places, bf16[10,80,128]{2,1,0:T(8,128)(2,1)S(1)} %get-tuple-element.85.refs_0_, bf16[10,80,128]{2,1,0:T(8,128)(2,1)S(1)} %collective-permute-done.27.refs_1_, ...), custom_call_target="tpu_custom_call" | custom-call | tf_op jit(solution)/shard_map/head_gradient/pallas_call | solution.py:294
  193.9 0.0 copy-done.8
  (7 shorter events, 0.1 us)
Async XLA Ops:
  0.6 87.1 %copy-start.7 = (s32[256,10]{0,1:T(8,128)S(1)}, s32[256,10]{0,1:T(8,128)}, u32[]{:S(2)}) copy-start(s32[256,10]{0,1:T(8,128)} %param.12) | copy-start | bytes 30724
  2.3 0.7 collective-permute-start.15
  33.1 4.3 %collective-permute-start.16 = (bf16[8,368,128]{2,1,0:T(8,128)(2,1)}, bf16[8,368,128]{2,1,0:T(8,128)(2,1)S(1)}, u32[]{:S(2)}, u32[]{:S(2)}) collective-permute-start(bf16[8,368,128]{2,1,0:T(8,128)(2,1)} %all_to_all.15.refs_0_), channel_id=1, source_target_pairs={{0,1},{1,0},{2,3},{3,2},{4,5},{5,4},{6,7},{7,6},{8,9},{9,8},{10,11... | collective-permute-start | bytes 2261000 | tf_op jit(solution)/shard_map/ppermute | solution.py:381
  37.4 45.7 %collective-permute-start.18 = (bf16[8,368,128]{2,1,0:T(8,128)(2,1)}, bf16[8,368,128]{2,1,0:T(8,128)(2,1)}, u32[]{:S(2)}, u32[]{:S(2)}) collective-permute-start(bf16[8,368,128]{2,1,0:T(8,128)(2,1)} %all_to_all.15.refs_0_), channel_id=1, source_target_pairs={{0,48},{16,0},{32,16},{48,32},{1,49},{17,1},{33,17},{49,33},{2,50}... | collective-permute-start | bytes 2261000 | tf_op jit(solution)/shard_map/ppermute | solution.py:338
  50.8 35.4 %collective-permute-start.19 = (bf16[8,368,128]{2,1,0:T(8,128)(2,1)}, bf16[8,368,128]{2,1,0:T(8,128)(2,1)}, u32[]{:S(2)}, u32[]{:S(2)}) collective-permute-start(bf16[8,368,128]{2,1,0:T(8,128)(2,1)} %all_to_all.15.refs_0_), channel_id=1, source_target_pairs={{0,16},{16,32},{32,48},{48,0},{1,17},{17,33},{33,49},{49,1},{2,18}... | collective-permute-start | bytes 2261000 | tf_op jit(solution)/shard_map/ppermute | solution.py:339
  50.8 53.9 %collective-permute-start.24 = (bf16[8,368,128]{2,1,0:T(8,128)(2,1)}, bf16[8,368,128]{2,1,0:T(8,128)(2,1)}, u32[]{:S(2)}, u32[]{:S(2)}) collective-permute-start(bf16[8,368,128]{2,1,0:T(8,128)(2,1)} %all_to_all.15.refs_0_), channel_id=1, source_target_pairs={{0,32},{16,48},{32,0},{48,16},{1,33},{17,49},{33,1},{49,17},{2,34}... | collective-permute-start | bytes 2261000 | tf_op jit(solution)/shard_map/ppermute | solution.py:343
  83.1 23.9 %collective-permute-start.20 = (bf16[8,368,128]{2,1,0:T(8,128)(2,1)}, bf16[8,368,128]{2,1,0:T(8,128)(2,1)S(1)}, u32[]{:S(2)}, u32[]{:S(2)}) collective-permute-start(bf16[8,368,128]{2,1,0:T(8,128)(2,1)} %collective-permute-done.18.refs_0_), channel_id=1, source_target_pairs={{0,1},{1,0},{2,3},{3,2},{4,5},{5,4},{6,7},{7,6},{8,9},{9,8},{10,11... | collective-permute-start | bytes 2261000 | tf_op jit(solution)/shard_map/ppermute | solution.py:381
  86.3 20.8 %collective-permute-start.21 = (bf16[8,368,128]{2,1,0:T(8,128)(2,1)}, bf16[8,368,128]{2,1,0:T(8,128)(2,1)}, u32[]{:S(2)}, u32[]{:S(2)}) collective-permute-start(bf16[8,368,128]{2,1,0:T(8,128)(2,1)} %collective-permute-done.19.refs_1_), channel_id=1, source_target_pairs={{0,1},{1,0},{2,3},{3,2},{4,5},{5,4},{6,7},{7,6},{8,9},{9,8},{10,11... | collective-permute-start | bytes 2261000 | tf_op jit(solution)/shard_map/ppermute | solution.py:381
  87.9 2.7 %collective-permute-start.12 = (s32[16,256]{1,0:T(8,128)S(1)}, s32[16,256]{1,0:T(8,128)S(1)}, u32[]{:S(2)}, u32[]{:S(2)}) collective-permute-start(s32[16,256]{1,0:T(8,128)S(1)} %get-tuple-element.165.pos), channel_id=1, source_target_pairs={{0,192},{64,0},{128,64},{192,128},{1,193},{65,1},{129,65},{193,129... | collective-permute-start | bytes 49160 | tf_op jit(solution)/shard_map/ppermute | solution.py:397
  88.8 4.1 %collective-permute-start.13 = (s32[16,256]{1,0:T(8,128)S(1)}, s32[16,256]{1,0:T(8,128)S(1)}, u32[]{:S(2)}, u32[]{:S(2)}) collective-permute-start(s32[16,256]{1,0:T(8,128)S(1)} %get-tuple-element.165.pos), channel_id=1, source_target_pairs={{0,128},{64,192},{128,0},{192,64},{1,129},{65,193},{129,1},{193,65... | collective-permute-start | bytes 49160 | tf_op jit(solution)/shard_map/ppermute | solution.py:397
  90.6 3.8 %collective-permute-start.14 = (s32[16,256]{1,0:T(8,128)S(1)}, s32[16,256]{1,0:T(8,128)S(1)}, u32[]{:S(2)}, u32[]{:S(2)}) collective-permute-start(s32[16,256]{1,0:T(8,128)S(1)} %get-tuple-element.165.pos), channel_id=1, source_target_pairs={{0,64},{64,128},{128,192},{192,0},{1,65},{65,129},{129,193},{193,1... | collective-permute-start | bytes 49160 | tf_op jit(solution)/shard_map/ppermute | solution.py:397
  94.4 12.6 %copy-start.13 = (bf16[896,1280]{1,0:T(8,128)(2,1)S(1)}, bf16[896,1280]{1,0:T(8,128)(2,1)}, u32[]{:S(2)}) copy-start(bf16[896,1280]{1,0:T(8,128)(2,1)} %refs_3_.3) | copy-start | bytes 6881284
  102.5 23.0 %slice-start = ((s8[5242880]{0:T(1024)(128)(4,1)}), s8[4194304]{0:T(1024)(128)(4,1)S(1)}, s32[]{:S(2)}) async-start(s8[5242880]{0:T(1024)(128)(4,1)} %bitcast.158), calls=%async_computation.3 | async-start | bytes 8388608
  102.5 23.0 %slice-start.1 = ((s8[5242880]{0:T(1024)(128)(4,1)}), s8[1048576]{0:T(1024)(128)(4,1)S(1)}, s32[]{:S(2)}) async-start(s8[5242880]{0:T(1024)(128)(4,1)} %bitcast.158), calls=%async_computation.4 | async-start | bytes 2097152
  102.5 35.1 %collective-permute-start.17 = (s16[1,2,816,128]{3,2,1,0:T(8,128)(2,1)}, s16[1,2,816,128]{3,2,1,0:T(8,128)(2,1)S(1)}, u32[]{:S(2)}, u32[]{:S(2)}) collective-permute-start(s16[1,2,816,128]{3,2,1,0:T(8,128)(2,1)} %get-tuple-element.78), channel_id=1, source_target_pairs={{0,0},{16,80},{32,160},{48,240},{64,192},{80,16},{96,96},{112,176}... | collective-permute-start | bytes 1253384 | tf_op jit(solution)/shard_map/ppermute | solution.py:319
  104.7 20.8 %collective-permute-start.25 = (bf16[8,368,128]{2,1,0:T(8,128)(2,1)}, bf16[8,368,128]{2,1,0:T(8,128)(2,1)S(1)}, u32[]{:S(2)}, u32[]{:S(2)}) collective-permute-start(bf16[8,368,128]{2,1,0:T(8,128)(2,1)} %collective-permute-done.24.refs_0_), channel_id=1, source_target_pairs={{0,1},{1,0},{2,3},{3,2},{4,5},{5,4},{6,7},{7,6},{8,9},{9,8},{10,11... | collective-permute-start | bytes 2261000 | tf_op jit(solution)/shard_map/ppermute | solution.py:381
  119.7 18.0 %collective-permute-start.22 = (s16[1,2,816,128]{3,2,1,0:T(8,128)(2,1)}, s16[1,2,816,128]{3,2,1,0:T(8,128)(2,1)S(1)}, u32[]{:S(2)}, u32[]{:S(2)}) collective-permute-start(s16[1,2,816,128]{3,2,1,0:T(8,128)(2,1)} %get-tuple-element.79), channel_id=1, source_target_pairs={{0,64},{16,144},{32,224},{48,48},{64,0},{80,80},{96,160},{112,240}... | collective-permute-start | bytes 1253384 | tf_op jit(solution)/shard_map/ppermute | solution.py:319
  123.4 14.3 %copy-start.12 = (s32[256]{0:T(256)S(1)}, s32[256]{0:T(256)}, u32[]{:S(2)}) copy-start(s32[256]{0:T(256)} %param.13) | copy-start | bytes 3076
  123.4 14.3 %collective-permute-start.23 = (s16[1,2,816,128]{3,2,1,0:T(8,128)(2,1)}, s16[1,2,816,128]{3,2,1,0:T(8,128)(2,1)}, u32[]{:S(2)}, u32[]{:S(2)}) collective-permute-start(s16[1,2,816,128]{3,2,1,0:T(8,128)(2,1)} %get-tuple-element.80), channel_id=1, source_target_pairs={{0,192},{16,16},{32,96},{48,176},{64,128},{80,208},{96,32},{112,11... | collective-permute-start | bytes 1253384 | tf_op jit(solution)/shard_map/ppermute | solution.py:319
  133.9 14.5 %collective-permute-start.26 = (s16[1,2,816,128]{3,2,1,0:T(8,128)(2,1)}, s16[1,2,816,128]{3,2,1,0:T(8,128)(2,1)S(1)}, u32[]{:S(2)}, u32[]{:S(2)}) collective-permute-start(s16[1,2,816,128]{3,2,1,0:T(8,128)(2,1)} %get-tuple-element.81), channel_id=1, source_target_pairs={{0,128},{16,208},{32,32},{48,112},{64,64},{80,144},{96,224},{112,4... | collective-permute-start | bytes 1253384 | tf_op jit(solution)/shard_map/ppermute | solution.py:319
  173.8 6.5 %collective-permute-start.27 = (bf16[10,80,128]{2,1,0:T(8,128)(2,1)S(1)}, bf16[10,80,128]{2,1,0:T(8,128)(2,1)S(1)}, u32[]{:S(2)}, u32[]{:S(2)}) collective-permute-start(bf16[10,80,128]{2,1,0:T(8,128)(2,1)S(1)} %get-tuple-element.85.refs_0_), channel_id=1, source_target_pairs={{0,192},{64,0},{128,64},{192,128},{1,193},{65,1},{129,65},{193,129... | collective-permute-start | bytes 614408 | tf_op jit(solution)/shard_map/ppermute | solution.py:397
  174.7 7.6 %collective-permute-start.28 = (bf16[10,80,128]{2,1,0:T(8,128)(2,1)S(1)}, bf16[10,80,128]{2,1,0:T(8,128)(2,1)S(1)}, u32[]{:S(2)}, u32[]{:S(2)}) collective-permute-start(bf16[10,80,128]{2,1,0:T(8,128)(2,1)S(1)} %get-tuple-element.85.refs_0_), channel_id=1, source_target_pairs={{0,128},{64,192},{128,0},{192,64},{1,129},{65,193},{129,1},{193,65... | collective-permute-start | bytes 614408 | tf_op jit(solution)/shard_map/ppermute | solution.py:397
  177.1 10.5 %collective-permute-start.29 = (bf16[10,80,128]{2,1,0:T(8,128)(2,1)S(1)}, bf16[10,80,128]{2,1,0:T(8,128)(2,1)S(1)}, u32[]{:S(2)}, u32[]{:S(2)}) collective-permute-start(bf16[10,80,128]{2,1,0:T(8,128)(2,1)S(1)} %get-tuple-element.85.refs_0_), channel_id=1, source_target_pairs={{0,64},{64,128},{128,192},{192,0},{1,65},{65,129},{129,193},{193,1... | collective-permute-start | bytes 614408 | tf_op jit(solution)/shard_map/ppermute | solution.py:397
  187.6 6.3 %copy-start.8 = (s32[256,10]{0,1:T(8,128)S(1)}, s32[256,10]{0,1:T(8,128)}, u32[]{:S(2)}) copy-start(s32[256,10]{0,1:T(8,128)} %param.12) | copy-start | bytes 30724

commit v3 on v2

--- a/solution.py
+++ b/solution.py
@@ -412,8 +412,10 @@
         part, stud0 = run((0,), [pay], [other])
         got = [to_owner(part, order[0])]
         far = opposite(pay)
-        part, other_part, stud1 = run((1, 2), [after, ahead], [other_core(after), other_core(ahead)])
-        got += [to_owner(part, order[1]), to_owner(other_part, order[2])]
+        part, stud1 = run((1,), [after], [other_core(after)])
+        got.append(to_owner(part, order[1]))
+        part, stud3 = run((2,), [ahead], [other_core(ahead)])
+        got.append(to_owner(part, order[2]))
         part, stud2 = run((3,), [far], [other_core(far)])
         got.append(to_owner(part, order[3]))
 
@@ -421,7 +423,7 @@
         logits, stats = row_stats(own_pos, target[None], places, early, got[3])
         grad, rows = row_grads(own_pos, everyone(stats), logits)
         grads = [grad] + [from_line(grad, far) for far in range(1, sx)]
-        head = head_gradient(meta, places, grads, [stud0, stud1, stud2])
+        head = head_gradient(meta, places, grads, [stud0, stud1, stud3, stud2])
         start = (rows[2, 0] >= CAP, rows[0], rows[1], head)
         pays = {0: pay, 1: after, 3: ahead, 2: far}
 

time: 195 us -> 196 us (level)
  waiting for transfers between devices: 56.5 us -> 48.8 us
  blocking collectives: 52.6 us -> 59.4 us
  Pallas kernels: 39.9 us -> 43.8 us
  starting transfers between devices: 40.3 us -> 38.1 us
    ppermute x1, waiting for transfers between devices: 31.1 us -> 6.72 us  [neighbours(): after = lax.ppermute(pay, 'y', shift(-1))]
    ppermute x1, waiting for transfers between devices: 1.9 us -> 16 us  [neighbours(): before = lax.ppermute(pay, 'y', shift(1))]
    all_to_all x1, blocking collectives: 22.6 us -> 29.4 us  [everyone(): lax.all_to_all(copies, LOCAL, split_axis=0, concat_axis=0, tiled=True)]
    ppermute x1, starting transfers between devices: 13.4 us -> 6.61 us  [neighbours(): after = lax.ppermute(pay, 'y', shift(-1))]
    ppermute x1, starting transfers between devices: 0.01 us -> 6.82 us  [neighbours(): before = lax.ppermute(pay, 'y', shift(1))]
    pallas_call x3 -> x4, Pallas kernels: 29 us -> 33 us  [partial_logits(): pl.pallas_call(functools.partial(partial_kernel, steps), name='partial_lo...]
    ppermute x4, starting transfers between devices: 7.3 us -> 4.45 us  [other_core(): return lax.ppermute(pay, 'c', [(0, 1), (1, 0)]) if sc > 1 else pay]
    ppermute x6, waiting for transfers between devices: 12.5 us -> 15 us  [from_line(): return lax.ppermute(a, 'x', [(x, (x - far) % sx) for x in range(sx)])]
  transfers between devices with their start and end apart: 18 -> 18, of which waited for: 10 -> 9; matrix products, arithmetic and copies ran while one was open for 1% -> 1% of each run, Pallas kernels for 16% -> 18%
where the time goes in v3:
time: 196 us; the launch traced here: 195 us
  blocking collectives  59.4 us (30%)
  waiting for transfers between devices  48.8 us (25%)
  Pallas kernels  43.8 us (22%)
  starting transfers between devices  38.1 us (19%)
  local copies, waits for them, and re-layouts  2.12 us (1%)
    pallas_call x4, Pallas kernels, partial_logits(): pl.pallas_call(functools.partial(partial_kernel, steps), name='partial_lo...  33 us
    all_to_all x1, blocking collectives, per_device(): lax.all_to_all(jnp.broadcast_to(pay[None], (sz, *pay.shape)), 'z', 0, 0,...  30 us
    all_to_all x1, blocking collectives, everyone(): lax.all_to_all(copies, LOCAL, split_axis=0, concat_axis=0, tiled=True)  29.4 us
    ppermute x1, waiting for transfers between devices, neighbours(): before = lax.ppermute(pay, 'y', shift(1))  16 us
    ppermute x6, waiting for transfers between devices, from_line(): return lax.ppermute(a, 'x', [(x, (x - far) % sx) for x in range(sx)])  15 us
    ppermute x4, starting transfers between devices, to_owner(): return lax.ppermute(a, ('x', 'y'), turn(step))  12.3 us
    ppermute x4, waiting for transfers between devices, to_owner(): return lax.ppermute(a, ('x', 'y'), turn(step))  9.06 us
    ppermute x1, starting transfers between devices, neighbours(): before = lax.ppermute(pay, 'y', shift(1))  6.82 us
  transfers between devices with their start and end apart: 18, of which 9 were waited for; matrix products, arithmetic and copies ran while one was open for 1% of the time, Pallas kernels for 18%

profile of v3, /device:TPU:1, one launch (start us, length us, event | category | flops | bytes accessed | tf_op | source)
XLA Modules:
  0.0 194.9 jit_solution(16174080227010862684)
XLA Ops:
  0.6 0.0 copy-start.7
  0.6 0.8 reshape.122
  1.4 0.8 pad_maximum_fusion.5
  2.3 0.7 collective-permute-start.15
  2.9 0.0 collective-permute-done.15
  2.9 0.1 broadcast_in_dim.66
  3.1 30.0 %all_to_all.15.refs_0_ = bf16[8,368,128]{2,1,0:T(8,128)(2,1)} all-to-all(bf16[8,368,128]{2,1,0:T(8,128)(2,1)S(1)} %broadcast_in_dim.66), channel_id=1, replica_groups=mesh['x'=4,'y'=4,'z'=8,'c'=2] {'z'}, dimensions={0} | all-to-all | bytes 1507328 | tf_op jit(solution)/shard_map/all_to_all | solution.py:401
  33.1 2.3 %collective-permute-start.16 = (bf16[8,368,128]{2,1,0:T(8,128)(2,1)}, bf16[8,368,128]{2,1,0:T(8,128)(2,1)S(1)}, u32[]{:S(2)}, u32[]{:S(2)}) collective-permute-start(bf16[8,368,128]{2,1,0:T(8,128)(2,1)} %all_to_all.15.refs_0_), channel_id=1, source_target_pairs={{0,1},{1,0},{2,3},{3,2},{4,5},{5,4},{6,7},{7,6},{8,9},{9,8},{10,11... | collective-permute-start | bytes 2261000 | tf_op jit(solution)/shard_map/ppermute | solution.py:381
  35.3 2.1 %collective-permute-done.16.refs_1_ = bf16[8,368,128]{2,1,0:T(8,128)(2,1)S(1)} collective-permute-done((bf16[8,368,128]{2,1,0:T(8,128)(2,1)}, bf16[8,368,128]{2,1,0:T(8,128)(2,1)S(1)}, u32[]{:S(2)}, u32[]{:S(2)}) %collective-permute-start.16) | collective-permute-done | bytes 753696 | tf_op jit(solution)/shard_map/ppermute | solution.py:381
  37.4 6.8 %collective-permute-start.21 = (bf16[8,368,128]{2,1,0:T(8,128)(2,1)}, bf16[8,368,128]{2,1,0:T(8,128)(2,1)}, u32[]{:S(2)}, u32[]{:S(2)}) collective-permute-start(bf16[8,368,128]{2,1,0:T(8,128)(2,1)} %all_to_all.15.refs_0_), channel_id=1, source_target_pairs={{0,16},{16,32},{32,48},{48,0},{1,17},{17,33},{33,49},{49,1},{2,18}... | collective-permute-start | bytes 2261000 | tf_op jit(solution)/shard_map/ppermute | solution.py:339
  44.2 6.6 %collective-permute-start.18 = (bf16[8,368,128]{2,1,0:T(8,128)(2,1)}, bf16[8,368,128]{2,1,0:T(8,128)(2,1)}, u32[]{:S(2)}, u32[]{:S(2)}) collective-permute-start(bf16[8,368,128]{2,1,0:T(8,128)(2,1)} %all_to_all.15.refs_0_), channel_id=1, source_target_pairs={{0,48},{16,0},{32,16},{48,32},{1,49},{17,1},{33,17},{49,33},{2,50}... | collective-permute-start | bytes 2261000 | tf_op jit(solution)/shard_map/ppermute | solution.py:338
  50.8 1.2 collective-permute-start.24
  52.0 16.0 %collective-permute-done.21.refs_0_ = bf16[8,368,128]{2,1,0:T(8,128)(2,1)} collective-permute-done((bf16[8,368,128]{2,1,0:T(8,128)(2,1)}, bf16[8,368,128]{2,1,0:T(8,128)(2,1)}, u32[]{:S(2)}, u32[]{:S(2)}) %collective-permute-start.21) | collective-permute-done | bytes 753696 | tf_op jit(solution)/shard_map/ppermute | solution.py:339
  68.0 0.9 collective-permute-start.22
  68.9 0.0 copy-done.7
  68.9 0.1 fusion.35
  69.1 0.8 collective-permute-start.12
  70.0 1.4 collective-permute-start.13
  71.4 0.8 collective-permute-done.12
  72.2 0.4 collective-permute-start.14
  72.6 0.1 stack.100.meta
  72.7 1.8 collective-permute-done.13
  74.4 1.9 collective-permute-done.14
  76.4 0.0 slice-start.1
  76.4 0.0 copy-start.13
  76.4 6.7 %collective-permute-done.18.refs_0_ = bf16[8,368,128]{2,1,0:T(8,128)(2,1)} collective-permute-done((bf16[8,368,128]{2,1,0:T(8,128)(2,1)}, bf16[8,368,128]{2,1,0:T(8,128)(2,1)}, u32[]{:S(2)}, u32[]{:S(2)}) %collective-permute-start.18) | collective-permute-done | bytes 753696 | tf_op jit(solution)/shard_map/ppermute | solution.py:338
  83.1 1.2 collective-permute-start.19
  84.4 7.9 %partial_logits.4 = (s16[1,2,816,128]{3,2,1,0:T(8,128)(2,1)}, bf16[1,896,256]{2,1,0:T(8,128)(2,1)S(1)}) custom-call(s32[5]{0:T(128)S(1)} %stack.100.meta, s32[4,16,256]{2,1,0:T(8,128)S(1)} %pad_add_fusion.pos.places, bf16[8,368,128]{2,1,0:T(8,128)(2,1)} %all_to_all.15.refs_0_, bf16[8,368,128]{2,1,0:T(8,128)(2,1)S(1)} %collective-permute-done.16.refs_1_, ...), custom_call_target="tpu_custom_call" | custom-call | flops 4823449600 | bytes 9043968 | tf_op jit(solution)/shard_map/partial_logits/pallas_call | solution.py:122
  92.3 1.7 collective-permute-start.17
  94.0 0.0 collective-permute-done.24.refs_0_
  94.0 0.0 collective-permute-start.25
  94.0 0.0 collective-permute-done.22.refs_1_
  94.0 0.0 slice-done
  94.0 0.0 slice-done.1
  94.0 0.0 copy-done.13
  94.0 8.3 %partial_logits.6 = (s16[1,2,816,128]{3,2,1,0:T(8,128)(2,1)}, bf16[1,896,256]{2,1,0:T(8,128)(2,1)S(1)}) custom-call(s32[5]{0:T(128)S(1)} %stack.100.meta, s32[4,16,256]{2,1,0:T(8,128)S(1)} %pad_add_fusion.pos.places, bf16[8,368,128]{2,1,0:T(8,128)(2,1)} %collective-permute-done.21.refs_0_, bf16[8,368,128]{2,1,0:T(8,128)(2,1)S(1)} %collective-permute-done.22.refs_1_, ...), custom_call_target="tpu_custom_call" | custom-call | flops 4823449600 | bytes 9043968 | tf_op jit(solution)/shard_map/partial_logits/pallas_call | solution.py:122
  102.3 5.3 %collective-permute-start.23 = (s16[1,2,816,128]{3,2,1,0:T(8,128)(2,1)}, s16[1,2,816,128]{3,2,1,0:T(8,128)(2,1)S(1)}, u32[]{:S(2)}, u32[]{:S(2)}) collective-permute-start(s16[1,2,816,128]{3,2,1,0:T(8,128)(2,1)} %get-tuple-element.81), channel_id=1, source_target_pairs={{0,192},{16,16},{32,96},{48,176},{64,128},{80,208},{96,32},{112,11... | collective-permute-start | bytes 1253384 | tf_op jit(solution)/shard_map/ppermute | solution.py:319
  107.7 0.0 collective-permute-done.19.refs_1_
  107.7 8.4 %partial_logits.5 = (s16[1,2,816,128]{3,2,1,0:T(8,128)(2,1)}, bf16[1,896,256]{2,1,0:T(8,128)(2,1)S(1)}) custom-call(s32[5]{0:T(128)S(1)} %stack.100.meta, s32[4,16,256]{2,1,0:T(8,128)S(1)} %pad_add_fusion.pos.places, bf16[8,368,128]{2,1,0:T(8,128)(2,1)} %collective-permute-done.18.refs_0_, bf16[8,368,128]{2,1,0:T(8,128)(2,1)S(1)} %collective-permute-done.19.refs_1_, ...), custom_call_target="tpu_custom_call" | custom-call | flops 4823449600 | bytes 9043968 | tf_op jit(solution)/shard_map/partial_logits/pallas_call | solution.py:122
  116.1 0.0 copy-start.12
  116.1 1.9 collective-permute-start.20
  118.0 0.0 collective-permute-done.25.refs_1_
  118.0 8.4 %partial_logits.7 = (s16[1,2,816,128]{3,2,1,0:T(8,128)(2,1)}, bf16[1,896,256]{2,1,0:T(8,128)(2,1)S(1)}) custom-call(s32[5]{0:T(128)S(1)} %stack.100.meta, s32[4,16,256]{2,1,0:T(8,128)S(1)} %pad_add_fusion.pos.places, bf16[8,368,128]{2,1,0:T(8,128)(2,1)} %collective-permute-done.24.refs_0_, bf16[8,368,128]{2,1,0:T(8,128)(2,1)S(1)} %collective-permute-done.25.refs_1_, ...), custom_call_target="tpu_custom_call" | custom-call | flops 4823449600 | bytes 9043968 | tf_op jit(solution)/shard_map/partial_logits/pallas_call | solution.py:122
  126.4 3.4 %collective-permute-start.26 = (s16[1,2,816,128]{3,2,1,0:T(8,128)(2,1)}, s16[1,2,816,128]{3,2,1,0:T(8,128)(2,1)S(1)}, u32[]{:S(2)}, u32[]{:S(2)}) collective-permute-start(s16[1,2,816,128]{3,2,1,0:T(8,128)(2,1)} %get-tuple-element.82), channel_id=1, source_target_pairs={{0,128},{16,208},{32,32},{48,112},{64,64},{80,144},{96,224},{112,4... | collective-permute-start | bytes 1253384 | tf_op jit(solution)/shard_map/ppermute | solution.py:319
  129.8 0.0 copy-done.12
  129.8 0.0 collective-permute-done.17.a0
  129.9 0.0 collective-permute-done.23.a2
  129.9 0.0 collective-permute-done.20.a1
  129.9 1.7 early_sum.1.early
  131.6 9.1 %collective-permute-done.26.last = s16[1,2,816,128]{3,2,1,0:T(8,128)(2,1)S(1)} collective-permute-done((s16[1,2,816,128]{3,2,1,0:T(8,128)(2,1)}, s16[1,2,816,128]{3,2,1,0:T(8,128)(2,1)S(1)}, u32[]{:S(2)}, u32[]{:S(2)}) %collective-permute-start.26) | collective-permute-done | bytes 417824 | tf_op jit(solution)/shard_map/ppermute | solution.py:319
  140.7 2.0 %row_stats.1 = (f32[2,10,80,128]{3,2,1,0:T(8,128)S(1)}, f32[8,256]{1,0:T(8,128)S(1)}) custom-call(s32[16,256]{1,0:T(8,128)S(1)} %get-tuple-element.167.pos, s32[1,256]{1,0:T(1,128)S(1)} %bitcast.151, s32[4,16,256]{2,1,0:T(8,128)S(1)} %pad_add_fusion.pos.places, f32[2,10,80,128]{3,2,1,0:T(8,128)S(1)} %early_sum.1.early, ...), custom_call_target="tpu_custom_call" | custom-call | tf_op jit(solution)/shard_map/row_stats/pallas_call | solution.py:215
  142.7 29.4 %all_to_all.16.seen = f32[64,8,256]{2,1,0:T(8,128)S(1)} all-to-all(f32[64,8,256]{2,1,0:T(8,128)S(1)} %broadcast_in_dim.67), channel_id=1, replica_groups=mesh['x'=4,'y'=4,'z'=8,'c'=2] {'y','z','c'}, dimensions={0} | all-to-all | bytes 1048576 | tf_op jit(solution)/shard_map/all_to_all | solution.py:347
  172.1 0.8 row_grads.1
  172.9 2.7 %collective-permute-start.27 = (bf16[10,80,128]{2,1,0:T(8,128)(2,1)S(1)}, bf16[10,80,128]{2,1,0:T(8,128)(2,1)S(1)}, u32[]{:S(2)}, u32[]{:S(2)}) collective-permute-start(bf16[10,80,128]{2,1,0:T(8,128)(2,1)S(1)} %get-tuple-element.86.refs_0_), channel_id=1, source_target_pairs={{0,192},{64,0},{128,64},{192,128},{1,193},{65,1},{129,65},{193,129... | collective-permute-start | bytes 614408 | tf_op jit(solution)/shard_map/ppermute | solution.py:397
  175.7 0.4 collective-permute-start.28
  176.1 0.3 collective-permute-start.29
  176.4 0.5 slice.71
  177.5 0.6 fusion.45
  178.1 6.0 %collective-permute-done.27.refs_1_ = bf16[10,80,128]{2,1,0:T(8,128)(2,1)S(1)} collective-permute-done((bf16[10,80,128]{2,1,0:T(8,128)(2,1)S(1)}, bf16[10,80,128]{2,1,0:T(8,128)(2,1)S(1)}, u32[]{:S(2)}, u32[]{:S(2)}) %collective-permute-start.27) | collective-permute-done | bytes 204832 | tf_op jit(solution)/shard_map/ppermute | solution.py:397
  184.1 0.0 collective-permute-done.28.refs_2_
  184.1 4.4 %collective-permute-done.29.refs_3_ = bf16[10,80,128]{2,1,0:T(8,128)(2,1)S(1)} collective-permute-done((bf16[10,80,128]{2,1,0:T(8,128)(2,1)S(1)}, bf16[10,80,128]{2,1,0:T(8,128)(2,1)S(1)}, u32[]{:S(2)}, u32[]{:S(2)}) %collective-permute-start.29) | collective-permute-done | bytes 204832 | tf_op jit(solution)/shard_map/ppermute | solution.py:397
  188.6 0.0 copy-start.8
  188.6 6.3 %head_gradient.1 = f32[896,1280]{1,0:T(8,128)} custom-call(s32[5]{0:T(128)S(1)} %stack.100.meta, s32[4,16,256]{2,1,0:T(8,128)S(1)} %pad_add_fusion.pos.places, bf16[10,80,128]{2,1,0:T(8,128)(2,1)S(1)} %get-tuple-element.86.refs_0_, bf16[10,80,128]{2,1,0:T(8,128)(2,1)S(1)} %collective-permute-done.27.refs_1_, ...), custom_call_target="tpu_custom_call" | custom-call | tf_op jit(solution)/shard_map/head_gradient/pallas_call | solution.py:294
  194.9 0.0 copy-done.8
  (8 shorter events, 0.1 us)
Async XLA Ops:
  0.6 68.3 %copy-start.7 = (s32[256,10]{0,1:T(8,128)S(1)}, s32[256,10]{0,1:T(8,128)}, u32[]{:S(2)}) copy-start(s32[256,10]{0,1:T(8,128)} %param.12) | copy-start | bytes 30724
  2.3 0.7 collective-permute-start.15
  33.1 4.3 %collective-permute-start.16 = (bf16[8,368,128]{2,1,0:T(8,128)(2,1)}, bf16[8,368,128]{2,1,0:T(8,128)(2,1)S(1)}, u32[]{:S(2)}, u32[]{:S(2)}) collective-permute-start(bf16[8,368,128]{2,1,0:T(8,128)(2,1)} %all_to_all.15.refs_0_), channel_id=1, source_target_pairs={{0,1},{1,0},{2,3},{3,2},{4,5},{5,4},{6,7},{7,6},{8,9},{9,8},{10,11... | collective-permute-start | bytes 2261000 | tf_op jit(solution)/shard_map/ppermute | solution.py:381
  37.4 30.6 %collective-permute-start.21 = (bf16[8,368,128]{2,1,0:T(8,128)(2,1)}, bf16[8,368,128]{2,1,0:T(8,128)(2,1)}, u32[]{:S(2)}, u32[]{:S(2)}) collective-permute-start(bf16[8,368,128]{2,1,0:T(8,128)(2,1)} %all_to_all.15.refs_0_), channel_id=1, source_target_pairs={{0,16},{16,32},{32,48},{48,0},{1,17},{17,33},{33,49},{49,1},{2,18}... | collective-permute-start | bytes 2261000 | tf_op jit(solution)/shard_map/ppermute | solution.py:339
  44.2 38.9 %collective-permute-start.18 = (bf16[8,368,128]{2,1,0:T(8,128)(2,1)}, bf16[8,368,128]{2,1,0:T(8,128)(2,1)}, u32[]{:S(2)}, u32[]{:S(2)}) collective-permute-start(bf16[8,368,128]{2,1,0:T(8,128)(2,1)} %all_to_all.15.refs_0_), channel_id=1, source_target_pairs={{0,48},{16,0},{32,16},{48,32},{1,49},{17,1},{33,17},{49,33},{2,50}... | collective-permute-start | bytes 2261000 | tf_op jit(solution)/shard_map/ppermute | solution.py:338
  50.8 43.1 %collective-permute-start.24 = (bf16[8,368,128]{2,1,0:T(8,128)(2,1)}, bf16[8,368,128]{2,1,0:T(8,128)(2,1)}, u32[]{:S(2)}, u32[]{:S(2)}) collective-permute-start(bf16[8,368,128]{2,1,0:T(8,128)(2,1)} %all_to_all.15.refs_0_), channel_id=1, source_target_pairs={{0,32},{16,48},{32,0},{48,16},{1,33},{17,49},{33,1},{49,17},{2,34}... | collective-permute-start | bytes 2261000 | tf_op jit(solution)/shard_map/ppermute | solution.py:343
  68.0 26.0 %collective-permute-start.22 = (bf16[8,368,128]{2,1,0:T(8,128)(2,1)}, bf16[8,368,128]{2,1,0:T(8,128)(2,1)S(1)}, u32[]{:S(2)}, u32[]{:S(2)}) collective-permute-start(bf16[8,368,128]{2,1,0:T(8,128)(2,1)} %collective-permute-done.21.refs_0_), channel_id=1, source_target_pairs={{0,1},{1,0},{2,3},{3,2},{4,5},{5,4},{6,7},{7,6},{8,9},{9,8},{10,11... | collective-permute-start | bytes 2261000 | tf_op jit(solution)/shard_map/ppermute | solution.py:381
  69.1 3.1 %collective-permute-start.12 = (s32[16,256]{1,0:T(8,128)S(1)}, s32[16,256]{1,0:T(8,128)S(1)}, u32[]{:S(2)}, u32[]{:S(2)}) collective-permute-start(s32[16,256]{1,0:T(8,128)S(1)} %get-tuple-element.167.pos), channel_id=1, source_target_pairs={{0,192},{64,0},{128,64},{192,128},{1,193},{65,1},{129,65},{193,129... | collective-permute-start | bytes 49160 | tf_op jit(solution)/shard_map/ppermute | solution.py:397
  70.0 4.5 %collective-permute-start.13 = (s32[16,256]{1,0:T(8,128)S(1)}, s32[16,256]{1,0:T(8,128)S(1)}, u32[]{:S(2)}, u32[]{:S(2)}) collective-permute-start(s32[16,256]{1,0:T(8,128)S(1)} %get-tuple-element.167.pos), channel_id=1, source_target_pairs={{0,128},{64,192},{128,0},{192,64},{1,129},{65,193},{129,1},{193,65... | collective-permute-start | bytes 49160 | tf_op jit(solution)/shard_map/ppermute | solution.py:397
  72.2 4.2 %collective-permute-start.14 = (s32[16,256]{1,0:T(8,128)S(1)}, s32[16,256]{1,0:T(8,128)S(1)}, u32[]{:S(2)}, u32[]{:S(2)}) collective-permute-start(s32[16,256]{1,0:T(8,128)S(1)} %get-tuple-element.167.pos), channel_id=1, source_target_pairs={{0,64},{64,128},{128,192},{192,0},{1,65},{65,129},{129,193},{193,1... | collective-permute-start | bytes 49160 | tf_op jit(solution)/shard_map/ppermute | solution.py:397
  76.4 17.6 %slice-start = ((s8[5242880]{0:T(1024)(128)(4,1)}), s8[4194304]{0:T(1024)(128)(4,1)S(1)}, s32[]{:S(2)}) async-start(s8[5242880]{0:T(1024)(128)(4,1)} %bitcast.158), calls=%async_computation.3 | async-start | bytes 8388608
  76.4 17.6 %slice-start.1 = ((s8[5242880]{0:T(1024)(128)(4,1)}), s8[1048576]{0:T(1024)(128)(4,1)S(1)}, s32[]{:S(2)}) async-start(s8[5242880]{0:T(1024)(128)(4,1)} %bitcast.158), calls=%async_computation.4 | async-start | bytes 2097152
  76.4 17.6 %copy-start.13 = (bf16[896,1280]{1,0:T(8,128)(2,1)S(1)}, bf16[896,1280]{1,0:T(8,128)(2,1)}, u32[]{:S(2)}) copy-start(bf16[896,1280]{1,0:T(8,128)(2,1)} %refs_3_.7) | copy-start | bytes 6881284
  83.1 24.5 %collective-permute-start.19 = (bf16[8,368,128]{2,1,0:T(8,128)(2,1)}, bf16[8,368,128]{2,1,0:T(8,128)(2,1)S(1)}, u32[]{:S(2)}, u32[]{:S(2)}) collective-permute-start(bf16[8,368,128]{2,1,0:T(8,128)(2,1)} %collective-permute-done.18.refs_0_), channel_id=1, source_target_pairs={{0,1},{1,0},{2,3},{3,2},{4,5},{5,4},{6,7},{7,6},{8,9},{9,8},{10,11... | collective-permute-start | bytes 2261000 | tf_op jit(solution)/shard_map/ppermute | solution.py:381
  92.3 37.6 %collective-permute-start.17 = (s16[1,2,816,128]{3,2,1,0:T(8,128)(2,1)}, s16[1,2,816,128]{3,2,1,0:T(8,128)(2,1)S(1)}, u32[]{:S(2)}, u32[]{:S(2)}) collective-permute-start(s16[1,2,816,128]{3,2,1,0:T(8,128)(2,1)} %get-tuple-element.79), channel_id=1, source_target_pairs={{0,0},{16,80},{32,160},{48,240},{64,192},{80,16},{96,96},{112,176}... | collective-permute-start | bytes 1253384 | tf_op jit(solution)/shard_map/ppermute | solution.py:319
  94.0 24.0 %collective-permute-start.25 = (bf16[8,368,128]{2,1,0:T(8,128)(2,1)}, bf16[8,368,128]{2,1,0:T(8,128)(2,1)S(1)}, u32[]{:S(2)}, u32[]{:S(2)}) collective-permute-start(bf16[8,368,128]{2,1,0:T(8,128)(2,1)} %collective-permute-done.24.refs_0_), channel_id=1, source_target_pairs={{0,1},{1,0},{2,3},{3,2},{4,5},{5,4},{6,7},{7,6},{8,9},{9,8},{10,11... | collective-permute-start | bytes 2261000 | tf_op jit(solution)/shard_map/ppermute | solution.py:381
  102.3 27.5 %collective-permute-start.23 = (s16[1,2,816,128]{3,2,1,0:T(8,128)(2,1)}, s16[1,2,816,128]{3,2,1,0:T(8,128)(2,1)S(1)}, u32[]{:S(2)}, u32[]{:S(2)}) collective-permute-start(s16[1,2,816,128]{3,2,1,0:T(8,128)(2,1)} %get-tuple-element.81), channel_id=1, source_target_pairs={{0,192},{16,16},{32,96},{48,176},{64,128},{80,208},{96,32},{112,11... | collective-permute-start | bytes 1253384 | tf_op jit(solution)/shard_map/ppermute | solution.py:319
  116.1 13.8 %copy-start.12 = (s32[256]{0:T(256)S(1)}, s32[256]{0:T(256)}, u32[]{:S(2)}) copy-start(s32[256]{0:T(256)} %param.13) | copy-start | bytes 3076
  116.1 13.8 %collective-permute-start.20 = (s16[1,2,816,128]{3,2,1,0:T(8,128)(2,1)}, s16[1,2,816,128]{3,2,1,0:T(8,128)(2,1)}, u32[]{:S(2)}, u32[]{:S(2)}) collective-permute-start(s16[1,2,816,128]{3,2,1,0:T(8,128)(2,1)} %get-tuple-element.80), channel_id=1, source_target_pairs={{0,64},{16,144},{32,224},{48,48},{64,0},{80,80},{96,160},{112,240}... | collective-permute-start | bytes 1253384 | tf_op jit(solution)/shard_map/ppermute | solution.py:319
  126.4 14.3 %collective-permute-start.26 = (s16[1,2,816,128]{3,2,1,0:T(8,128)(2,1)}, s16[1,2,816,128]{3,2,1,0:T(8,128)(2,1)S(1)}, u32[]{:S(2)}, u32[]{:S(2)}) collective-permute-start(s16[1,2,816,128]{3,2,1,0:T(8,128)(2,1)} %get-tuple-element.82), channel_id=1, source_target_pairs={{0,128},{16,208},{32,32},{48,112},{64,64},{80,144},{96,224},{112,4... | collective-permute-start | bytes 1253384 | tf_op jit(solution)/shard_map/ppermute | solution.py:319
  172.9 11.2 %collective-permute-start.27 = (bf16[10,80,128]{2,1,0:T(8,128)(2,1)S(1)}, bf16[10,80,128]{2,1,0:T(8,128)(2,1)S(1)}, u32[]{:S(2)}, u32[]{:S(2)}) collective-permute-start(bf16[10,80,128]{2,1,0:T(8,128)(2,1)S(1)} %get-tuple-element.86.refs_0_), channel_id=1, source_target_pairs={{0,192},{64,0},{128,64},{192,128},{1,193},{65,1},{129,65},{193,129... | collective-permute-start | bytes 614408 | tf_op jit(solution)/shard_map/ppermute | solution.py:397
  175.7 8.5 %collective-permute-start.28 = (bf16[10,80,128]{2,1,0:T(8,128)(2,1)S(1)}, bf16[10,80,128]{2,1,0:T(8,128)(2,1)S(1)}, u32[]{:S(2)}, u32[]{:S(2)}) collective-permute-start(bf16[10,80,128]{2,1,0:T(8,128)(2,1)S(1)} %get-tuple-element.86.refs_0_), channel_id=1, source_target_pairs={{0,128},{64,192},{128,0},{192,64},{1,129},{65,193},{129,1},{193,65... | collective-permute-start | bytes 614408 | tf_op jit(solution)/shard_map/ppermute | solution.py:397
  176.1 12.5 %collective-permute-start.29 = (bf16[10,80,128]{2,1,0:T(8,128)(2,1)S(1)}, bf16[10,80,128]{2,1,0:T(8,128)(2,1)S(1)}, u32[]{:S(2)}, u32[]{:S(2)}) collective-permute-start(bf16[10,80,128]{2,1,0:T(8,128)(2,1)S(1)} %get-tuple-element.86.refs_0_), channel_id=1, source_target_pairs={{0,64},{64,128},{128,192},{192,0},{1,65},{65,129},{129,193},{193,1... | collective-permute-start | bytes 614408 | tf_op jit(solution)/shard_map/ppermute | solution.py:397
  188.6 6.3 %copy-start.8 = (s32[256,10]{0,1:T(8,128)S(1)}, s32[256,10]{0,1:T(8,128)}, u32[]{:S(2)}) copy-start(s32[256,10]{0,1:T(8,128)} %param.12) | copy-start | bytes 30724

commit v4 on v3

--- a/solution.py
+++ b/solution.py
@@ -9,6 +9,8 @@
 from jax.sharding import PartitionSpec as P
 
 CAP = 80
+LIST = 512
+STARTS = 8
 NEG = -1e30
 BLOCK = 128
 LOCAL = ("y", "z", "c")
@@ -22,9 +24,19 @@
     return pltpu.CompilerParams(vmem_limit_bytes=36 << 20, **kw)
 
 
-def selector(pos_row):
+def window(meta, held, b):
+    run = meta[STARTS + held * 16 + b]
+    start = pl.multiple_of(jnp.minimum(run, LIST - CAP), 16)
+    return start, pl.ds(start, CAP), run - start
+
+
+def selector(pos_row, start):
     lines = lax.broadcasted_iota(jnp.int32, (CAP, pos_row.shape[-1]), 0)
-    return lines == pos_row
+    return lines + start == pos_row
+
+
+def from_row(first):
+    return lax.broadcasted_iota(jnp.int32, (CAP, BLOCK), 0) >= first
 
 
 def diagonal():
@@ -36,7 +48,7 @@
     peak = jnp.max(jnp.abs(logits), axis=1, keepdims=True)
     power = jnp.floor(jnp.log2(jnp.maximum(peak, 1e-30)))
     scaled = jnp.round(logits * jnp.exp2(14.0 - power))
-    values = jnp.clip(scaled, -32767.0, 32767.0).astype(jnp.int32).astype(jnp.int16)
+    values = jnp.clip(scaled, -32767.0, 32767.0).astype(jnp.int32)
     return values, jnp.sum(jnp.where(diagonal(), power, 0.0), axis=0, keepdims=True)
 
 
@@ -55,16 +67,18 @@
     fetch_s = pltpu.make_async_copy(far_s, head_s, sems.at[1])
     fetch_t.start()
     fetch_s.start()
-    blocks = sel.shape[0] // CAP
+    blocks = far_t.shape[1] // BLOCK
     depth, tokens = mine[0].shape[0], sel.shape[1]
     both = kept.shape[1] // depth
     first = meta[0] == 0
     powers[...] = jnp.zeros_like(powers)
     for i in range(count):
         held = meta[1 + steps[i]]
+        sel[...] = jnp.zeros_like(sel)
         for k in range(blocks):
-            mark = selector(pos[held, k : k + 1, :]).astype(jnp.float32)
-            sel[k * CAP : (k + 1) * CAP, :] = mark.astype(jnp.bfloat16)
+            start, here, _ = window(meta, held, k)
+            mark = selector(pos[held, k : k + 1, :], start).astype(jnp.float32)
+            sel[here, :] = (sel[here, :].astype(jnp.float32) + mark).astype(jnp.bfloat16)
 
         def chunk(z, _, i=i):
             a, o = mine[i][z, :tokens, :], others[i][z, :tokens, :]
@@ -91,16 +105,23 @@
             )
 
     def two_blocks(b, _):
-        here = pl.ds(pl.multiple_of(b * 2 * CAP, 16), 2 * CAP)
         columns = pl.ds(pl.multiple_of(b * 2 * BLOCK, 2 * BLOCK), 2 * BLOCK)
+        runs = [
+            [window(meta, meta[1 + steps[i]], 2 * b + k) for k in range(2)] for i in range(count)
+        ]
         for h, (rows, head) in enumerate(((rows_t, head_t), (rows_s, head_s))):
-            lines = rows[:, here, :].reshape(count * 2 * CAP, rows.shape[-1])
+            lines = jnp.concatenate(
+                [rows[i, runs[i][k][1], :] for i in range(count) for k in range(2)], axis=0
+            )
             product = dot(lines, head[:, columns], ((1,), (0,)))
             for i in range(count):
                 for k in range(2):
                     at = (2 * i + k) * CAP
                     values, power = coded(product[at : at + CAP, k * BLOCK : (k + 1) * BLOCK])
-                    outs[i][0, h, pl.ds(pl.multiple_of((2 * b + k) * CAP, 16), CAP), :] = values
+                    _, here, first = runs[i][k]
+                    before = outs[i][0, h, here, :].astype(jnp.int32)
+                    values = jnp.where(from_row(first), values, before)
+                    outs[i][0, h, here, :] = values.astype(jnp.int16)
                     powers[2 * i + h, pl.ds(2 * b + k, 1), :] = power
         return 0
 
@@ -109,7 +130,7 @@
     lax.fori_loop(0, blocks // 2, two_blocks, 0)
     for i in range(count):
         for h in range(2):
-            outs[i][0, h, blocks * CAP :, :] = powers[2 * i + h].astype(jnp.int32).astype(jnp.int16)
+            outs[i][0, h, LIST:, :] = powers[2 * i + h].astype(jnp.int32).astype(jnp.int16)
 
 
 def partial_logits(meta, pos, steps, mine, others, head_t, head_s):
@@ -118,7 +139,7 @@
     deep_t, width = head_t.shape
     deep_s = head_s.shape[0]
     blocks = width // BLOCK
-    coded_rows = blocks * CAP + 16
+    coded_rows = LIST + 16
     return pl.pallas_call(
         functools.partial(partial_kernel, steps),
         name="partial_logits",
@@ -126,9 +147,9 @@
         + [pl.BlockSpec(memory_space=pltpu.VMEM)] * (2 * count + 1)
         + [pl.BlockSpec(memory_space=pl.ANY)] * 2,
         scratch_shapes=[
-            pltpu.VMEM((blocks * CAP, tokens), jnp.bfloat16),
-            pltpu.VMEM((count, blocks * CAP, deep_t), jnp.bfloat16),
-            pltpu.VMEM((count, blocks * CAP, deep_s), jnp.bfloat16),
+            pltpu.VMEM((LIST, tokens), jnp.bfloat16),
+            pltpu.VMEM((count, LIST, deep_t), jnp.bfloat16),
+            pltpu.VMEM((count, LIST, deep_s), jnp.bfloat16),
             pltpu.VMEM((2 * count, 16, BLOCK), jnp.float32),
             pltpu.VMEM(head_t.shape, head_t.dtype),
             pltpu.VMEM(head_s.shape, head_s.dtype),
@@ -153,40 +174,47 @@
     return jnp.sum(jnp.where(mark, column, jnp.zeros_like(column)), axis=0, keepdims=True)
 
 
-def unpacked(ref, h, blocks):
-    powers = ref[0, h, blocks * CAP :, :].astype(jnp.int32).astype(jnp.float32)
+def unpacked(meta, ref, h, blocks):
+    powers = ref[0, h, LIST:, :].astype(jnp.int32).astype(jnp.float32)
     return [
-        decoded(ref[0, h, b * CAP : (b + 1) * CAP, :], powers[b : b + 1, :]) for b in range(blocks)
+        decoded(ref[0, h, window(meta, 0, b)[1], :], powers[b : b + 1, :]) for b in range(blocks)
     ]
 
 
-def early_kernel(a0, a1, a2, total):
+def early_kernel(meta, a0, a1, a2, total):
     blocks = total.shape[1]
     for h in range(2):
-        for b, (x, y, z) in enumerate(zip(*(unpacked(a, h, blocks) for a in (a0, a1, a2)))):
+        parts = zip(*(unpacked(meta, a, h, blocks) for a in (a0, a1, a2)))
+        for b, (x, y, z) in enumerate(parts):
             total[h, b] = x + y + z
 
 
-def early_sum(parts):
-    blocks = parts[0].shape[2] // CAP
+def scalars_first(arrays):
+    return [pl.BlockSpec(memory_space=pltpu.SMEM)] + [
+        pl.BlockSpec(memory_space=pltpu.VMEM)
+    ] * arrays
+
+
+def early_sum(meta, blocks, parts):
     return pl.pallas_call(
         early_kernel,
         name="early_sum",
+        in_specs=scalars_first(3),
         out_shape=jax.ShapeDtypeStruct((2, blocks, CAP, BLOCK), jnp.float32),
         compiler_params=params(),
-    )(*parts)
-
-
-def stats_kernel(pos, target, places, early, last, logits, stats):
+    )(meta, *parts)
+
+
+def stats_kernel(meta, pos, target, places, early, last, logits, stats):
     blocks = logits.shape[1]
     tokens = pos.shape[-1]
     tops = [jnp.full((1, tokens), NEG, jnp.float32) for _ in range(2)]
     for h in range(2):
-        for b, part in enumerate(unpacked(last, h, blocks)):
+        for b, part in enumerate(unpacked(meta, last, h, blocks)):
             total = early[h, b] + part
             logits[h, b] = total
             peak = jnp.max(total, axis=1, keepdims=True)
-            mark = selector(pos[b : b + 1, :])
+            mark = selector(pos[b : b + 1, :], window(meta, 0, b)[0])
             tops[h] = jnp.maximum(
                 tops[h], jnp.max(jnp.where(mark, peak, NEG), axis=0, keepdims=True)
             )
@@ -194,7 +222,7 @@
     sum_t, cross, sum_s, picked = zero, zero, zero, zero
     lanes = lax.broadcasted_iota(jnp.int32, (CAP, BLOCK), 1)
     for b in range(blocks):
-        mark = selector(pos[b : b + 1, :])
+        mark = selector(pos[b : b + 1, :], window(meta, 0, b)[0])
         lt, ls = logits[0, b], logits[1, b]
         et = jnp.exp(lt - spread(mark, tops[0]))
         es = jnp.exp(ls - spread(mark, tops[1]))
@@ -205,22 +233,23 @@
         picked = picked + fold(
             mark, jnp.sum(jnp.where(lanes == wanted, ls, 0.0), axis=1, keepdims=True)
         )
-    most = jnp.max(places[...].astype(jnp.float32), axis=(0, 1))[None]
-    most = jnp.broadcast_to(jnp.max(most, axis=1, keepdims=True), zero.shape)
+    most = jnp.max(jnp.concatenate([places[t, 11:12, :] for t in range(4)]), axis=0, keepdims=True)
+    most = most.astype(jnp.float32)
     lines = [tops[0], sum_t, cross, tops[1], sum_s, picked, most, zero]
     stats[...] = jnp.concatenate(lines, axis=0)
 
 
-def row_stats(pos, target, places, early, last):
+def row_stats(meta, pos, target, places, early, last):
     return pl.pallas_call(
         stats_kernel,
         name="row_stats",
+        in_specs=scalars_first(5),
         out_shape=[
             jax.ShapeDtypeStruct(early.shape, jnp.float32),
             jax.ShapeDtypeStruct((8, pos.shape[-1]), jnp.float32),
         ],
         compiler_params=params(),
-    )(pos, target, places, early, last)
+    )(meta, pos, target, places, early, last)
 
 
 def combined(seen):
@@ -238,28 +267,35 @@
     return top_t, sum_t, top_s, sum_s, cross / sum_t - log_t + log_s, picked - log_s
 
 
-def grad_kernel(pos, seen, logits, grad, rows):
+def grad_kernel(meta, pos, seen, logits, grad, rows, lines):
     top_t, sum_t, top_s, sum_s, row_kl, logprob = combined(seen[...])
     most = jnp.max(seen[:, 6, :], axis=0, keepdims=True)
     rows[...] = jnp.concatenate([row_kl, logprob, most] + [most] * 5, axis=0)
     inv_t, inv_s = 1.0 / sum_t, 1.0 / sum_s
+    lines[...] = jnp.zeros_like(lines)
     for b in range(logits.shape[1]):
-        mark = selector(pos[b : b + 1, :])
-        et = jnp.exp(logits[0, b] - spread(mark, top_t)) * spread(mark, inv_t)
-        es = jnp.exp(logits[1, b] - spread(mark, top_s)) * spread(mark, inv_s)
-        grad[b] = (es - et).astype(jnp.bfloat16)
-
-
-def row_grads(pos, seen, logits):
+        start, here, first = window(meta, 0, b)
+        mark = selector(pos[b : b + 1, :], start)
+        share_t, share_s = spread(mark, inv_t), spread(mark, inv_s)
+        et = jnp.exp(logits[0, b] - spread(mark, top_t)) * share_t
+        es = jnp.exp(logits[1, b] - spread(mark, top_s)) * share_s
+        own = jnp.where(share_s > 0.0, es - et, 0.0)
+        lines[here, :] = jnp.where(from_row(first), own, lines[here, :])
+    grad[...] = lines[...].astype(jnp.bfloat16)
+
+
+def row_grads(meta, pos, seen, logits):
     return pl.pallas_call(
         grad_kernel,
         name="row_grads",
+        in_specs=scalars_first(3),
         out_shape=[
-            jax.ShapeDtypeStruct(logits.shape[1:], jnp.bfloat16),
+            jax.ShapeDtypeStruct((LIST, BLOCK), jnp.bfloat16),
             jax.ShapeDtypeStruct((8, pos.shape[-1]), jnp.float32),
         ],
+        scratch_shapes=[pltpu.VMEM((LIST, BLOCK), jnp.float32)],
         compiler_params=params(),
-    )(pos, seen, logits)
+    )(meta, pos, seen, logits)
 
 
 def head_kernel(meta, places, *refs):
@@ -281,15 +317,16 @@
     for t, grad in enumerate(grads):
         pair = []
         for k in range(2):
-            mark = selector(places[t, 2 * b + k][None]).astype(jnp.float32).astype(jnp.bfloat16)
-            pair.append(dot(mark, grad[k], ((0,), (0,))).astype(jnp.bfloat16))
+            start, here, _ = window(meta, t, 2 * b + k)
+            mark = selector(places[t, 2 * b + k][None], start).astype(jnp.float32)
+            mark = mark.astype(jnp.bfloat16)
+            pair.append(dot(mark, grad[here, :], ((0,), (0,))).astype(jnp.bfloat16))
         right.append(jnp.concatenate(pair, axis=1))
     out[...] = dot(left[...], jnp.concatenate(right, axis=0), ((1,), (0,)))
 
 
-def head_gradient(meta, places, grads, studs):
+def head_gradient(meta, places, grads, studs, blocks):
     deep, tokens = studs[0].shape[1:]
-    blocks = grads[0].shape[0]
     whole = lambda a: pl.BlockSpec(a.shape, lambda b, meta: (0,) * a.ndim)
     return pl.pallas_call(
         head_kernel,
@@ -298,8 +335,7 @@
             num_scalar_prefetch=1,
             grid=(blocks // 2,),
             in_specs=[whole(places)]
-            + [pl.BlockSpec((2, CAP, BLOCK), lambda b, meta: (b, 0, 0)) for _ in grads]
-            + [whole(a) for a in studs],
+            + [whole(a) for a in (*grads, *studs)],
             out_specs=pl.BlockSpec((deep, 2 * BLOCK), lambda b, meta: (0, b)),
             scratch_shapes=[pltpu.VMEM((deep, 4 * tokens), jnp.bfloat16)],
         ),
@@ -389,8 +425,19 @@
         open_ = (allowed > 0).T.astype(jnp.float32)
         before = jnp.triu(jnp.ones((tokens, tokens), jnp.float32), 1)
         place = dot(open_.astype(jnp.bfloat16), before.astype(jnp.bfloat16), ((1,), (0,)))
-        own_pos = jnp.where(open_ > 0, place.astype(jnp.int32), -1)
-        own_pos = jnp.pad(own_pos, ((0, -blocks % 8), (0, 0)), constant_values=-1)
+        count = jnp.sum(open_, axis=1).astype(jnp.int32)
+        room = (count + 15) // 16 * 16
+        ahead_of = jnp.arange(blocks)[None, :] < jnp.arange(blocks)[:, None]
+        runs = jnp.sum(jnp.where(ahead_of, room[None, :], 0), axis=1)
+        over = jnp.logical_or(jnp.sum(room) > LIST, jnp.max(count) > CAP).astype(jnp.int32)
+        own_pos = jnp.where(open_ > 0, place.astype(jnp.int32) + runs[:, None], -1)
+        own_pos = jnp.concatenate(
+            [
+                own_pos,
+                jnp.pad(jnp.minimum(runs, LIST), (0, tokens - blocks))[None],
+                jnp.broadcast_to(over, (6 - blocks % 8 + 1, tokens)),
+            ]
+        )
         order = (0, 1, 3, 2)
 
         def from_line(a, far):
@@ -400,7 +447,8 @@
         places = jnp.stack(places)
         pay = lax.all_to_all(jnp.broadcast_to(pay[None], (sz, *pay.shape)), "z", 0, 0, tiled=True)
         here, row, core = (lax.axis_index(name).astype(jnp.int32) for name in ("x", "y", "c"))
-        meta = jnp.stack([core] + [(row + step - 2 * here) % sx for step in order])
+        meta = jnp.stack([core] + [(row + step - 2 * here) % sx for step in order] + [core] * 3)
+        meta = jnp.concatenate([meta, places[:, blocks, :16].reshape(-1)])
         place_of = (row * sz + lax.axis_index("z")) * sc + core
         target = sampled - place_of * width
 
@@ -419,12 +467,12 @@
         part, stud2 = run((3,), [far], [other_core(far)])
         got.append(to_owner(part, order[3]))
 
-        early = early_sum(got[:3])
-        logits, stats = row_stats(own_pos, target[None], places, early, got[3])
-        grad, rows = row_grads(own_pos, everyone(stats), logits)
+        early = early_sum(meta, blocks, got[:3])
+        logits, stats = row_stats(meta, own_pos, target[None], places, early, got[3])
+        grad, rows = row_grads(meta, own_pos, everyone(stats), logits)
         grads = [grad] + [from_line(grad, far) for far in range(1, sx)]
-        head = head_gradient(meta, places, grads, [stud0, stud1, stud3, stud2])
-        start = (rows[2, 0] >= CAP, rows[0], rows[1], head)
+        head = head_gradient(meta, places, grads, [stud0, stud1, stud3, stud2], blocks)
+        start = (rows[2, 0] > 0.5, rows[0], rows[1], head)
         pays = {0: pay, 1: after, 3: ahead, 2: far}
 
         def redo(_):

time: 196 us -> 178 us (0.908)
  waiting for transfers between devices: 48.8 us -> 39.9 us
  blocking collectives: 59.4 us -> 51.9 us
  starting transfers between devices: 38.1 us -> 36.1 us
    ppermute x6, waiting for transfers between devices: 15 us -> 6.76 us  [from_line(): return lax.ppermute(a, 'x', [(x, (x - far) % sx) for x in range(sx)])]
    all_to_all x1, blocking collectives: 29.4 us -> 21.9 us  [everyone(): lax.all_to_all(copies, LOCAL, split_axis=0, concat_axis=0, tiled=True)]
    ppermute x1, waiting for transfers between devices: 6.72 us -> 14.1 us  [neighbours(): after = lax.ppermute(pay, 'y', shift(-1))]
    ppermute x1, waiting for transfers between devices: 16 us -> 11.2 us  [neighbours(): before = lax.ppermute(pay, 'y', shift(1))]
    ppermute x4, waiting for transfers between devices: 9.06 us -> 6.45 us  [to_owner(): return lax.ppermute(a, ('x', 'y'), turn(step))]
    pallas_call x4, Pallas kernels: 33 us -> 30.7 us  [partial_logits(): pl.pallas_call(functools.partial(partial_kernel, steps), name='partial_lo...]
  transfers between devices with their start and end apart: 18 -> 18, of which waited for: 9 -> 8; matrix products, arithmetic and copies ran while one was open for 1% -> 1% of each run, Pallas kernels for 18% -> 18%
where the time goes in v4:
time: 178 us; the launch traced here: 177 us
  blocking collectives  51.9 us (29%)
  Pallas kernels  42.1 us (24%)
  waiting for transfers between devices  39.9 us (22%)
  starting transfers between devices  36.1 us (20%)
  between operations  2.95 us (2%)
  local copies, waits for them, and re-layouts  2.3 us (1%)
  other arithmetic  1.89 us (1%)
    pallas_call x4, Pallas kernels, partial_logits(): pl.pallas_call(functools.partial(partial_kernel, steps), name='partial_lo...  30.7 us
    all_to_all x1, blocking collectives, per_device(): lax.all_to_all(jnp.broadcast_to(pay[None], (sz, *pay.shape)), 'z', 0, 0,...  30 us
    all_to_all x1, blocking collectives, everyone(): lax.all_to_all(copies, LOCAL, split_axis=0, concat_axis=0, tiled=True)  21.9 us
    ppermute x1, waiting for transfers between devices, neighbours(): after = lax.ppermute(pay, 'y', shift(-1))  14.1 us
    ppermute x4, starting transfers between devices, to_owner(): return lax.ppermute(a, ('x', 'y'), turn(step))  12 us
    ppermute x1, waiting for transfers between devices, neighbours(): before = lax.ppermute(pay, 'y', shift(1))  11.2 us
    ppermute x1, starting transfers between devices, neighbours(): before = lax.ppermute(pay, 'y', shift(1))  6.82 us
    ppermute x6, waiting for transfers between devices, from_line(): return lax.ppermute(a, 'x', [(x, (x - far) % sx) for x in range(sx)])  6.76 us
  transfers between devices with their start and end apart: 18, of which 8 were waited for; matrix products, arithmetic and copies ran while one was open for 1% of the time, Pallas kernels for 18%

profile of v4, /device:TPU:1, one launch (start us, length us, event | category | flops | bytes accessed | tf_op | source)
XLA Modules:
  0.0 177.3 jit_solution(12790551472649391215)
XLA Ops:
  0.6 0.0 copy-start.7
  0.6 0.8 reshape.143
  1.4 0.8 pad_maximum_fusion.5
  2.3 0.7 collective-permute-start.15
  2.9 0.0 collective-permute-done.15
  2.9 0.1 broadcast_in_dim.92
  3.1 30.0 %all_to_all.15.refs_0_ = bf16[8,368,128]{2,1,0:T(8,128)(2,1)} all-to-all(bf16[8,368,128]{2,1,0:T(8,128)(2,1)S(1)} %broadcast_in_dim.92), channel_id=1, replica_groups=mesh['x'=4,'y'=4,'z'=8,'c'=2] {'z'}, dimensions={0} | all-to-all | bytes 1507328 | tf_op jit(solution)/shard_map/all_to_all | solution.py:448
  33.1 2.3 %collective-permute-start.16 = (bf16[8,368,128]{2,1,0:T(8,128)(2,1)}, bf16[8,368,128]{2,1,0:T(8,128)(2,1)S(1)}, u32[]{:S(2)}, u32[]{:S(2)}) collective-permute-start(bf16[8,368,128]{2,1,0:T(8,128)(2,1)} %all_to_all.15.refs_0_), channel_id=1, source_target_pairs={{0,1},{1,0},{2,3},{3,2},{4,5},{5,4},{6,7},{7,6},{8,9},{9,8},{10,11... | collective-permute-start | bytes 2261000 | tf_op jit(solution)/shard_map/ppermute | solution.py:417
  35.3 0.1 convert_reduce_fusion
  35.4 0.7 fusion.43
  36.1 1.3 collective-permute-done.16.refs_1_
  37.4 6.8 %collective-permute-start.21 = (bf16[8,368,128]{2,1,0:T(8,128)(2,1)}, bf16[8,368,128]{2,1,0:T(8,128)(2,1)}, u32[]{:S(2)}, u32[]{:S(2)}) collective-permute-start(bf16[8,368,128]{2,1,0:T(8,128)(2,1)} %all_to_all.15.refs_0_), channel_id=1, source_target_pairs={{0,16},{16,32},{32,48},{48,0},{1,17},{17,33},{33,49},{49,1},{2,18}... | collective-permute-start | bytes 2261000 | tf_op jit(solution)/shard_map/ppermute | solution.py:375
  44.2 0.1 select_reduce_fusion.1
  44.3 0.1 fusion.36
  44.5 6.7 %collective-permute-start.18 = (bf16[8,368,128]{2,1,0:T(8,128)(2,1)}, bf16[8,368,128]{2,1,0:T(8,128)(2,1)}, u32[]{:S(2)}, u32[]{:S(2)}) collective-permute-start(bf16[8,368,128]{2,1,0:T(8,128)(2,1)} %all_to_all.15.refs_0_), channel_id=1, source_target_pairs={{0,48},{16,0},{32,16},{48,32},{1,49},{17,1},{33,17},{49,33},{2,50}... | collective-permute-start | bytes 2261000 | tf_op jit(solution)/shard_map/ppermute | solution.py:374
  52.4 0.1 pad.31.clone
  52.5 0.1 add_add_fusion.1.pos
  52.6 0.8 collective-permute-start.12
  53.4 1.4 collective-permute-start.13
  54.8 0.0 collective-permute-start.14
  54.8 0.8 collective-permute-done.12
  55.6 1.2 collective-permute-start.24
  56.8 11.2 %collective-permute-done.21.refs_0_ = bf16[8,368,128]{2,1,0:T(8,128)(2,1)} collective-permute-done((bf16[8,368,128]{2,1,0:T(8,128)(2,1)}, bf16[8,368,128]{2,1,0:T(8,128)(2,1)}, u32[]{:S(2)}, u32[]{:S(2)}) %collective-permute-start.21) | collective-permute-done | bytes 753696 | tf_op jit(solution)/shard_map/ppermute | solution.py:375
  68.0 0.9 collective-permute-start.22
  68.9 0.1 fusion.52
  69.0 0.0 collective-permute-done.13
  69.0 0.0 collective-permute-done.14
  69.1 0.1 reshape_squeeze.3
  69.2 0.1 concatenate.22.meta
  69.3 14.1 %collective-permute-done.18.refs_0_ = bf16[8,368,128]{2,1,0:T(8,128)(2,1)} collective-permute-done((bf16[8,368,128]{2,1,0:T(8,128)(2,1)}, bf16[8,368,128]{2,1,0:T(8,128)(2,1)}, u32[]{:S(2)}, u32[]{:S(2)}) %collective-permute-start.18) | collective-permute-done | bytes 753696 | tf_op jit(solution)/shard_map/ppermute | solution.py:374
  83.4 1.2 collective-permute-start.19
  84.6 7.3 %partial_logits.4 = (s16[1,2,528,128]{3,2,1,0:T(8,128)(2,1)S(1)}, bf16[1,896,256]{2,1,0:T(8,128)(2,1)S(1)}) custom-call(s32[72]{0:T(128)S(1)} %concatenate.22.meta, s32[4,16,256]{2,1,0:T(8,128)S(1)} %pad_add_fusion.pos.places, bf16[8,368,128]{2,1,0:T(8,128)(2,1)} %all_to_all.15.refs_0_, bf16[8,368,128]{2,1,0:T(8,128)(2,1)S(1)} %collective-permute-done.16.refs_1_, ...), custom_call_target="tpu_custom_call" | custom-call | flops 4823449600 | bytes 9043968 | tf_op jit(solution)/shard_map/partial_logits/pallas_call | solution.py:143
  91.9 0.0 slice-start
  91.9 0.0 slice-start.1
  91.9 0.8 collective-permute-start.17
  92.8 0.0 collective-permute-done.24.refs_0_
  92.8 0.1 collective-permute-start.25
  92.9 0.0 collective-permute-done.22.refs_1_
  92.9 7.4 %partial_logits.6 = (s16[1,2,528,128]{3,2,1,0:T(8,128)(2,1)S(1)}, bf16[1,896,256]{2,1,0:T(8,128)(2,1)S(1)}) custom-call(s32[72]{0:T(128)S(1)} %concatenate.22.meta, s32[4,16,256]{2,1,0:T(8,128)S(1)} %pad_add_fusion.pos.places, bf16[8,368,128]{2,1,0:T(8,128)(2,1)} %collective-permute-done.21.refs_0_, ...), custom_call_target="tpu_custom_call" | custom-call | flops 4823449600 | bytes 9043968 | tf_op jit(solution)/shard_map/partial_logits/pallas_call | solution.py:143
  100.3 5.8 %collective-permute-start.23 = (s16[1,2,528,128]{3,2,1,0:T(8,128)(2,1)S(1)}, s16[1,2,528,128]{3,2,1,0:T(8,128)(2,1)S(1)}, u32[]{:S(2)}, u32[]{:S(2)}) collective-permute-start(s16[1,2,528,128]{3,2,1,0:T(8,128)(2,1)S(1)} %get-tuple-element.81), channel_id=1, source_target_pairs={{0,192},{16,16},{32,96},{48,176},{64,128},{80,208},{96,32},{112,11... | collective-permute-start | bytes 811016 | tf_op jit(solution)/shard_map/ppermute | solution.py:355
  106.2 0.0 collective-permute-done.19.refs_1_
  106.2 8.0 %partial_logits.5 = (s16[1,2,528,128]{3,2,1,0:T(8,128)(2,1)}, bf16[1,896,256]{2,1,0:T(8,128)(2,1)S(1)}) custom-call(s32[72]{0:T(128)S(1)} %concatenate.22.meta, s32[4,16,256]{2,1,0:T(8,128)S(1)} %pad_add_fusion.pos.places, bf16[8,368,128]{2,1,0:T(8,128)(2,1)} %collective-permute-done.18.refs_0_, bf16[8,368,128]{2,1,0:T(8,128)(2,1)S(1)} %collective-permute-done.19.refs_1_, ...), custom_call_target="tpu_custom_call" | custom-call | flops 4823449600 | bytes 9043968 | tf_op jit(solution)/shard_map/partial_logits/pallas_call | solution.py:143
  114.2 0.0 copy-start.11
  114.2 1.9 %collective-permute-start.20 = (s16[1,2,528,128]{3,2,1,0:T(8,128)(2,1)}, s16[1,2,528,128]{3,2,1,0:T(8,128)(2,1)S(1)}, u32[]{:S(2)}, u32[]{:S(2)}) collective-permute-start(s16[1,2,528,128]{3,2,1,0:T(8,128)(2,1)} %get-tuple-element.80), channel_id=1, source_target_pairs={{0,64},{16,144},{32,224},{48,48},{64,0},{80,80},{96,160},{112,240}... | collective-permute-start | bytes 811016 | tf_op jit(solution)/shard_map/ppermute | solution.py:355
  116.1 0.0 collective-permute-done.25.refs_1_
  116.1 8.0 %partial_logits.7 = (s16[1,2,528,128]{3,2,1,0:T(8,128)(2,1)}, bf16[1,896,256]{2,1,0:T(8,128)(2,1)S(1)}) custom-call(s32[72]{0:T(128)S(1)} %concatenate.22.meta, s32[4,16,256]{2,1,0:T(8,128)S(1)} %pad_add_fusion.pos.places, bf16[8,368,128]{2,1,0:T(8,128)(2,1)} %collective-permute-done.24.refs_0_, bf16[8,368,128]{2,1,0:T(8,128)(2,1)S(1)} %collective-permute-done.25.refs_1_, ...), custom_call_target="tpu_custom_call" | custom-call | flops 4823449600 | bytes 9043968 | tf_op jit(solution)/shard_map/partial_logits/pallas_call | solution.py:143
  124.1 3.4 %collective-permute-start.26 = (s16[1,2,528,128]{3,2,1,0:T(8,128)(2,1)}, s16[1,2,528,128]{3,2,1,0:T(8,128)(2,1)S(1)}, u32[]{:S(2)}, u32[]{:S(2)}) collective-permute-start(s16[1,2,528,128]{3,2,1,0:T(8,128)(2,1)} %get-tuple-element.82), channel_id=1, source_target_pairs={{0,128},{16,208},{32,32},{48,112},{64,64},{80,144},{96,224},{112,4... | collective-permute-start | bytes 811016 | tf_op jit(solution)/shard_map/ppermute | solution.py:355
  127.6 0.0 collective-permute-done.17.a0
  127.6 0.0 collective-permute-done.23.a2
  127.6 0.0 collective-permute-done.20.a1
  127.6 1.3 early_sum.1.early
  128.9 6.4 %collective-permute-done.26.last = s16[1,2,528,128]{3,2,1,0:T(8,128)(2,1)S(1)} collective-permute-done((s16[1,2,528,128]{3,2,1,0:T(8,128)(2,1)}, s16[1,2,528,128]{3,2,1,0:T(8,128)(2,1)S(1)}, u32[]{:S(2)}, u32[]{:S(2)}) %collective-permute-start.26) | collective-permute-done | bytes 270368 | tf_op jit(solution)/shard_map/ppermute | solution.py:355
  135.3 2.5 %row_stats.1 = (f32[2,10,80,128]{3,2,1,0:T(8,128)S(1)}, f32[8,256]{1,0:T(8,128)S(1)}) custom-call(s32[72]{0:T(128)S(1)} %concatenate.22.meta, s32[16,256]{1,0:T(8,128)S(1)} %add_add_fusion.1.pos, s32[1,256]{1,0:T(1,128)S(1)} %bitcast.152, s32[4,16,256]{2,1,0:T(8,128)S(1)} %pad_add_fusion.pos.places, f32[2,10,80,128]{3,2,1,0:T(8,128)S(1)} %early_sum.1.early, ...), custom_call_target="tpu_custom_call" | custom-call | tf_op jit(solution)/shard_map/row_stats/pallas_call | solution.py:243
  137.9 21.9 %all_to_all.16.seen = f32[64,8,256]{2,1,0:T(8,128)S(1)} all-to-all(f32[64,8,256]{2,1,0:T(8,128)S(1)} %broadcast_in_dim.93), channel_id=1, replica_groups=mesh['x'=4,'y'=4,'z'=8,'c'=2] {'y','z','c'}, dimensions={0} | all-to-all | bytes 1048576 | tf_op jit(solution)/shard_map/all_to_all | solution.py:383
  159.8 1.4 row_grads.1
  161.1 0.2 collective-permute-start.27
  161.4 1.4 collective-permute-start.28
  162.8 0.5 collective-permute-start.29
  163.3 0.5 slice.75
  164.4 0.6 fusion.46
  165.0 1.0 collective-permute-done.27.refs_1_
  166.0 1.4 collective-permute-done.28.refs_2_
  167.4 3.6 %collective-permute-done.29.refs_3_ = bf16[512,128]{1,0:T(8,128)(2,1)S(1)} collective-permute-done((bf16[512,128]{1,0:T(8,128)(2,1)S(1)}, bf16[512,128]{1,0:T(8,128)(2,1)S(1)}, u32[]{:S(2)}, u32[]{:S(2)}) %collective-permute-start.29) | collective-permute-done | bytes 131104 | tf_op jit(solution)/shard_map/ppermute | solution.py:444
  171.0 6.3 %head_gradient.1 = f32[896,1280]{1,0:T(8,128)} custom-call(s32[72]{0:T(128)S(1)} %concatenate.22.meta, s32[4,16,256]{2,1,0:T(8,128)S(1)} %pad_add_fusion.pos.places, bf16[512,128]{1,0:T(8,128)(2,1)S(1)} %get-tuple-element.86.refs_0_, bf16[512,128]{1,0:T(8,128)(2,1)S(1)} %collective-permute-done.27.refs_1_, ...), custom_call_target="tpu_custom_call" | custom-call | tf_op jit(solution)/shard_map/head_gradient/pallas_call | solution.py:331
  (22 shorter events, 0.1 us)
Async XLA Ops:
  0.6 34.7 %copy-start.7 = (s32[256,10]{0,1:T(8,128)S(1)}, s32[256,10]{0,1:T(8,128)}, u32[]{:S(2)}) copy-start(s32[256,10]{0,1:T(8,128)} %param.12) | copy-start | bytes 30724
  2.3 0.7 collective-permute-start.15
  33.1 4.3 %collective-permute-start.16 = (bf16[8,368,128]{2,1,0:T(8,128)(2,1)}, bf16[8,368,128]{2,1,0:T(8,128)(2,1)S(1)}, u32[]{:S(2)}, u32[]{:S(2)}) collective-permute-start(bf16[8,368,128]{2,1,0:T(8,128)(2,1)} %all_to_all.15.refs_0_), channel_id=1, source_target_pairs={{0,1},{1,0},{2,3},{3,2},{4,5},{5,4},{6,7},{7,6},{8,9},{9,8},{10,11... | collective-permute-start | bytes 2261000 | tf_op jit(solution)/shard_map/ppermute | solution.py:417
  37.4 30.6 %collective-permute-start.21 = (bf16[8,368,128]{2,1,0:T(8,128)(2,1)}, bf16[8,368,128]{2,1,0:T(8,128)(2,1)}, u32[]{:S(2)}, u32[]{:S(2)}) collective-permute-start(bf16[8,368,128]{2,1,0:T(8,128)(2,1)} %all_to_all.15.refs_0_), channel_id=1, source_target_pairs={{0,16},{16,32},{32,48},{48,0},{1,17},{17,33},{33,49},{49,1},{2,18}... | collective-permute-start | bytes 2261000 | tf_op jit(solution)/shard_map/ppermute | solution.py:375
  44.5 38.9 %collective-permute-start.18 = (bf16[8,368,128]{2,1,0:T(8,128)(2,1)}, bf16[8,368,128]{2,1,0:T(8,128)(2,1)}, u32[]{:S(2)}, u32[]{:S(2)}) collective-permute-start(bf16[8,368,128]{2,1,0:T(8,128)(2,1)} %all_to_all.15.refs_0_), channel_id=1, source_target_pairs={{0,48},{16,0},{32,16},{48,32},{1,49},{17,1},{33,17},{49,33},{2,50}... | collective-permute-start | bytes 2261000 | tf_op jit(solution)/shard_map/ppermute | solution.py:374
  52.6 3.0 %collective-permute-start.12 = (s32[16,256]{1,0:T(8,128)S(1)}, s32[16,256]{1,0:T(8,128)S(1)}, u32[]{:S(2)}, u32[]{:S(2)}) collective-permute-start(s32[16,256]{1,0:T(8,128)S(1)} %add_add_fusion.1.pos), channel_id=1, source_target_pairs={{0,192},{64,0},{128,64},{192,128},{1,193},{65,1},{129,65},{193,129... | collective-permute-start | bytes 49160 | tf_op jit(solution)/shard_map/ppermute | solution.py:444
  53.4 15.7 %collective-permute-start.13 = (s32[16,256]{1,0:T(8,128)S(1)}, s32[16,256]{1,0:T(8,128)S(1)}, u32[]{:S(2)}, u32[]{:S(2)}) collective-permute-start(s32[16,256]{1,0:T(8,128)S(1)} %add_add_fusion.1.pos), channel_id=1, source_target_pairs={{0,128},{64,192},{128,0},{192,64},{1,129},{65,193},{129,1},{193,65... | collective-permute-start | bytes 49160 | tf_op jit(solution)/shard_map/ppermute | solution.py:444
  54.8 14.2 %collective-permute-start.14 = (s32[16,256]{1,0:T(8,128)S(1)}, s32[16,256]{1,0:T(8,128)S(1)}, u32[]{:S(2)}, u32[]{:S(2)}) collective-permute-start(s32[16,256]{1,0:T(8,128)S(1)} %add_add_fusion.1.pos), channel_id=1, source_target_pairs={{0,64},{64,128},{128,192},{192,0},{1,65},{65,129},{129,193},{193,1... | collective-permute-start | bytes 49160 | tf_op jit(solution)/shard_map/ppermute | solution.py:444
  55.6 37.2 %collective-permute-start.24 = (bf16[8,368,128]{2,1,0:T(8,128)(2,1)}, bf16[8,368,128]{2,1,0:T(8,128)(2,1)}, u32[]{:S(2)}, u32[]{:S(2)}) collective-permute-start(bf16[8,368,128]{2,1,0:T(8,128)(2,1)} %all_to_all.15.refs_0_), channel_id=1, source_target_pairs={{0,32},{16,48},{32,0},{48,16},{1,33},{17,49},{33,1},{49,17},{2,34}... | collective-permute-start | bytes 2261000 | tf_op jit(solution)/shard_map/ppermute | solution.py:379
  68.0 24.9 %collective-permute-start.22 = (bf16[8,368,128]{2,1,0:T(8,128)(2,1)}, bf16[8,368,128]{2,1,0:T(8,128)(2,1)S(1)}, u32[]{:S(2)}, u32[]{:S(2)}) collective-permute-start(bf16[8,368,128]{2,1,0:T(8,128)(2,1)} %collective-permute-done.21.refs_0_), channel_id=1, source_target_pairs={{0,1},{1,0},{2,3},{3,2},{4,5},{5,4},{6,7},{7,6},{8,9},{9,8},{10,11... | collective-permute-start | bytes 2261000 | tf_op jit(solution)/shard_map/ppermute | solution.py:417
  69.3 23.6 %copy-start.12 = (bf16[896,1280]{1,0:T(8,128)(2,1)S(1)}, bf16[896,1280]{1,0:T(8,128)(2,1)}, u32[]{:S(2)}) copy-start(bf16[896,1280]{1,0:T(8,128)(2,1)} %refs_3_.7) | copy-start | bytes 6881284
  83.4 22.8 %collective-permute-start.19 = (bf16[8,368,128]{2,1,0:T(8,128)(2,1)}, bf16[8,368,128]{2,1,0:T(8,128)(2,1)S(1)}, u32[]{:S(2)}, u32[]{:S(2)}) collective-permute-start(bf16[8,368,128]{2,1,0:T(8,128)(2,1)} %collective-permute-done.18.refs_0_), channel_id=1, source_target_pairs={{0,1},{1,0},{2,3},{3,2},{4,5},{5,4},{6,7},{7,6},{8,9},{9,8},{10,11... | collective-permute-start | bytes 2261000 | tf_op jit(solution)/shard_map/ppermute | solution.py:417
  91.9 14.3 %slice-start = ((s8[5242880]{0:T(1024)(128)(4,1)}), s8[4194304]{0:T(1024)(128)(4,1)S(1)}, s32[]{:S(2)}) async-start(s8[5242880]{0:T(1024)(128)(4,1)} %bitcast.161), calls=%async_computation.3 | async-start | bytes 8388608
  91.9 14.3 %slice-start.1 = ((s8[5242880]{0:T(1024)(128)(4,1)}), s8[1048576]{0:T(1024)(128)(4,1)S(1)}, s32[]{:S(2)}) async-start(s8[5242880]{0:T(1024)(128)(4,1)} %bitcast.161), calls=%async_computation.4 | async-start | bytes 2097152
  91.9 35.6 %collective-permute-start.17 = (s16[1,2,528,128]{3,2,1,0:T(8,128)(2,1)S(1)}, s16[1,2,528,128]{3,2,1,0:T(8,128)(2,1)S(1)}, u32[]{:S(2)}, u32[]{:S(2)}) collective-permute-start(s16[1,2,528,128]{3,2,1,0:T(8,128)(2,1)S(1)} %get-tuple-element.79), channel_id=1, source_target_pairs={{0,0},{16,80},{32,160},{48,240},{64,192},{80,16},{96,96},{112,176}... | collective-permute-start | bytes 811016 | tf_op jit(solution)/shard_map/ppermute | solution.py:355
  92.8 23.4 %collective-permute-start.25 = (bf16[8,368,128]{2,1,0:T(8,128)(2,1)}, bf16[8,368,128]{2,1,0:T(8,128)(2,1)S(1)}, u32[]{:S(2)}, u32[]{:S(2)}) collective-permute-start(bf16[8,368,128]{2,1,0:T(8,128)(2,1)} %collective-permute-done.24.refs_0_), channel_id=1, source_target_pairs={{0,1},{1,0},{2,3},{3,2},{4,5},{5,4},{6,7},{7,6},{8,9},{9,8},{10,11... | collective-permute-start | bytes 2261000 | tf_op jit(solution)/shard_map/ppermute | solution.py:417
  100.3 27.3 %collective-permute-start.23 = (s16[1,2,528,128]{3,2,1,0:T(8,128)(2,1)S(1)}, s16[1,2,528,128]{3,2,1,0:T(8,128)(2,1)S(1)}, u32[]{:S(2)}, u32[]{:S(2)}) collective-permute-start(s16[1,2,528,128]{3,2,1,0:T(8,128)(2,1)S(1)} %get-tuple-element.81), channel_id=1, source_target_pairs={{0,192},{16,16},{32,96},{48,176},{64,128},{80,208},{96,32},{112,11... | collective-permute-start | bytes 811016 | tf_op jit(solution)/shard_map/ppermute | solution.py:355
  114.2 13.4 %copy-start.11 = (s32[256]{0:T(256)S(1)}, s32[256]{0:T(256)}, u32[]{:S(2)}) copy-start(s32[256]{0:T(256)} %param.13) | copy-start | bytes 3076
  114.2 13.4 %collective-permute-start.20 = (s16[1,2,528,128]{3,2,1,0:T(8,128)(2,1)}, s16[1,2,528,128]{3,2,1,0:T(8,128)(2,1)S(1)}, u32[]{:S(2)}, u32[]{:S(2)}) collective-permute-start(s16[1,2,528,128]{3,2,1,0:T(8,128)(2,1)} %get-tuple-element.80), channel_id=1, source_target_pairs={{0,64},{16,144},{32,224},{48,48},{64,0},{80,80},{96,160},{112,240}... | collective-permute-start | bytes 811016 | tf_op jit(solution)/shard_map/ppermute | solution.py:355
  124.1 11.2 %collective-permute-start.26 = (s16[1,2,528,128]{3,2,1,0:T(8,128)(2,1)}, s16[1,2,528,128]{3,2,1,0:T(8,128)(2,1)S(1)}, u32[]{:S(2)}, u32[]{:S(2)}) collective-permute-start(s16[1,2,528,128]{3,2,1,0:T(8,128)(2,1)} %get-tuple-element.82), channel_id=1, source_target_pairs={{0,128},{16,208},{32,32},{48,112},{64,64},{80,144},{96,224},{112,4... | collective-permute-start | bytes 811016 | tf_op jit(solution)/shard_map/ppermute | solution.py:355
  127.6 32.2 %copy-start.9 = (s32[256]{0:T(256)}, s32[256]{0:T(256)S(1)}, u32[]{:S(2)}) copy-start(s32[256]{0:T(256)S(1)} %broadcast_subtract_fusion) | copy-start | bytes 3076
  161.1 4.8 %collective-permute-start.27 = (bf16[512,128]{1,0:T(8,128)(2,1)S(1)}, bf16[512,128]{1,0:T(8,128)(2,1)S(1)}, u32[]{:S(2)}, u32[]{:S(2)}) collective-permute-start(bf16[512,128]{1,0:T(8,128)(2,1)S(1)} %get-tuple-element.86.refs_0_), channel_id=1, source_target_pairs={{0,192},{64,0},{128,64},{192,128},{1,193},{65,1},{129,65},{193,129... | collective-permute-start | bytes 393224 | tf_op jit(solution)/shard_map/ppermute | solution.py:444
  161.4 6.1 %collective-permute-start.28 = (bf16[512,128]{1,0:T(8,128)(2,1)S(1)}, bf16[512,128]{1,0:T(8,128)(2,1)S(1)}, u32[]{:S(2)}, u32[]{:S(2)}) collective-permute-start(bf16[512,128]{1,0:T(8,128)(2,1)S(1)} %get-tuple-element.86.refs_0_), channel_id=1, source_target_pairs={{0,128},{64,192},{128,0},{192,64},{1,129},{65,193},{129,1},{193,65... | collective-permute-start | bytes 393224 | tf_op jit(solution)/shard_map/ppermute | solution.py:444
  162.8 8.2 %collective-permute-start.29 = (bf16[512,128]{1,0:T(8,128)(2,1)S(1)}, bf16[512,128]{1,0:T(8,128)(2,1)S(1)}, u32[]{:S(2)}, u32[]{:S(2)}) collective-permute-start(bf16[512,128]{1,0:T(8,128)(2,1)S(1)} %get-tuple-element.86.refs_0_), channel_id=1, source_target_pairs={{0,64},{64,128},{128,192},{192,0},{1,65},{65,129},{129,193},{193,1... | collective-permute-start | bytes 393224 | tf_op jit(solution)/shard_map/ppermute | solution.py:444
  171.0 6.3 %copy-start.8 = (s32[256,10]{0,1:T(8,128)S(1)}, s32[256,10]{0,1:T(8,128)}, u32[]{:S(2)}) copy-start(s32[256,10]{0,1:T(8,128)} %param.12) | copy-start | bytes 30724
  171.0 6.3 %copy-start.10 = (s32[256]{0:T(256)S(1)}, s32[256]{0:T(256)}, u32[]{:S(2)}) copy-start(s32[256]{0:T(256)} %copy-done.9) | copy-start | bytes 3076

commit v5 on v4

--- a/solution.py
+++ b/solution.py
@@ -12,6 +12,7 @@
 LIST = 512
 STARTS = 8
 NEG = -1e30
+OVER = 1e30
 BLOCK = 128
 LOCAL = ("y", "z", "c")
 
@@ -205,6 +206,16 @@
     )(meta, *parts)
 
 
+def packed(top_t, sum_t, cross, top_s, sum_s, picked, over):
+    some = sum_t > 0.0
+    safe_t, safe_s = jnp.where(some, sum_t, 1.0), jnp.where(some, sum_s, 1.0)
+    lse_t = jnp.where(some, top_t + jnp.log(safe_t), NEG)
+    lse_s = jnp.where(some, top_s + jnp.log(safe_s), NEG)
+    lines = [jnp.where(over, OVER, lse_t), jnp.where(some, cross / safe_t, 0.0), lse_s, picked]
+    half = picked.shape[-1] // 2
+    return jnp.concatenate([part for a in lines for part in (a[:, :half], a[:, half:])], axis=0)
+
+
 def stats_kernel(meta, pos, target, places, early, last, logits, stats):
     blocks = logits.shape[1]
     tokens = pos.shape[-1]
@@ -233,10 +244,8 @@
         picked = picked + fold(
             mark, jnp.sum(jnp.where(lanes == wanted, ls, 0.0), axis=1, keepdims=True)
         )
-    most = jnp.max(jnp.concatenate([places[t, 11:12, :] for t in range(4)]), axis=0, keepdims=True)
-    most = most.astype(jnp.float32)
-    lines = [tops[0], sum_t, cross, tops[1], sum_s, picked, most, zero]
-    stats[...] = jnp.concatenate(lines, axis=0)
+    over = jnp.max(jnp.concatenate([places[t, 11:12, :] for t in range(4)]), axis=0, keepdims=True)
+    stats[...] = packed(tops[0], sum_t, cross, tops[1], sum_s, picked, over > 0)
 
 
 def row_stats(meta, pos, target, places, early, last):
@@ -246,40 +255,37 @@
         in_specs=scalars_first(5),
         out_shape=[
             jax.ShapeDtypeStruct(early.shape, jnp.float32),
-            jax.ShapeDtypeStruct((8, pos.shape[-1]), jnp.float32),
+            jax.ShapeDtypeStruct((8, pos.shape[-1] // 2), jnp.float32),
         ],
         compiler_params=params(),
     )(meta, pos, target, places, early, last)
 
 
 def combined(seen):
-    top_t = jnp.max(seen[:, 0, :], axis=0, keepdims=True)
-    top_s = jnp.max(seen[:, 3, :], axis=0, keepdims=True)
-    scale_t = jnp.exp(seen[:, 0, :] - top_t)
-    scale_s = jnp.exp(seen[:, 3, :] - top_s)
+    lse_t, ratio, lse_s, picked = (
+        jnp.concatenate([seen[:, 2 * k, :], seen[:, 2 * k + 1, :]], axis=1) for k in range(4)
+    )
     total = lambda a: jnp.sum(a, axis=0, keepdims=True)
-    sum_t = total(seen[:, 1, :] * scale_t)
-    cross = total(seen[:, 2, :] * scale_t)
-    sum_s = total(seen[:, 4, :] * scale_s)
-    picked = total(seen[:, 5, :])
+    top_t = jnp.max(lse_t, axis=0, keepdims=True)
+    top_s = jnp.max(lse_s, axis=0, keepdims=True)
+    share_t = jnp.exp(lse_t - top_t)
+    sum_t = total(share_t)
     log_t = top_t + jnp.log(sum_t)
-    log_s = top_s + jnp.log(sum_s)
-    return top_t, sum_t, top_s, sum_s, cross / sum_t - log_t + log_s, picked - log_s
+    log_s = top_s + jnp.log(total(jnp.exp(lse_s - top_s)))
+    row_kl = total(share_t * ratio) / sum_t - log_t + log_s
+    return log_t, log_s, row_kl, total(picked) - log_s, top_t
 
 
 def grad_kernel(meta, pos, seen, logits, grad, rows, lines):
-    top_t, sum_t, top_s, sum_s, row_kl, logprob = combined(seen[...])
-    most = jnp.max(seen[:, 6, :], axis=0, keepdims=True)
-    rows[...] = jnp.concatenate([row_kl, logprob, most] + [most] * 5, axis=0)
-    inv_t, inv_s = 1.0 / sum_t, 1.0 / sum_s
+    log_t, log_s, row_kl, logprob, top = combined(seen[...])
+    rows[...] = jnp.concatenate([row_kl, logprob, top] + [top] * 5, axis=0)
     lines[...] = jnp.zeros_like(lines)
     for b in range(logits.shape[1]):
         start, here, first = window(meta, 0, b)
         mark = selector(pos[b : b + 1, :], start)
-        share_t, share_s = spread(mark, inv_t), spread(mark, inv_s)
-        et = jnp.exp(logits[0, b] - spread(mark, top_t)) * share_t
-        es = jnp.exp(logits[1, b] - spread(mark, top_s)) * share_s
-        own = jnp.where(share_s > 0.0, es - et, 0.0)
+        et = jnp.exp(logits[0, b] - spread(mark, log_t))
+        es = jnp.exp(logits[1, b] - spread(mark, log_s))
+        own = jnp.where(spread(mark, jnp.ones_like(log_t)) > 0.0, es - et, 0.0)
         lines[here, :] = jnp.where(from_row(first), own, lines[here, :])
     grad[...] = lines[...].astype(jnp.bfloat16)
 
@@ -404,10 +410,10 @@
         et = jnp.where(open_, jnp.exp(jnp.where(open_, lt, NEG) - top_t[:, None]), 0.0)
         es = jnp.where(open_, jnp.exp(jnp.where(open_, ls, NEG) - top_s[:, None]), 0.0)
         lines = [top_t, et.sum(1), (et * (lt - ls)).sum(1), top_s, es.sum(1), picked]
-        stats = jnp.stack(lines + [jnp.zeros_like(top_t)] * 2)
-        all_t, sum_t, all_s, sum_s, row_kl, logprob = combined(everyone(stats))
-        scale_t = (jnp.exp(top_t[None] - all_t) / sum_t)[0]
-        scale_s = (jnp.exp(top_s[None] - all_s) / sum_s)[0]
+        stats = packed(*(line[None] for line in lines), False)
+        log_t, log_s, row_kl, logprob, _ = combined(everyone(stats))
+        scale_t = jnp.exp(top_t - log_t[0])
+        scale_s = jnp.exp(top_s - log_s[0])
         grad = (es * scale_s[:, None] - et * scale_t[:, None]).astype(jnp.bfloat16)
         grads = jnp.concatenate([to_owner(grad, step) for step in range(sx)])
         head = dot(studs, grads, ((1,), (0,)))
@@ -455,7 +461,7 @@
         def run(steps, mine, others):
             return partial_logits(meta, places, steps, mine, others, head_t, head_s)
 
-        pay, other = lax.optimization_barrier((pay, other_core(pay)))
+        other = other_core(pay)
         after, ahead = neighbours(pay)
         part, stud0 = run((0,), [pay], [other])
         got = [to_owner(part, order[0])]
@@ -472,7 +478,7 @@
         grad, rows = row_grads(meta, own_pos, everyone(stats), logits)
         grads = [grad] + [from_line(grad, far) for far in range(1, sx)]
         head = head_gradient(meta, places, grads, [stud0, stud1, stud3, stud2], blocks)
-        start = (rows[2, 0] > 0.5, rows[0], rows[1], head)
+        start = (rows[2, 0] > 0.5 * OVER, rows[0], rows[1], head)
         pays = {0: pay, 1: after, 3: ahead, 2: far}
 
         def redo(_):

time: 178 us -> 171 us (0.961)
  blocking collectives: 51.9 us -> 16.6 us
  waiting for transfers between devices: 39.9 us -> 59.2 us
  starting transfers between devices: 36.1 us -> 44.4 us
    all_to_all x1 -> x0, blocking collectives: 30 us -> none  [per_device(): lax.all_to_all(jnp.broadcast_to(pay[None], (sz, *pay.shape)), 'z', 0, 0,...]
    all_to_all x0 -> x1, waiting for transfers between devices: none -> 22.2 us  [per_device(): lax.all_to_all(jnp.broadcast_to(pay[None], (sz, *pay.shape)), 'z', 0, 0,...]
    all_to_all x0 -> x1, starting transfers between devices: none -> 9 us  [per_device(): lax.all_to_all(jnp.broadcast_to(pay[None], (sz, *pay.shape)), 'z', 0, 0,...]
    all_to_all x1, blocking collectives: 21.9 us -> 16.6 us  [everyone(): lax.all_to_all(copies, LOCAL, split_axis=0, concat_axis=0, tiled=True)]
    ppermute x1, waiting for transfers between devices: 11.2 us -> 8.37 us  [neighbours(): before = lax.ppermute(pay, 'y', shift(1))]
  transfers between devices with their start and end apart: 18 -> 19, of which waited for: 8 -> 9; matrix products, arithmetic and copies ran while one was open for 1% -> 1% of each run, Pallas kernels for 18% -> 19%
where the time goes in v5:
time: 171 us; the launch traced here: 170 us
  waiting for transfers between devices  59.2 us (35%)
  starting transfers between devices  44.4 us (26%)
  Pallas kernels  41.9 us (25%)
  blocking collectives  16.6 us (10%)
  local copies, waits for them, and re-layouts  3.16 us (2%)
  between operations  2.94 us (2%)
  other arithmetic  1.89 us (1%)
    pallas_call x4, Pallas kernels, partial_logits(): pl.pallas_call(functools.partial(partial_kernel, steps), name='partial_lo...  30.7 us
    all_to_all x1, waiting for transfers between devices, per_device(): lax.all_to_all(jnp.broadcast_to(pay[None], (sz, *pay.shape)), 'z', 0, 0,...  22.2 us
    all_to_all x1, blocking collectives, everyone(): lax.all_to_all(copies, LOCAL, split_axis=0, concat_axis=0, tiled=True)  16.6 us
    ppermute x1, waiting for transfers between devices, neighbours(): after = lax.ppermute(pay, 'y', shift(-1))  14 us
    ppermute x4, starting transfers between devices, to_owner(): return lax.ppermute(a, ('x', 'y'), turn(step))  11.9 us
    all_to_all x1, starting transfers between devices, per_device(): lax.all_to_all(jnp.broadcast_to(pay[None], (sz, *pay.shape)), 'z', 0, 0,...  9 us
    ppermute x1, starting transfers between devices, neighbours(): after = lax.ppermute(pay, 'y', shift(-1))  8.37 us
    ppermute x1, waiting for transfers between devices, neighbours(): before = lax.ppermute(pay, 'y', shift(1))  8.37 us
  transfers between devices with their start and end apart: 19, of which 9 were waited for; matrix products, arithmetic and copies ran while one was open for 1% of the time, Pallas kernels for 19%

profile of v5, /device:TPU:1, one launch (start us, length us, event | category | flops | bytes accessed | tf_op | source)
XLA Modules:
  0.0 170.1 jit_solution(15827565578574695440)
XLA Ops:
  0.6 0.0 copy-start.7
  0.6 0.8 reshape.209
  1.4 0.8 pad_maximum_fusion.7
  2.3 0.7 collective-permute-start.15
  2.9 0.0 collective-permute-done.15
  2.9 1.0 broadcast_in_dim.112
  3.9 9.0 %all-to-all-start.1 = ((bf16[8,368,128]{2,1,0:T(8,128)(2,1)}), bf16[8,368,128]{2,1,0:T(8,128)(2,1)}, u32[]{:S(2)}, u32[]{:S(2)}) async-start(bf16[8,368,128]{2,1,0:T(8,128)(2,1)} %broadcast_in_dim.112), calls=%async_computation.1 | async-start | bytes 1507328 | tf_op jit(solution)/shard_map/all_to_all | solution.py:454
  12.9 0.1 convert_reduce_fusion
  13.0 0.7 fusion.38
  13.7 22.2 %all-to-all-done.1.refs_0_ = bf16[8,368,128]{2,1,0:T(8,128)(2,1)} async-done(((bf16[8,368,128]{2,1,0:T(8,128)(2,1)}), bf16[8,368,128]{2,1,0:T(8,128)(2,1)}, u32[]{:S(2)}, u32[]{:S(2)}) %all-to-all-start.1) | async-done | bytes 753696 | tf_op jit(solution)/shard_map/all_to_all | solution.py:454
  35.9 5.1 %collective-permute-start.21 = (bf16[8,368,128]{2,1,0:T(8,128)(2,1)}, bf16[8,368,128]{2,1,0:T(8,128)(2,1)}, u32[]{:S(2)}, u32[]{:S(2)}) collective-permute-start(bf16[8,368,128]{2,1,0:T(8,128)(2,1)} %all-to-all-done.1.refs_0_), channel_id=1, source_target_pairs={{0,16},{16,32},{32,48},{48,0},{1,17},{17,33},{33,49},{49,1},{2,18}... | collective-permute-start | bytes 2261000 | tf_op jit(solution)/shard_map/ppermute | solution.py:381
  41.0 0.1 select_reduce_fusion.1
  41.1 0.1 fusion.31
  41.2 8.4 %collective-permute-start.18 = (bf16[8,368,128]{2,1,0:T(8,128)(2,1)}, bf16[8,368,128]{2,1,0:T(8,128)(2,1)}, u32[]{:S(2)}, u32[]{:S(2)}) collective-permute-start(bf16[8,368,128]{2,1,0:T(8,128)(2,1)} %all-to-all-done.1.refs_0_), channel_id=1, source_target_pairs={{0,48},{16,0},{32,16},{48,32},{1,49},{17,1},{33,17},{49,33},{2,50}... | collective-permute-start | bytes 2261000 | tf_op jit(solution)/shard_map/ppermute | solution.py:380
  49.6 0.8 collective-permute-start.16
  51.7 0.1 pad.39.clone
  51.8 0.1 add_add_fusion.1.pos
  51.9 0.8 collective-permute-start.12
  52.6 1.4 collective-permute-start.13
  54.1 0.8 collective-permute-done.12
  54.9 0.4 collective-permute-start.14
  55.3 1.5 collective-permute-done.13
  56.7 1.3 collective-permute-start.24
  58.0 8.4 %collective-permute-done.21.refs_0_ = bf16[8,368,128]{2,1,0:T(8,128)(2,1)} collective-permute-done((bf16[8,368,128]{2,1,0:T(8,128)(2,1)}, bf16[8,368,128]{2,1,0:T(8,128)(2,1)}, u32[]{:S(2)}, u32[]{:S(2)}) %collective-permute-start.21) | collective-permute-done | bytes 753696 | tf_op jit(solution)/shard_map/ppermute | solution.py:381
  66.4 1.1 collective-permute-start.22
  67.4 0.1 fusion.51
  67.5 0.0 collective-permute-done.14
  67.6 0.1 reshape_squeeze.3
  67.7 0.1 concatenate.37.meta
  67.7 14.0 %collective-permute-done.18.refs_0_ = bf16[8,368,128]{2,1,0:T(8,128)(2,1)} collective-permute-done((bf16[8,368,128]{2,1,0:T(8,128)(2,1)}, bf16[8,368,128]{2,1,0:T(8,128)(2,1)}, u32[]{:S(2)}, u32[]{:S(2)}) %collective-permute-start.18) | collective-permute-done | bytes 753696 | tf_op jit(solution)/shard_map/ppermute | solution.py:380
  81.8 1.3 collective-permute-start.19
  83.1 0.0 collective-permute-done.16.refs_1_
  83.1 7.3 %partial_logits.4 = (s16[1,2,528,128]{3,2,1,0:T(8,128)(2,1)S(1)}, bf16[1,896,256]{2,1,0:T(8,128)(2,1)S(1)}) custom-call(s32[72]{0:T(128)S(1)} %concatenate.37.meta, s32[4,16,256]{2,1,0:T(8,128)S(1)} %pad_add_fusion.pos.places, bf16[8,368,128]{2,1,0:T(8,128)(2,1)} %all-to-all-done.1.refs_0_, bf16[8,368,128]{2,1,0:T(8,128)(2,1)S(1)} %collective-permute-done.16.refs_1_, ...), custom_call_target="tpu_custom_call" | custom-call | flops 4823449600 | bytes 9043968 | tf_op jit(solution)/shard_map/partial_logits/pallas_call | solution.py:144
  90.4 0.0 slice-start
  90.4 0.0 slice-start.1
  90.4 0.8 collective-permute-start.17
  91.3 0.0 collective-permute-done.24.refs_0_
  91.3 0.1 collective-permute-start.25
  91.4 0.0 collective-permute-done.22.refs_1_
  91.4 7.4 %partial_logits.6 = (s16[1,2,528,128]{3,2,1,0:T(8,128)(2,1)S(1)}, bf16[1,896,256]{2,1,0:T(8,128)(2,1)S(1)}) custom-call(s32[72]{0:T(128)S(1)} %concatenate.37.meta, s32[4,16,256]{2,1,0:T(8,128)S(1)} %pad_add_fusion.pos.places, bf16[8,368,128]{2,1,0:T(8,128)(2,1)} %collective-permute-done.21.refs_0_, ...), custom_call_target="tpu_custom_call" | custom-call | flops 4823449600 | bytes 9043968 | tf_op jit(solution)/shard_map/partial_logits/pallas_call | solution.py:144
  98.8 5.8 %collective-permute-start.23 = (s16[1,2,528,128]{3,2,1,0:T(8,128)(2,1)S(1)}, s16[1,2,528,128]{3,2,1,0:T(8,128)(2,1)S(1)}, u32[]{:S(2)}, u32[]{:S(2)}) collective-permute-start(s16[1,2,528,128]{3,2,1,0:T(8,128)(2,1)S(1)} %get-tuple-element.77), channel_id=1, source_target_pairs={{0,192},{16,16},{32,96},{48,176},{64,128},{80,208},{96,32},{112,11... | collective-permute-start | bytes 811016 | tf_op jit(solution)/shard_map/ppermute | solution.py:361
  104.7 0.0 collective-permute-done.19.refs_1_
  104.7 8.0 %partial_logits.5 = (s16[1,2,528,128]{3,2,1,0:T(8,128)(2,1)}, bf16[1,896,256]{2,1,0:T(8,128)(2,1)S(1)}) custom-call(s32[72]{0:T(128)S(1)} %concatenate.37.meta, s32[4,16,256]{2,1,0:T(8,128)S(1)} %pad_add_fusion.pos.places, bf16[8,368,128]{2,1,0:T(8,128)(2,1)} %collective-permute-done.18.refs_0_, bf16[8,368,128]{2,1,0:T(8,128)(2,1)S(1)} %collective-permute-done.19.refs_1_, ...), custom_call_target="tpu_custom_call" | custom-call | flops 4823449600 | bytes 9043968 | tf_op jit(solution)/shard_map/partial_logits/pallas_call | solution.py:144
  112.7 0.0 copy-start.11
  112.7 1.9 %collective-permute-start.20 = (s16[1,2,528,128]{3,2,1,0:T(8,128)(2,1)}, s16[1,2,528,128]{3,2,1,0:T(8,128)(2,1)S(1)}, u32[]{:S(2)}, u32[]{:S(2)}) collective-permute-start(s16[1,2,528,128]{3,2,1,0:T(8,128)(2,1)} %get-tuple-element.76), channel_id=1, source_target_pairs={{0,64},{16,144},{32,224},{48,48},{64,0},{80,80},{96,160},{112,240}... | collective-permute-start | bytes 811016 | tf_op jit(solution)/shard_map/ppermute | solution.py:361
  114.6 0.0 collective-permute-done.25.refs_1_
  114.6 8.0 %partial_logits.7 = (s16[1,2,528,128]{3,2,1,0:T(8,128)(2,1)}, bf16[1,896,256]{2,1,0:T(8,128)(2,1)S(1)}) custom-call(s32[72]{0:T(128)S(1)} %concatenate.37.meta, s32[4,16,256]{2,1,0:T(8,128)S(1)} %pad_add_fusion.pos.places, bf16[8,368,128]{2,1,0:T(8,128)(2,1)} %collective-permute-done.24.refs_0_, bf16[8,368,128]{2,1,0:T(8,128)(2,1)S(1)} %collective-permute-done.25.refs_1_, ...), custom_call_target="tpu_custom_call" | custom-call | flops 4823449600 | bytes 9043968 | tf_op jit(solution)/shard_map/partial_logits/pallas_call | solution.py:144
  122.7 3.4 %collective-permute-start.26 = (s16[1,2,528,128]{3,2,1,0:T(8,128)(2,1)}, s16[1,2,528,128]{3,2,1,0:T(8,128)(2,1)S(1)}, u32[]{:S(2)}, u32[]{:S(2)}) collective-permute-start(s16[1,2,528,128]{3,2,1,0:T(8,128)(2,1)} %get-tuple-element.78), channel_id=1, source_target_pairs={{0,128},{16,208},{32,32},{48,112},{64,64},{80,144},{96,224},{112,4... | collective-permute-start | bytes 811016 | tf_op jit(solution)/shard_map/ppermute | solution.py:361
  126.1 0.0 collective-permute-done.17.a0
  126.1 0.0 collective-permute-done.20.a1
  126.1 1.3 early_sum.1.early
  127.4 6.4 %collective-permute-done.26.last = s16[1,2,528,128]{3,2,1,0:T(8,128)(2,1)S(1)} collective-permute-done((s16[1,2,528,128]{3,2,1,0:T(8,128)(2,1)}, s16[1,2,528,128]{3,2,1,0:T(8,128)(2,1)S(1)}, u32[]{:S(2)}, u32[]{:S(2)}) %collective-permute-start.26) | collective-permute-done | bytes 270368 | tf_op jit(solution)/shard_map/ppermute | solution.py:361
  133.8 2.5 %row_stats.1 = (f32[2,10,80,128]{3,2,1,0:T(8,128)S(1)}, f32[8,128]{1,0:T(8,128)S(1)}) custom-call(s32[72]{0:T(128)S(1)} %concatenate.37.meta, s32[16,256]{1,0:T(8,128)S(1)} %add_add_fusion.1.pos, s32[1,256]{1,0:T(1,128)S(1)} %bitcast.150, s32[4,16,256]{2,1,0:T(8,128)S(1)} %pad_add_fusion.pos.places, f32[2,10,80,128]{3,2,1,0:T(8,128)S(1)} %early_sum.1.early, ...), custom_call_target="tpu_custom_call" | custom-call | tf_op jit(solution)/shard_map/row_stats/pallas_call | solution.py:252
  136.4 16.6 %all_to_all.15.seen = f32[64,8,128]{2,1,0:T(8,128)S(1)} all-to-all(f32[64,8,128]{2,1,0:T(8,128)S(1)} %broadcast_in_dim.113), channel_id=1, replica_groups=mesh['x'=4,'y'=4,'z'=8,'c'=2] {'y','z','c'}, dimensions={0} | all-to-all | bytes 524288 | tf_op jit(solution)/shard_map/all_to_all | solution.py:389
  152.9 1.1 row_grads.1
  154.1 0.1 collective-permute-start.27
  154.1 1.5 collective-permute-start.28
  155.6 0.5 collective-permute-start.29
  156.2 0.5 slice.103
  157.3 0.6 fusion.45
  157.9 0.7 collective-permute-done.27.refs_1_
  158.7 1.5 collective-permute-done.28.refs_2_
  160.2 3.6 %collective-permute-done.29.refs_3_ = bf16[512,128]{1,0:T(8,128)(2,1)S(1)} collective-permute-done((bf16[512,128]{1,0:T(8,128)(2,1)S(1)}, bf16[512,128]{1,0:T(8,128)(2,1)S(1)}, u32[]{:S(2)}, u32[]{:S(2)}) %collective-permute-start.29) | collective-permute-done | bytes 131104 | tf_op jit(solution)/shard_map/ppermute | solution.py:450
  163.8 6.3 %head_gradient.1 = f32[896,1280]{1,0:T(8,128)} custom-call(s32[72]{0:T(128)S(1)} %concatenate.37.meta, s32[4,16,256]{2,1,0:T(8,128)S(1)} %pad_add_fusion.pos.places, bf16[512,128]{1,0:T(8,128)(2,1)S(1)} %get-tuple-element.82.refs_0_, bf16[512,128]{1,0:T(8,128)(2,1)S(1)} %collective-permute-done.27.refs_1_, ...), custom_call_target="tpu_custom_call" | custom-call | tf_op jit(solution)/shard_map/head_gradient/pallas_call | solution.py:337
  (23 shorter events, 0.1 us)
Async XLA Ops:
  0.6 12.3 %copy-start.7 = (s32[256,10]{0,1:T(8,128)S(1)}, s32[256,10]{0,1:T(8,128)}, u32[]{:S(2)}) copy-start(s32[256,10]{0,1:T(8,128)} %param.12) | copy-start | bytes 30724
  2.3 0.7 collective-permute-start.15
  3.9 32.0 %all-to-all-start.1 = ((bf16[8,368,128]{2,1,0:T(8,128)(2,1)}), bf16[8,368,128]{2,1,0:T(8,128)(2,1)}, u32[]{:S(2)}, u32[]{:S(2)}) async-start(bf16[8,368,128]{2,1,0:T(8,128)(2,1)} %broadcast_in_dim.112), calls=%async_computation.1 | async-start | bytes 1507328 | tf_op jit(solution)/shard_map/all_to_all | solution.py:454
  35.9 30.5 %collective-permute-start.21 = (bf16[8,368,128]{2,1,0:T(8,128)(2,1)}, bf16[8,368,128]{2,1,0:T(8,128)(2,1)}, u32[]{:S(2)}, u32[]{:S(2)}) collective-permute-start(bf16[8,368,128]{2,1,0:T(8,128)(2,1)} %all-to-all-done.1.refs_0_), channel_id=1, source_target_pairs={{0,16},{16,32},{32,48},{48,0},{1,17},{17,33},{33,49},{49,1},{2,18}... | collective-permute-start | bytes 2261000 | tf_op jit(solution)/shard_map/ppermute | solution.py:381
  41.2 40.5 %collective-permute-start.18 = (bf16[8,368,128]{2,1,0:T(8,128)(2,1)}, bf16[8,368,128]{2,1,0:T(8,128)(2,1)}, u32[]{:S(2)}, u32[]{:S(2)}) collective-permute-start(bf16[8,368,128]{2,1,0:T(8,128)(2,1)} %all-to-all-done.1.refs_0_), channel_id=1, source_target_pairs={{0,48},{16,0},{32,16},{48,32},{1,49},{17,1},{33,17},{49,33},{2,50}... | collective-permute-start | bytes 2261000 | tf_op jit(solution)/shard_map/ppermute | solution.py:380
  49.6 33.5 %collective-permute-start.16 = (bf16[8,368,128]{2,1,0:T(8,128)(2,1)}, bf16[8,368,128]{2,1,0:T(8,128)(2,1)S(1)}, u32[]{:S(2)}, u32[]{:S(2)}) collective-permute-start(bf16[8,368,128]{2,1,0:T(8,128)(2,1)} %all-to-all-done.1.refs_0_), channel_id=1, source_target_pairs={{0,1},{1,0},{2,3},{3,2},{4,5},{5,4},{6,7},{7,6},{8,9},{9,8},{10,11... | collective-permute-start | bytes 2261000 | tf_op jit(solution)/shard_map/ppermute | solution.py:423
  51.9 3.0 %collective-permute-start.12 = (s32[16,256]{1,0:T(8,128)S(1)}, s32[16,256]{1,0:T(8,128)S(1)}, u32[]{:S(2)}, u32[]{:S(2)}) collective-permute-start(s32[16,256]{1,0:T(8,128)S(1)} %add_add_fusion.1.pos), channel_id=1, source_target_pairs={{0,192},{64,0},{128,64},{192,128},{1,193},{65,1},{129,65},{193,129... | collective-permute-start | bytes 49160 | tf_op jit(solution)/shard_map/ppermute | solution.py:450
  52.6 4.1 %collective-permute-start.13 = (s32[16,256]{1,0:T(8,128)S(1)}, s32[16,256]{1,0:T(8,128)S(1)}, u32[]{:S(2)}, u32[]{:S(2)}) collective-permute-start(s32[16,256]{1,0:T(8,128)S(1)} %add_add_fusion.1.pos), channel_id=1, source_target_pairs={{0,128},{64,192},{128,0},{192,64},{1,129},{65,193},{129,1},{193,65... | collective-permute-start | bytes 49160 | tf_op jit(solution)/shard_map/ppermute | solution.py:450
  54.9 12.7 %collective-permute-start.14 = (s32[16,256]{1,0:T(8,128)S(1)}, s32[16,256]{1,0:T(8,128)S(1)}, u32[]{:S(2)}, u32[]{:S(2)}) collective-permute-start(s32[16,256]{1,0:T(8,128)S(1)} %add_add_fusion.1.pos), channel_id=1, source_target_pairs={{0,64},{64,128},{128,192},{192,0},{1,65},{65,129},{129,193},{193,1... | collective-permute-start | bytes 49160 | tf_op jit(solution)/shard_map/ppermute | solution.py:450
  56.7 34.5 %collective-permute-start.24 = (bf16[8,368,128]{2,1,0:T(8,128)(2,1)}, bf16[8,368,128]{2,1,0:T(8,128)(2,1)}, u32[]{:S(2)}, u32[]{:S(2)}) collective-permute-start(bf16[8,368,128]{2,1,0:T(8,128)(2,1)} %all-to-all-done.1.refs_0_), channel_id=1, source_target_pairs={{0,32},{16,48},{32,0},{48,16},{1,33},{17,49},{33,1},{49,17},{2,34}... | collective-permute-start | bytes 2261000 | tf_op jit(solution)/shard_map/ppermute | solution.py:385
  66.4 25.0 %collective-permute-start.22 = (bf16[8,368,128]{2,1,0:T(8,128)(2,1)}, bf16[8,368,128]{2,1,0:T(8,128)(2,1)S(1)}, u32[]{:S(2)}, u32[]{:S(2)}) collective-permute-start(bf16[8,368,128]{2,1,0:T(8,128)(2,1)} %collective-permute-done.21.refs_0_), channel_id=1, source_target_pairs={{0,1},{1,0},{2,3},{3,2},{4,5},{5,4},{6,7},{7,6},{8,9},{9,8},{10,11... | collective-permute-start | bytes 2261000 | tf_op jit(solution)/shard_map/ppermute | solution.py:423
  67.7 23.6 %copy-start.12 = (bf16[896,1280]{1,0:T(8,128)(2,1)S(1)}, bf16[896,1280]{1,0:T(8,128)(2,1)}, u32[]{:S(2)}) copy-start(bf16[896,1280]{1,0:T(8,128)(2,1)} %refs_3_.7) | copy-start | bytes 6881284
  81.8 22.9 %collective-permute-start.19 = (bf16[8,368,128]{2,1,0:T(8,128)(2,1)}, bf16[8,368,128]{2,1,0:T(8,128)(2,1)S(1)}, u32[]{:S(2)}, u32[]{:S(2)}) collective-permute-start(bf16[8,368,128]{2,1,0:T(8,128)(2,1)} %collective-permute-done.18.refs_0_), channel_id=1, source_target_pairs={{0,1},{1,0},{2,3},{3,2},{4,5},{5,4},{6,7},{7,6},{8,9},{9,8},{10,11... | collective-permute-start | bytes 2261000 | tf_op jit(solution)/shard_map/ppermute | solution.py:423
  90.4 14.3 %slice-start = ((s8[5242880]{0:T(1024)(128)(4,1)}), s8[4194304]{0:T(1024)(128)(4,1)S(1)}, s32[]{:S(2)}) async-start(s8[5242880]{0:T(1024)(128)(4,1)} %bitcast.159), calls=%async_computation.3 | async-start | bytes 8388608
  90.4 14.3 %slice-start.1 = ((s8[5242880]{0:T(1024)(128)(4,1)}), s8[1048576]{0:T(1024)(128)(4,1)S(1)}, s32[]{:S(2)}) async-start(s8[5242880]{0:T(1024)(128)(4,1)} %bitcast.159), calls=%async_computation.4 | async-start | bytes 2097152
  90.4 35.7 %collective-permute-start.17 = (s16[1,2,528,128]{3,2,1,0:T(8,128)(2,1)S(1)}, s16[1,2,528,128]{3,2,1,0:T(8,128)(2,1)S(1)}, u32[]{:S(2)}, u32[]{:S(2)}) collective-permute-start(s16[1,2,528,128]{3,2,1,0:T(8,128)(2,1)S(1)} %get-tuple-element.75), channel_id=1, source_target_pairs={{0,0},{16,80},{32,160},{48,240},{64,192},{80,16},{96,96},{112,176}... | collective-permute-start | bytes 811016 | tf_op jit(solution)/shard_map/ppermute | solution.py:361
  91.3 23.4 %collective-permute-start.25 = (bf16[8,368,128]{2,1,0:T(8,128)(2,1)}, bf16[8,368,128]{2,1,0:T(8,128)(2,1)S(1)}, u32[]{:S(2)}, u32[]{:S(2)}) collective-permute-start(bf16[8,368,128]{2,1,0:T(8,128)(2,1)} %collective-permute-done.24.refs_0_), channel_id=1, source_target_pairs={{0,1},{1,0},{2,3},{3,2},{4,5},{5,4},{6,7},{7,6},{8,9},{9,8},{10,11... | collective-permute-start | bytes 2261000 | tf_op jit(solution)/shard_map/ppermute | solution.py:423
  98.8 27.3 %collective-permute-start.23 = (s16[1,2,528,128]{3,2,1,0:T(8,128)(2,1)S(1)}, s16[1,2,528,128]{3,2,1,0:T(8,128)(2,1)S(1)}, u32[]{:S(2)}, u32[]{:S(2)}) collective-permute-start(s16[1,2,528,128]{3,2,1,0:T(8,128)(2,1)S(1)} %get-tuple-element.77), channel_id=1, source_target_pairs={{0,192},{16,16},{32,96},{48,176},{64,128},{80,208},{96,32},{112,11... | collective-permute-start | bytes 811016 | tf_op jit(solution)/shard_map/ppermute | solution.py:361
  112.7 13.4 %copy-start.11 = (s32[256]{0:T(256)S(1)}, s32[256]{0:T(256)}, u32[]{:S(2)}) copy-start(s32[256]{0:T(256)} %param.13) | copy-start | bytes 3076
  112.7 13.4 %collective-permute-start.20 = (s16[1,2,528,128]{3,2,1,0:T(8,128)(2,1)}, s16[1,2,528,128]{3,2,1,0:T(8,128)(2,1)S(1)}, u32[]{:S(2)}, u32[]{:S(2)}) collective-permute-start(s16[1,2,528,128]{3,2,1,0:T(8,128)(2,1)} %get-tuple-element.76), channel_id=1, source_target_pairs={{0,64},{16,144},{32,224},{48,48},{64,0},{80,80},{96,160},{112,240}... | collective-permute-start | bytes 811016 | tf_op jit(solution)/shard_map/ppermute | solution.py:361
  122.7 11.2 %collective-permute-start.26 = (s16[1,2,528,128]{3,2,1,0:T(8,128)(2,1)}, s16[1,2,528,128]{3,2,1,0:T(8,128)(2,1)S(1)}, u32[]{:S(2)}, u32[]{:S(2)}) collective-permute-start(s16[1,2,528,128]{3,2,1,0:T(8,128)(2,1)} %get-tuple-element.78), channel_id=1, source_target_pairs={{0,128},{16,208},{32,32},{48,112},{64,64},{80,144},{96,224},{112,4... | collective-permute-start | bytes 811016 | tf_op jit(solution)/shard_map/ppermute | solution.py:361
  126.1 26.8 %copy-start.9 = (s32[256]{0:T(256)}, s32[256]{0:T(256)S(1)}, u32[]{:S(2)}) copy-start(s32[256]{0:T(256)S(1)} %broadcast_subtract_fusion) | copy-start | bytes 3076
  154.1 4.6 %collective-permute-start.27 = (bf16[512,128]{1,0:T(8,128)(2,1)S(1)}, bf16[512,128]{1,0:T(8,128)(2,1)S(1)}, u32[]{:S(2)}, u32[]{:S(2)}) collective-permute-start(bf16[512,128]{1,0:T(8,128)(2,1)S(1)} %get-tuple-element.82.refs_0_), channel_id=1, source_target_pairs={{0,192},{64,0},{128,64},{192,128},{1,193},{65,1},{129,65},{193,129... | collective-permute-start | bytes 393224 | tf_op jit(solution)/shard_map/ppermute | solution.py:450
  154.1 6.0 %collective-permute-start.28 = (bf16[512,128]{1,0:T(8,128)(2,1)S(1)}, bf16[512,128]{1,0:T(8,128)(2,1)S(1)}, u32[]{:S(2)}, u32[]{:S(2)}) collective-permute-start(bf16[512,128]{1,0:T(8,128)(2,1)S(1)} %get-tuple-element.82.refs_0_), channel_id=1, source_target_pairs={{0,128},{64,192},{128,0},{192,64},{1,129},{65,193},{129,1},{193,65... | collective-permute-start | bytes 393224 | tf_op jit(solution)/shard_map/ppermute | solution.py:450
  155.6 8.1 %collective-permute-start.29 = (bf16[512,128]{1,0:T(8,128)(2,1)S(1)}, bf16[512,128]{1,0:T(8,128)(2,1)S(1)}, u32[]{:S(2)}, u32[]{:S(2)}) collective-permute-start(bf16[512,128]{1,0:T(8,128)(2,1)S(1)} %get-tuple-element.82.refs_0_), channel_id=1, source_target_pairs={{0,64},{64,128},{128,192},{192,0},{1,65},{65,129},{129,193},{193,1... | collective-permute-start | bytes 393224 | tf_op jit(solution)/shard_map/ppermute | solution.py:450
  163.8 6.3 %copy-start.8 = (s32[256,10]{0,1:T(8,128)S(1)}, s32[256,10]{0,1:T(8,128)}, u32[]{:S(2)}) copy-start(s32[256,10]{0,1:T(8,128)} %param.12) | copy-start | bytes 30724
  163.8 6.3 %copy-start.10 = (s32[256]{0:T(256)S(1)}, s32[256]{0:T(256)}, u32[]{:S(2)}) copy-start(s32[256]{0:T(256)} %copy-done.9) | copy-start | bytes 3076

commit v6 on v5

--- a/solution.py
+++ b/solution.py
@@ -304,50 +304,75 @@
     )(meta, pos, seen, logits)
 
 
-def head_kernel(meta, places, *refs):
-    *studs, out, left = refs
-    grads, studs = studs[:4], studs[4:]
+def scattered(meta, places, grad, t, pair):
+    sides = []
+    for k in range(2):
+        start, here, _ = window(meta, t, 2 * pair + k)
+        mark = selector(places[t, 2 * pair + k][None], start).astype(jnp.float32)
+        mark = mark.astype(jnp.bfloat16)
+        sides.append(dot(mark, grad[here, :], ((0,), (0,))).astype(jnp.bfloat16))
+    return jnp.concatenate(sides, axis=1)
+
+
+def own_head_kernel(meta, places, grad, *refs):
+    *studs, left, base = refs
+    tokens = places.shape[-1]
+    for step, ref in enumerate(studs):
+        at = pl.multiple_of(meta[1 + step] * tokens, tokens)
+        left[:, pl.ds(at, tokens)] = ref[0]
+
+    def pair(b, _):
+        columns = pl.ds(pl.multiple_of(b * 2 * BLOCK, 2 * BLOCK), 2 * BLOCK)
+        right = scattered(meta, places, grad, 0, b)
+        base[:, columns] = dot(left[:, :tokens], right, ((1,), (0,)))
+        return 0
+
+    lax.fori_loop(0, base.shape[1] // (2 * BLOCK), pair, 0)
+
+
+def own_head(meta, places, grad, studs, blocks):
+    deep, tokens = studs[0].shape[1:]
+    return pl.pallas_call(
+        own_head_kernel,
+        name="own_head",
+        in_specs=scalars_first(2 + len(studs)),
+        out_shape=[
+            jax.ShapeDtypeStruct((deep, len(studs) * tokens), jnp.bfloat16),
+            jax.ShapeDtypeStruct((deep, blocks * BLOCK), jnp.float32),
+        ],
+        compiler_params=params(),
+        cost_estimate=pl.CostEstimate(
+            flops=2 * deep * tokens * blocks * BLOCK,
+            bytes_accessed=deep * (4 * tokens + 4 * blocks * BLOCK),
+            transcendentals=0,
+        ),
+    )(meta, places, grad, *studs)
+
+
+def head_kernel(meta, places, left, base, *refs):
+    *grads, out = refs
     tokens = places.shape[-1]
     b = pl.program_id(0)
-
-    @pl.when(b == 0)
-    def _():
-        step = 1
-        for ref in studs:
-            for i in range(ref.shape[0]):
-                at = pl.multiple_of(meta[step] * tokens, tokens)
-                left[:, pl.ds(at, tokens)] = ref[i]
-                step += 1
-
-    right = []
-    for t, grad in enumerate(grads):
-        pair = []
-        for k in range(2):
-            start, here, _ = window(meta, t, 2 * b + k)
-            mark = selector(places[t, 2 * b + k][None], start).astype(jnp.float32)
-            mark = mark.astype(jnp.bfloat16)
-            pair.append(dot(mark, grad[here, :], ((0,), (0,))).astype(jnp.bfloat16))
-        right.append(jnp.concatenate(pair, axis=1))
-    out[...] = dot(left[...], jnp.concatenate(right, axis=0), ((1,), (0,)))
-
-
-def head_gradient(meta, places, grads, studs, blocks):
-    deep, tokens = studs[0].shape[1:]
+    right = [scattered(meta, places, grad, t + 1, b) for t, grad in enumerate(grads)]
+    out[...] = base[...] + dot(left[:, tokens:], jnp.concatenate(right, axis=0), ((1,), (0,)))
+
+
+def head_gradient(meta, places, left, base, grads):
+    deep, width = base.shape
     whole = lambda a: pl.BlockSpec(a.shape, lambda b, meta: (0,) * a.ndim)
+    columns = pl.BlockSpec((deep, 2 * BLOCK), lambda b, meta: (0, b))
     return pl.pallas_call(
         head_kernel,
         name="head_gradient",
         grid_spec=pltpu.PrefetchScalarGridSpec(
             num_scalar_prefetch=1,
-            grid=(blocks // 2,),
-            in_specs=[whole(places)]
-            + [whole(a) for a in (*grads, *studs)],
-            out_specs=pl.BlockSpec((deep, 2 * BLOCK), lambda b, meta: (0, b)),
-            scratch_shapes=[pltpu.VMEM((deep, 4 * tokens), jnp.bfloat16)],
+            grid=(width // (2 * BLOCK),),
+            in_specs=[whole(places), whole(left), columns] + [whole(a) for a in grads],
+            out_specs=columns,
         ),
-        out_shape=jax.ShapeDtypeStruct((deep, blocks * BLOCK), jnp.float32),
+        out_shape=jax.ShapeDtypeStruct((deep, width), jnp.float32),
         compiler_params=params(),
-    )(meta, places, *grads, *studs)
+    )(meta, places, left, base, *grads)
 
 
 def build(sx, sz, sc):
@@ -476,8 +501,9 @@
         early = early_sum(meta, blocks, got[:3])
         logits, stats = row_stats(meta, own_pos, target[None], places, early, got[3])
         grad, rows = row_grads(meta, own_pos, everyone(stats), logits)
-        grads = [grad] + [from_line(grad, far) for far in range(1, sx)]
-        head = head_gradient(meta, places, grads, [stud0, stud1, stud3, stud2], blocks)
+        grads = [from_line(grad, far) for far in range(1, sx)]
+        left, base = own_head(meta, places, grad, [stud0, stud1, stud3, stud2], blocks)
+        head = head_gradient(meta, places, left, base, grads)
         start = (rows[2, 0] > 0.5 * OVER, rows[0], rows[1], head)
         pays = {0: pay, 1: after, 3: ahead, 2: far}
 

time: 171 us -> 170 us (level)
  waiting for transfers between devices: 59.2 us -> 55.8 us
    pallas_call x0 -> x1, Pallas kernels: none -> 3.17 us  [own_head(): pl.pallas_call(own_head_kernel, name='own_head', in_specs=scalars_first(2...]
    ppermute x6, waiting for transfers between devices: 8.11 us -> 4.97 us  [from_line(): return lax.ppermute(a, 'x', [(x, (x - far) % sx) for x in range(sx)])]
  transfers between devices with their start and end apart: 19 -> 19, of which waited for: 9 -> 7; matrix products, arithmetic and copies ran while one was open for 1% -> 1% of each run, Pallas kernels for 19% -> 20%
where the time goes in v6:
time: 170 us
  waiting for transfers between devices  55.8 us (33%)
  starting transfers between devices  44.5 us (26%)
  Pallas kernels  43.2 us (25%)
  blocking collectives  16.6 us (10%)
  local copies, waits for them, and re-layouts  4.68 us (3%)
  between operations  2.9 us (2%)
  other arithmetic  1.89 us (1%)
    pallas_call x4, Pallas kernels, partial_logits(): pl.pallas_call(functools.partial(partial_kernel, steps), name='partial_lo...  29.3 us
    all_to_all x1, waiting for transfers between devices, per_device(): lax.all_to_all(jnp.broadcast_to(pay[None], (sz, *pay.shape)), 'z', 0, 0,...  22.2 us
    all_to_all x1, blocking collectives, everyone(): lax.all_to_all(copies, LOCAL, split_axis=0, concat_axis=0, tiled=True)  16.6 us
    ppermute x1, waiting for transfers between devices, neighbours(): after = lax.ppermute(pay, 'y', shift(-1))  14 us
    ppermute x4, starting transfers between devices, to_owner(): return lax.ppermute(a, ('x', 'y'), turn(step))  12.1 us
    all_to_all x1, starting transfers between devices, per_device(): lax.all_to_all(jnp.broadcast_to(pay[None], (sz, *pay.shape)), 'z', 0, 0,...  9 us
    ppermute x1, starting transfers between devices, neighbours(): after = lax.ppermute(pay, 'y', shift(-1))  8.37 us
    ppermute x1, waiting for transfers between devices, neighbours(): before = lax.ppermute(pay, 'y', shift(1))  8.37 us
  transfers between devices with their start and end apart: 19, of which 7 were waited for; matrix products, arithmetic and copies ran while one was open for 1% of the time, Pallas kernels for 20%

profile of v6, /device:TPU:1, one launch (start us, length us, event | category | flops | bytes accessed | tf_op | source)
XLA Modules:
  0.0 169.7 jit_solution(4357475291755758971)
XLA Ops:
  0.6 0.0 copy-start.11
  0.6 0.8 reshape.209
  1.4 0.8 pad_maximum_fusion.7
  2.3 0.7 collective-permute-start.15
  2.9 0.0 collective-permute-done.15
  2.9 1.0 broadcast_in_dim.112
  3.9 9.0 %all-to-all-start.1 = ((bf16[8,368,128]{2,1,0:T(8,128)(2,1)}), bf16[8,368,128]{2,1,0:T(8,128)(2,1)}, u32[]{:S(2)}, u32[]{:S(2)}) async-start(bf16[8,368,128]{2,1,0:T(8,128)(2,1)} %broadcast_in_dim.112), calls=%async_computation.1 | async-start | bytes 1507328 | tf_op jit(solution)/shard_map/all_to_all | solution.py:479
  12.9 0.1 convert_reduce_fusion
  13.0 0.7 fusion.38
  13.7 22.2 %all-to-all-done.1.refs_0_ = bf16[8,368,128]{2,1,0:T(8,128)(2,1)} async-done(((bf16[8,368,128]{2,1,0:T(8,128)(2,1)}), bf16[8,368,128]{2,1,0:T(8,128)(2,1)}, u32[]{:S(2)}, u32[]{:S(2)}) %all-to-all-start.1) | async-done | bytes 753696 | tf_op jit(solution)/shard_map/all_to_all | solution.py:479
  35.9 5.1 %collective-permute-start.21 = (bf16[8,368,128]{2,1,0:T(8,128)(2,1)}, bf16[8,368,128]{2,1,0:T(8,128)(2,1)}, u32[]{:S(2)}, u32[]{:S(2)}) collective-permute-start(bf16[8,368,128]{2,1,0:T(8,128)(2,1)} %all-to-all-done.1.refs_0_), channel_id=1, source_target_pairs={{0,16},{16,32},{32,48},{48,0},{1,17},{17,33},{33,49},{49,1},{2,18}... | collective-permute-start | bytes 2261000 | tf_op jit(solution)/shard_map/ppermute | solution.py:406
  41.0 0.1 select_reduce_fusion.1
  41.1 0.1 fusion.31
  41.2 8.4 %collective-permute-start.18 = (bf16[8,368,128]{2,1,0:T(8,128)(2,1)}, bf16[8,368,128]{2,1,0:T(8,128)(2,1)}, u32[]{:S(2)}, u32[]{:S(2)}) collective-permute-start(bf16[8,368,128]{2,1,0:T(8,128)(2,1)} %all-to-all-done.1.refs_0_), channel_id=1, source_target_pairs={{0,48},{16,0},{32,16},{48,32},{1,49},{17,1},{33,17},{49,33},{2,50}... | collective-permute-start | bytes 2261000 | tf_op jit(solution)/shard_map/ppermute | solution.py:405
  49.6 0.8 collective-permute-start.16
  51.7 0.1 pad.39.clone
  51.8 0.1 add_add_fusion.1.pos
  51.9 0.8 collective-permute-start.12
  52.6 1.4 collective-permute-start.13
  54.1 0.8 collective-permute-done.12
  54.9 0.4 collective-permute-start.14
  55.3 1.5 collective-permute-done.13
  56.7 1.3 collective-permute-start.24
  58.0 8.4 %collective-permute-done.21.refs_0_ = bf16[8,368,128]{2,1,0:T(8,128)(2,1)} collective-permute-done((bf16[8,368,128]{2,1,0:T(8,128)(2,1)}, bf16[8,368,128]{2,1,0:T(8,128)(2,1)}, u32[]{:S(2)}, u32[]{:S(2)}) %collective-permute-start.21) | collective-permute-done | bytes 753696 | tf_op jit(solution)/shard_map/ppermute | solution.py:406
  66.4 1.1 collective-permute-start.22
  67.4 0.1 fusion.51
  67.6 0.1 reshape_squeeze.3
  67.7 0.1 concatenate.37.meta
  67.7 14.0 %collective-permute-done.18.refs_0_ = bf16[8,368,128]{2,1,0:T(8,128)(2,1)} collective-permute-done((bf16[8,368,128]{2,1,0:T(8,128)(2,1)}, bf16[8,368,128]{2,1,0:T(8,128)(2,1)}, u32[]{:S(2)}, u32[]{:S(2)}) %collective-permute-start.18) | collective-permute-done | bytes 753696 | tf_op jit(solution)/shard_map/ppermute | solution.py:405
  81.8 1.3 collective-permute-start.19
  83.1 7.3 %partial_logits.4 = (s16[1,2,528,128]{3,2,1,0:T(8,128)(2,1)S(1)}, bf16[1,896,256]{2,1,0:T(8,128)(2,1)S(1)}) custom-call(s32[72]{0:T(128)S(1)} %concatenate.37.meta, s32[4,16,256]{2,1,0:T(8,128)S(1)} %pad_add_fusion.pos.places, bf16[8,368,128]{2,1,0:T(8,128)(2,1)} %all-to-all-done.1.refs_0_, bf16[8,368,128]{2,1,0:T(8,128)(2,1)S(1)} %collective-permute-done.16.refs_1_, ...), custom_call_target="tpu_custom_call" | custom-call | flops 4823449600 | bytes 9043968 | tf_op jit(solution)/shard_map/partial_logits/pallas_call | solution.py:144
  90.4 0.0 slice-start
  90.4 0.0 slice-start.1
  90.4 0.8 collective-permute-start.17
  91.3 0.0 collective-permute-done.24.refs_0_
  91.3 0.1 collective-permute-start.25
  91.4 7.5 %partial_logits.6 = (s16[1,2,528,128]{3,2,1,0:T(8,128)(2,1)S(1)}, bf16[1,896,256]{2,1,0:T(8,128)(2,1)S(1)}) custom-call(s32[72]{0:T(128)S(1)} %concatenate.37.meta, s32[4,16,256]{2,1,0:T(8,128)S(1)} %pad_add_fusion.pos.places, bf16[8,368,128]{2,1,0:T(8,128)(2,1)} %collective-permute-done.21.refs_0_, ...), custom_call_target="tpu_custom_call" | custom-call | flops 4823449600 | bytes 9043968 | tf_op jit(solution)/shard_map/partial_logits/pallas_call | solution.py:144
  98.9 5.8 %collective-permute-start.23 = (s16[1,2,528,128]{3,2,1,0:T(8,128)(2,1)S(1)}, s16[1,2,528,128]{3,2,1,0:T(8,128)(2,1)S(1)}, u32[]{:S(2)}, u32[]{:S(2)}) collective-permute-start(s16[1,2,528,128]{3,2,1,0:T(8,128)(2,1)S(1)} %get-tuple-element.79), channel_id=1, source_target_pairs={{0,192},{16,16},{32,96},{48,176},{64,128},{80,208},{96,32},{112,11... | collective-permute-start | bytes 811016 | tf_op jit(solution)/shard_map/ppermute | solution.py:386
  104.7 0.0 collective-permute-done.19.refs_1_
  104.8 7.3 %partial_logits.5 = (s16[1,2,528,128]{3,2,1,0:T(8,128)(2,1)S(1)}, bf16[1,896,256]{2,1,0:T(8,128)(2,1)S(1)}) custom-call(s32[72]{0:T(128)S(1)} %concatenate.37.meta, s32[4,16,256]{2,1,0:T(8,128)S(1)} %pad_add_fusion.pos.places, bf16[8,368,128]{2,1,0:T(8,128)(2,1)} %collective-permute-done.18.refs_0_, ...), custom_call_target="tpu_custom_call" | custom-call | flops 4823449600 | bytes 9043968 | tf_op jit(solution)/shard_map/partial_logits/pallas_call | solution.py:144
  112.1 0.0 copy-start
  112.1 0.8 copy-done
  112.8 2.0 %collective-permute-start.20 = (s16[1,2,528,128]{3,2,1,0:T(8,128)(2,1)S(1)}, s16[1,2,528,128]{3,2,1,0:T(8,128)(2,1)S(1)}, u32[]{:S(2)}, u32[]{:S(2)}) collective-permute-start(s16[1,2,528,128]{3,2,1,0:T(8,128)(2,1)S(1)} %get-tuple-element.78), channel_id=1, source_target_pairs={{0,64},{16,144},{32,224},{48,48},{64,0},{80,80},{96,160},{112,240}... | collective-permute-start | bytes 811016 | tf_op jit(solution)/shard_map/ppermute | solution.py:386
  114.9 0.0 collective-permute-done.25.refs_1_
  114.9 7.3 %partial_logits.7 = (s16[1,2,528,128]{3,2,1,0:T(8,128)(2,1)S(1)}, bf16[1,896,256]{2,1,0:T(8,128)(2,1)S(1)}) custom-call(s32[72]{0:T(128)S(1)} %concatenate.37.meta, s32[4,16,256]{2,1,0:T(8,128)S(1)} %pad_add_fusion.pos.places, bf16[8,368,128]{2,1,0:T(8,128)(2,1)} %collective-permute-done.24.refs_0_, ...), custom_call_target="tpu_custom_call" | custom-call | flops 4823449600 | bytes 9043968 | tf_op jit(solution)/shard_map/partial_logits/pallas_call | solution.py:144
  122.2 0.8 copy-done.2
  123.0 3.4 %collective-permute-start.26 = (s16[1,2,528,128]{3,2,1,0:T(8,128)(2,1)S(1)}, s16[1,2,528,128]{3,2,1,0:T(8,128)(2,1)S(1)}, u32[]{:S(2)}, u32[]{:S(2)}) collective-permute-start(s16[1,2,528,128]{3,2,1,0:T(8,128)(2,1)S(1)} %get-tuple-element.80), channel_id=1, source_target_pairs={{0,128},{16,208},{32,32},{48,112},{64,64},{80,144},{96,224},{112,4... | collective-permute-start | bytes 811016 | tf_op jit(solution)/shard_map/ppermute | solution.py:386
  126.4 0.0 collective-permute-done.23.a2
  126.4 0.0 collective-permute-done.20.a1
  126.4 1.3 early_sum.1.early
  127.7 0.0 copy-start.1
  127.7 6.2 %collective-permute-done.26.last = s16[1,2,528,128]{3,2,1,0:T(8,128)(2,1)S(1)} collective-permute-done((s16[1,2,528,128]{3,2,1,0:T(8,128)(2,1)S(1)}, s16[1,2,528,128]{3,2,1,0:T(8,128)(2,1)S(1)}, u32[]{:S(2)}, u32[]{:S(2)}) %collective-permute-start.26) | collective-permute-done | bytes 270368 | tf_op jit(solution)/shard_map/ppermute | solution.py:386
  133.9 2.5 %row_stats.1 = (f32[2,10,80,128]{3,2,1,0:T(8,128)S(1)}, f32[8,128]{1,0:T(8,128)S(1)}) custom-call(s32[72]{0:T(128)S(1)} %concatenate.37.meta, s32[16,256]{1,0:T(8,128)S(1)} %add_add_fusion.1.pos, s32[1,256]{1,0:T(1,128)S(1)} %bitcast.150, s32[4,16,256]{2,1,0:T(8,128)S(1)} %pad_add_fusion.pos.places, f32[2,10,80,128]{3,2,1,0:T(8,128)S(1)} %early_sum.1.early, ...), custom_call_target="tpu_custom_call" | custom-call | tf_op jit(solution)/shard_map/row_stats/pallas_call | solution.py:252
  136.4 16.6 %all_to_all.15.seen = f32[64,8,128]{2,1,0:T(8,128)S(1)} all-to-all(f32[64,8,128]{2,1,0:T(8,128)S(1)} %broadcast_in_dim.113), channel_id=1, replica_groups=mesh['x'=4,'y'=4,'z'=8,'c'=2] {'y','z','c'}, dimensions={0} | all-to-all | bytes 524288 | tf_op jit(solution)/shard_map/all_to_all | solution.py:414
  153.0 1.1 row_grads.1
  154.2 0.1 collective-permute-start.27
  154.2 1.5 collective-permute-start.28
  155.8 0.5 collective-permute-start.29
  156.3 0.6 fusion.45
  156.9 0.5 slice.103
  158.0 3.2 %own_head.1 = (bf16[896,1024]{1,0:T(8,128)(2,1)S(1)}, f32[896,1280]{1,0:T(8,128)S(1)}) custom-call(s32[72]{0:T(128)S(1)} %concatenate.37.meta, s32[4,16,256]{2,1,0:T(8,128)S(1)} %pad_add_fusion.pos.places, bf16[512,128]{1,0:T(8,128)(2,1)S(1)} %get-tuple-element.84.grad, bf16[1,896,256]{2,1,0:T(8,128)(2,1)S(1)} %get-tuple-element.85.refs_0_, ...), custom_call_target="tpu_custom_call" | custom-call | flops 587202560 | bytes 5505024 | tf_op jit(solution)/shard_map/own_head/pallas_call | solution.py:335
  161.1 0.0 collective-permute-done.27.refs_0_
  161.1 2.7 %collective-permute-done.29.refs_2_ = bf16[512,128]{1,0:T(8,128)(2,1)S(1)} collective-permute-done((bf16[512,128]{1,0:T(8,128)(2,1)S(1)}, bf16[512,128]{1,0:T(8,128)(2,1)S(1)}, u32[]{:S(2)}, u32[]{:S(2)}) %collective-permute-start.29) | collective-permute-done | bytes 131104 | tf_op jit(solution)/shard_map/ppermute | solution.py:475
  163.8 5.8 %head_gradient.1 = f32[896,1280]{1,0:T(8,128)} custom-call(s32[72]{0:T(128)S(1)} %concatenate.37.meta, s32[4,16,256]{2,1,0:T(8,128)S(1)} %pad_add_fusion.pos.places, bf16[896,1024]{1,0:T(8,128)(2,1)S(1)} %get-tuple-element.89.left, f32[896,1280]{1,0:T(8,128)S(1)} %get-tuple-element.90.base, bf16[512,128]{1,0:T(8,128)(2,1)S(1)} %collective-permute-done.27.refs_0_, ...), custom_call_target="tpu_custom_call" | custom-call | tf_op jit(solution)/shard_map/head_gradient/pallas_call | solution.py:364
  (28 shorter events, 0.1 us)
Async XLA Ops:
  0.6 12.3 %copy-start.11 = (s32[256,10]{0,1:T(8,128)S(1)}, s32[256,10]{0,1:T(8,128)}, u32[]{:S(2)}) copy-start(s32[256,10]{0,1:T(8,128)} %param.12) | copy-start | bytes 30724
  2.3 0.7 collective-permute-start.15
  3.9 32.0 %all-to-all-start.1 = ((bf16[8,368,128]{2,1,0:T(8,128)(2,1)}), bf16[8,368,128]{2,1,0:T(8,128)(2,1)}, u32[]{:S(2)}, u32[]{:S(2)}) async-start(bf16[8,368,128]{2,1,0:T(8,128)(2,1)} %broadcast_in_dim.112), calls=%async_computation.1 | async-start | bytes 1507328 | tf_op jit(solution)/shard_map/all_to_all | solution.py:479
  35.9 30.5 %collective-permute-start.21 = (bf16[8,368,128]{2,1,0:T(8,128)(2,1)}, bf16[8,368,128]{2,1,0:T(8,128)(2,1)}, u32[]{:S(2)}, u32[]{:S(2)}) collective-permute-start(bf16[8,368,128]{2,1,0:T(8,128)(2,1)} %all-to-all-done.1.refs_0_), channel_id=1, source_target_pairs={{0,16},{16,32},{32,48},{48,0},{1,17},{17,33},{33,49},{49,1},{2,18}... | collective-permute-start | bytes 2261000 | tf_op jit(solution)/shard_map/ppermute | solution.py:406
  41.2 40.5 %collective-permute-start.18 = (bf16[8,368,128]{2,1,0:T(8,128)(2,1)}, bf16[8,368,128]{2,1,0:T(8,128)(2,1)}, u32[]{:S(2)}, u32[]{:S(2)}) collective-permute-start(bf16[8,368,128]{2,1,0:T(8,128)(2,1)} %all-to-all-done.1.refs_0_), channel_id=1, source_target_pairs={{0,48},{16,0},{32,16},{48,32},{1,49},{17,1},{33,17},{49,33},{2,50}... | collective-permute-start | bytes 2261000 | tf_op jit(solution)/shard_map/ppermute | solution.py:405
  49.6 33.5 %collective-permute-start.16 = (bf16[8,368,128]{2,1,0:T(8,128)(2,1)}, bf16[8,368,128]{2,1,0:T(8,128)(2,1)S(1)}, u32[]{:S(2)}, u32[]{:S(2)}) collective-permute-start(bf16[8,368,128]{2,1,0:T(8,128)(2,1)} %all-to-all-done.1.refs_0_), channel_id=1, source_target_pairs={{0,1},{1,0},{2,3},{3,2},{4,5},{5,4},{6,7},{7,6},{8,9},{9,8},{10,11... | collective-permute-start | bytes 2261000 | tf_op jit(solution)/shard_map/ppermute | solution.py:448
  51.9 3.0 %collective-permute-start.12 = (s32[16,256]{1,0:T(8,128)S(1)}, s32[16,256]{1,0:T(8,128)S(1)}, u32[]{:S(2)}, u32[]{:S(2)}) collective-permute-start(s32[16,256]{1,0:T(8,128)S(1)} %add_add_fusion.1.pos), channel_id=1, source_target_pairs={{0,192},{64,0},{128,64},{192,128},{1,193},{65,1},{129,65},{193,129... | collective-permute-start | bytes 49160 | tf_op jit(solution)/shard_map/ppermute | solution.py:475
  52.6 4.1 %collective-permute-start.13 = (s32[16,256]{1,0:T(8,128)S(1)}, s32[16,256]{1,0:T(8,128)S(1)}, u32[]{:S(2)}, u32[]{:S(2)}) collective-permute-start(s32[16,256]{1,0:T(8,128)S(1)} %add_add_fusion.1.pos), channel_id=1, source_target_pairs={{0,128},{64,192},{128,0},{192,64},{1,129},{65,193},{129,1},{193,65... | collective-permute-start | bytes 49160 | tf_op jit(solution)/shard_map/ppermute | solution.py:475
  54.9 12.7 %collective-permute-start.14 = (s32[16,256]{1,0:T(8,128)S(1)}, s32[16,256]{1,0:T(8,128)S(1)}, u32[]{:S(2)}, u32[]{:S(2)}) collective-permute-start(s32[16,256]{1,0:T(8,128)S(1)} %add_add_fusion.1.pos), channel_id=1, source_target_pairs={{0,64},{64,128},{128,192},{192,0},{1,65},{65,129},{129,193},{193,1... | collective-permute-start | bytes 49160 | tf_op jit(solution)/shard_map/ppermute | solution.py:475
  56.7 34.5 %collective-permute-start.24 = (bf16[8,368,128]{2,1,0:T(8,128)(2,1)}, bf16[8,368,128]{2,1,0:T(8,128)(2,1)}, u32[]{:S(2)}, u32[]{:S(2)}) collective-permute-start(bf16[8,368,128]{2,1,0:T(8,128)(2,1)} %all-to-all-done.1.refs_0_), channel_id=1, source_target_pairs={{0,32},{16,48},{32,0},{48,16},{1,33},{17,49},{33,1},{49,17},{2,34}... | collective-permute-start | bytes 2261000 | tf_op jit(solution)/shard_map/ppermute | solution.py:410
  66.4 25.0 %collective-permute-start.22 = (bf16[8,368,128]{2,1,0:T(8,128)(2,1)}, bf16[8,368,128]{2,1,0:T(8,128)(2,1)S(1)}, u32[]{:S(2)}, u32[]{:S(2)}) collective-permute-start(bf16[8,368,128]{2,1,0:T(8,128)(2,1)} %collective-permute-done.21.refs_0_), channel_id=1, source_target_pairs={{0,1},{1,0},{2,3},{3,2},{4,5},{5,4},{6,7},{7,6},{8,9},{9,8},{10,11... | collective-permute-start | bytes 2261000 | tf_op jit(solution)/shard_map/ppermute | solution.py:448
  67.7 23.6 %copy-start.17 = (bf16[896,1280]{1,0:T(8,128)(2,1)S(1)}, bf16[896,1280]{1,0:T(8,128)(2,1)}, u32[]{:S(2)}) copy-start(bf16[896,1280]{1,0:T(8,128)(2,1)} %refs_3_.7) | copy-start | bytes 6881284
  81.8 23.0 %collective-permute-start.19 = (bf16[8,368,128]{2,1,0:T(8,128)(2,1)}, bf16[8,368,128]{2,1,0:T(8,128)(2,1)S(1)}, u32[]{:S(2)}, u32[]{:S(2)}) collective-permute-start(bf16[8,368,128]{2,1,0:T(8,128)(2,1)} %collective-permute-done.18.refs_0_), channel_id=1, source_target_pairs={{0,1},{1,0},{2,3},{3,2},{4,5},{5,4},{6,7},{7,6},{8,9},{9,8},{10,11... | collective-permute-start | bytes 2261000 | tf_op jit(solution)/shard_map/ppermute | solution.py:448
  90.4 14.3 %slice-start = ((s8[5242880]{0:T(1024)(128)(4,1)}), s8[4194304]{0:T(1024)(128)(4,1)S(1)}, s32[]{:S(2)}) async-start(s8[5242880]{0:T(1024)(128)(4,1)} %bitcast.159), calls=%async_computation.3 | async-start | bytes 8388608
  90.4 14.3 %slice-start.1 = ((s8[5242880]{0:T(1024)(128)(4,1)}), s8[1048576]{0:T(1024)(128)(4,1)S(1)}, s32[]{:S(2)}) async-start(s8[5242880]{0:T(1024)(128)(4,1)} %bitcast.159), calls=%async_computation.4 | async-start | bytes 2097152
  90.4 36.0 %collective-permute-start.17 = (s16[1,2,528,128]{3,2,1,0:T(8,128)(2,1)S(1)}, s16[1,2,528,128]{3,2,1,0:T(8,128)(2,1)S(1)}, u32[]{:S(2)}, u32[]{:S(2)}) collective-permute-start(s16[1,2,528,128]{3,2,1,0:T(8,128)(2,1)S(1)} %get-tuple-element.77), channel_id=1, source_target_pairs={{0,0},{16,80},{32,160},{48,240},{64,192},{80,16},{96,96},{112,176}... | collective-permute-start | bytes 811016 | tf_op jit(solution)/shard_map/ppermute | solution.py:386
  91.3 23.6 %collective-permute-start.25 = (bf16[8,368,128]{2,1,0:T(8,128)(2,1)}, bf16[8,368,128]{2,1,0:T(8,128)(2,1)S(1)}, u32[]{:S(2)}, u32[]{:S(2)}) collective-permute-start(bf16[8,368,128]{2,1,0:T(8,128)(2,1)} %collective-permute-done.24.refs_0_), channel_id=1, source_target_pairs={{0,1},{1,0},{2,3},{3,2},{4,5},{5,4},{6,7},{7,6},{8,9},{9,8},{10,11... | collective-permute-start | bytes 2261000 | tf_op jit(solution)/shard_map/ppermute | solution.py:448
  98.9 27.5 %collective-permute-start.23 = (s16[1,2,528,128]{3,2,1,0:T(8,128)(2,1)S(1)}, s16[1,2,528,128]{3,2,1,0:T(8,128)(2,1)S(1)}, u32[]{:S(2)}, u32[]{:S(2)}) collective-permute-start(s16[1,2,528,128]{3,2,1,0:T(8,128)(2,1)S(1)} %get-tuple-element.79), channel_id=1, source_target_pairs={{0,192},{16,16},{32,96},{48,176},{64,128},{80,208},{96,32},{112,11... | collective-permute-start | bytes 811016 | tf_op jit(solution)/shard_map/ppermute | solution.py:386
  112.1 0.8 copy-start
  112.8 13.5 %copy-start.16 = (s32[256]{0:T(256)S(1)}, s32[256]{0:T(256)}, u32[]{:S(2)}) copy-start(s32[256]{0:T(256)} %param.13) | copy-start | bytes 3076
  112.8 13.6 %collective-permute-start.20 = (s16[1,2,528,128]{3,2,1,0:T(8,128)(2,1)S(1)}, s16[1,2,528,128]{3,2,1,0:T(8,128)(2,1)S(1)}, u32[]{:S(2)}, u32[]{:S(2)}) collective-permute-start(s16[1,2,528,128]{3,2,1,0:T(8,128)(2,1)S(1)} %get-tuple-element.78), channel_id=1, source_target_pairs={{0,64},{16,144},{32,224},{48,48},{64,0},{80,80},{96,160},{112,240}... | collective-permute-start | bytes 811016 | tf_op jit(solution)/shard_map/ppermute | solution.py:386
  122.2 0.8 copy-start.2
  123.0 10.9 %collective-permute-start.26 = (s16[1,2,528,128]{3,2,1,0:T(8,128)(2,1)S(1)}, s16[1,2,528,128]{3,2,1,0:T(8,128)(2,1)S(1)}, u32[]{:S(2)}, u32[]{:S(2)}) collective-permute-start(s16[1,2,528,128]{3,2,1,0:T(8,128)(2,1)S(1)} %get-tuple-element.80), channel_id=1, source_target_pairs={{0,128},{16,208},{32,32},{48,112},{64,64},{80,144},{96,224},{112,4... | collective-permute-start | bytes 811016 | tf_op jit(solution)/shard_map/ppermute | solution.py:386
  127.7 30.2 %copy-start.1 = (bf16[1,896,256]{2,1,0:T(8,128)(2,1)S(1)}, bf16[1,896,256]{2,1,0:T(8,128)(2,1)}, u32[]{:S(2)}) copy-start(bf16[1,896,256]{2,1,0:T(8,128)(2,1)} %copy-done) | copy-start | bytes 1376260
  127.7 30.2 %copy-start.3 = (bf16[1,896,256]{2,1,0:T(8,128)(2,1)S(1)}, bf16[1,896,256]{2,1,0:T(8,128)(2,1)}, u32[]{:S(2)}) copy-start(bf16[1,896,256]{2,1,0:T(8,128)(2,1)} %copy-done.2) | copy-start | bytes 1376260
  154.2 7.0 %collective-permute-start.27 = (bf16[512,128]{1,0:T(8,128)(2,1)S(1)}, bf16[512,128]{1,0:T(8,128)(2,1)S(1)}, u32[]{:S(2)}, u32[]{:S(2)}) collective-permute-start(bf16[512,128]{1,0:T(8,128)(2,1)S(1)} %get-tuple-element.84.grad), channel_id=1, source_target_pairs={{0,192},{64,0},{128,64},{192,128},{1,193},{65,1},{129,65},{193,129... | collective-permute-start | bytes 393224 | tf_op jit(solution)/shard_map/ppermute | solution.py:475
  154.2 6.9 %collective-permute-start.28 = (bf16[512,128]{1,0:T(8,128)(2,1)S(1)}, bf16[512,128]{1,0:T(8,128)(2,1)S(1)}, u32[]{:S(2)}, u32[]{:S(2)}) collective-permute-start(bf16[512,128]{1,0:T(8,128)(2,1)S(1)} %get-tuple-element.84.grad), channel_id=1, source_target_pairs={{0,128},{64,192},{128,0},{192,64},{1,129},{65,193},{129,1},{193,65... | collective-permute-start | bytes 393224 | tf_op jit(solution)/shard_map/ppermute | solution.py:475
  155.8 8.1 %collective-permute-start.29 = (bf16[512,128]{1,0:T(8,128)(2,1)S(1)}, bf16[512,128]{1,0:T(8,128)(2,1)S(1)}, u32[]{:S(2)}, u32[]{:S(2)}) collective-permute-start(bf16[512,128]{1,0:T(8,128)(2,1)S(1)} %get-tuple-element.84.grad), channel_id=1, source_target_pairs={{0,64},{64,128},{128,192},{192,0},{1,65},{65,129},{129,193},{193,1... | collective-permute-start | bytes 393224 | tf_op jit(solution)/shard_map/ppermute | solution.py:475
  163.8 5.8 %copy-start.12 = (s32[256,10]{0,1:T(8,128)S(1)}, s32[256,10]{0,1:T(8,128)}, u32[]{:S(2)}) copy-start(s32[256,10]{0,1:T(8,128)} %param.12) | copy-start | bytes 30724
